TPU v7x, 128 devices: a whole 4x4x4 slice. The times are simulated.
128 devices in a mesh: inp: 8 (over x, z_lo), freq: 16 (over y, z_hi, core).
Axes of the slice: x: 4, y: 4, z: 4 (z_hi: 2, z_lo: 2; z = z_hi * 2 + z_lo), core: 2. Of those that a mesh axis runs over, the one named last changes fastest.
Arguments:
- volts: bfloat16 [32, 2, 4096, 1024], P('freq', None, 'inp'), parts along dimension 0, may hold values from -6 to 6
- position_input: int32 [16, 256], P('inp'), may hold values from 0 to 255, each once within a row
- tile_group: int32 [16, 4, 2], P('inp'), may hold values from 0 to 63
Outputs:
- stacked: float32 [64, 32, 2, 511], P('inp', 'freq'), parts along dimension 1
There are 16 independent parts, one for each index of `freq`. A program takes and returns all parts, laid end to end along the dimension named above; an argument that names none is the same for every part. Nothing has to cross between parts.
Inputs may be any that keep to these rules, and one draw needn't show every extreme that they name: `position_input`: each row holds every position's input index within the block once. `tile_group`: entry [a, l, b] names the row group of the tile of block a with the b-th block of the device at level l of block a's device.
All inputs are finite; a program needn't handle non-finite values.
Results may differ from a plain program's by a relative error of at most 0.0003.
Values may be sent and summed in bfloat16 or wider, within the bound.
A program may use at most 192 MiB of HBM per device.

v0:
```python
import jax
import jax.numpy as jnp
from jax import lax
from jax.experimental import pallas as pl
from jax.experimental.pallas import tpu as pltpu
from jax.sharding import PartitionSpec as P

RG_DEV = 8
HIGH = lax.Precision.HIGHEST
NT = (((1,), (1,)), ((), ()))


def lag_kernel(sel_ref, x_ref, y_ref, o_ref):
    width = x_ref.shape[3]
    for a in range(2):
        xre = x_ref[0, 0, a]
        xim = x_ref[0, 1, a]
        for b in range(2):
            yre = y_ref[0, 0, b]
            yim = y_ref[0, 1, b]
            dot = lambda u, v: lax.dot_general(u, v, NT, preferred_element_type=jnp.float32)
            real_part = dot(xre, yre) + dot(xim, yim)
            imag_part = dot(xim, yre) - dot(xre, yim)
            for c, part in enumerate((real_part, imag_part)):
                padded = jnp.concatenate([part, jnp.zeros_like(part)], axis=1)
                sheared = pltpu.roll(padded, 0, 1, stride=1, stride_axis=0)
                row = (a * 2 + b) * 2 + c
                o_ref[0, pl.ds(row, 1), :] = jnp.sum(sheared, axis=0, keepdims=True)
    del width


def pair_lags(sel, x_all, y_all, y_by_sel):
    n = sel.shape[0]
    _, _, _, width, samples = x_all.shape
    x_spec = pl.BlockSpec((1, 2, 2, width, samples), lambda i, s: (s[i], 0, 0, 0, 0))
    if y_by_sel:
        y_spec = pl.BlockSpec((1, 2, 2, width, samples), lambda i, s: (s[i], 0, 0, 0, 0))
    else:
        y_spec = pl.BlockSpec((1, 2, 2, width, samples), lambda i, s: (i, 0, 0, 0, 0))
    out_spec = pl.BlockSpec((1, 8, 2 * width), lambda i, s: (i, 0, 0))
    flops = n * 16 * 2 * width * width * samples
    return pl.pallas_call(
        lag_kernel,
        out_shape=jax.ShapeDtypeStruct((n, 8, 2 * width), jnp.float32),
        grid_spec=pltpu.PrefetchScalarGridSpec(
            num_scalar_prefetch=1,
            grid=(n,),
            in_specs=[x_spec, y_spec],
            out_specs=out_spec,
        ),
        compiler_params=pltpu.CompilerParams(vmem_limit_bytes=48 * 1024 * 1024),
        cost_estimate=pl.CostEstimate(
            flops=flops, transcendentals=0, bytes_accessed=n * 2 * 4 * width * samples * 2
        ),
    )(sel, x_all, y_all)


def on_device(volts, position_input, tile_group):
    blocks, width = position_input.shape
    channels, _, _, samples = volts.shape
    diffs = 2 * width - 1
    n_inp = lax.axis_size("inp")
    levels = n_inp.bit_length() - 1
    me = lax.axis_index("inp")

    ids = jnp.arange(width, dtype=jnp.int32)
    perm = (position_input[:, :, None] == ids[None, None, :]).astype(volts.dtype)
    perm_rev = perm[:, ::-1, :]
    v5 = volts.reshape(channels, 2, blocks, width, samples)
    ordered = jnp.einsum("api,fcais->fcaps", perm, v5, preferred_element_type=jnp.float32).astype(volts.dtype)
    reversed_ = jnp.einsum("api,fcais->fcaps", perm_rev, v5, preferred_element_type=jnp.float32).astype(volts.dtype)

    groups_all = RG_DEV * n_inp
    group_ids = jnp.arange(groups_all, dtype=jnp.int32)
    tg_all = lax.all_gather(tile_group, "inp", tiled=True)

    lag0 = pair_lags(jnp.arange(channels, dtype=jnp.int32), ordered, reversed_, True)
    lag0 = lag0.reshape(channels, 2, 2, 2, 2 * width)
    center = (jnp.arange(2 * width) == width - 1)
    same = jnp.eye(2, dtype=bool)
    lag0 = jnp.where(same[None, :, :, None, None] & center[None, None, None, None, :], 0.0, lag0)
    w0 = (tile_group[:, 0, :, None] == group_ids).astype(jnp.float32)
    dense_rev = jnp.einsum("abg,fabcj->gfcj", w0, lag0, precision=HIGH)
    dense_fwd = None
    chan_ids = jnp.arange(channels, dtype=jnp.int32)
    sign = jnp.array([1.0, -1.0], jnp.float32)
    for bit in range(levels):
        partner = me ^ (1 << bit)
        mine = (me >> bit) & 1
        send = lax.dynamic_index_in_dim(reversed_, 1 - mine, axis=0, keepdims=True)
        got = lax.ppermute(send, "inp", [(i, i ^ (1 << bit)) for i in range(n_inp)])
        lag = pair_lags(mine[None].astype(jnp.int32), ordered, got, False)
        lag = lag.reshape(2, 2, 2, 2 * width)
        fmask = (chan_ids == mine).astype(jnp.float32)
        w_direct = (tile_group[:, bit + 1, :, None] == group_ids).astype(jnp.float32)
        tg_partner = lax.dynamic_slice_in_dim(tg_all, partner * blocks, blocks, axis=0)
        w_trans = (tg_partner[:, bit + 1, :, None] == group_ids).astype(jnp.float32)
        dense_rev = dense_rev + jnp.einsum("abg,f,abcj->gfcj", w_direct, fmask, lag, precision=HIGH)
        term = jnp.einsum("bag,f,c,abcj->gfcj", w_trans, fmask, sign, lag, precision=HIGH)
        dense_fwd = term if dense_fwd is None else dense_fwd + term
    dense = jnp.flip(dense_rev[..., :diffs], axis=-1) + dense_fwd[..., :diffs]
    dense = dense * (1.0 / samples)
    return lax.psum_scatter(dense, "inp", scatter_dimension=0, tiled=True)


def solution(mesh):
    return jax.shard_map(
        on_device,
        mesh=mesh,
        in_specs=(P("freq", None, "inp", None), P("inp", None), P("inp", None, None)),
        out_specs=P("inp", "freq", None, None),
        check_vma=False,
    )
```

profile of v0, /device:TPU:32, one launch (start us, length us, event | category | flops | bytes accessed | tf_op | source)
XLA Modules:
  0.0 192.1 jit_solution(11395989583752514408)
XLA Ops:
  6.5 0.0 reduce-scatter.2.cloned.1.call-start
  6.5 0.8 fusion.1
  7.4 0.3 rev.7
  7.7 3.4 %convolution_convert_fusion = bf16[2,256,2,2,1024]{4,1,0,3,2:T(8,128)(2,1)S(1)} fusion(bf16[2,2,2,256,1024]{4,3,2,1,0:T(8,128)(2,1)} %bitcast.88, bf16[2,256,256]{2,1,0:T(8,128)(2,1)S(1)} %rev.7), kind=kOutput, calls=%fused_computation.1 | convolution fusion | flops 1075838976 | bytes 8650752 | tf_op jit(solution)/shard_map/api,fcais->fcaps/dot_general | solution.py:71
  11.2 0.0 copy-start.1
  11.2 0.0 copy-start.2
  11.2 0.0 copy-start.4
  11.2 3.2 %dynamic-slice_bitcast_fusion.2 = (bf16[1,2,2,256,1024]{4,3,2,1,0:T(8,128)(2,1)}, bf16[1,2,2,256,1024]{4,3,2,1,0:T(8,128)(2,1)}, bf16[1,2,2,256,1024]{4,3,2,1,0:T(8,128)(2,1)}) fusion(bf16[2,256,2,2,1024]{4,1,0,3,2:T(8,128)(2,1)S(1)} %convolution_convert_fusion, s32[]{:T(128)S(6)} %select_n.24, s32[]{:T(128)S(6)} %select_n.26, s32[]{:T(128)S(6)} %select_n.25), kind=kLoop, calls=%fused_computation.4 | loop fusion | bytes 12582924 | tf_op jit(solution)/shard_map/jit(dynamic_index_in_dim)/dynamic_slice | solution.py:90
  14.4 1.6 copy-done.1
  16.0 1.5 collective-permute-start.1
  17.5 2.7 %collective-permute-start.2 = (bf16[1,2,2,256,1024]{4,3,2,1,0:T(8,128)(2,1)}, bf16[1,2,2,256,1024]{4,3,2,1,0:T(8,128)(2,1)}, u32[]{:S(2)}, u32[]{:S(2)}) collective-permute-start(bf16[1,2,2,256,1024]{4,3,2,1,0:T(8,128)(2,1)} %get-tuple-element.10), channel_id=1, source_target_pairs={{0,64},{16,80},{32,96},{48,112},{64,0},{80,16},{96,32},{112,48},{1... | collective-permute-start | bytes 6291464 | tf_op jit(solution)/shard_map/ppermute | solution.py:91
  20.2 0.1 collective-permute-start
  20.3 0.0 copy-done.2
  20.3 0.0 copy-done.4
  20.4 3.2 %convert_bitcast_fusion.x_ref = bf16[2,2,2,256,1024]{4,3,2,1,0:T(8,128)(2,1)} fusion(bf16[2,2,2,256,1024]{4,3,2,1,0:T(8,128)(2,1)S(1)} %bitcast.89, s32[2,256]{1,0:T(2,128)S(1)} %copy-done.4), kind=kOutput, calls=%fused_computation | convolution fusion | flops 1075970048 | bytes 8390656 | tf_op jit(solution)/shard_map/api,fcais->fcaps/dot_general | solution.py:70
  23.6 2.2 %copy-done = bf16[2,2,2,256,1024]{4,3,2,1,0:T(8,128)(2,1)S(1)} copy-done((bf16[2,2,2,256,1024]{4,3,2,1,0:T(8,128)(2,1)S(1)}, bf16[2,2,2,256,1024]{4,3,2,1,0:T(8,128)(2,1)}, u32[]{:S(2)}) %copy-start) | copy-done | bytes 4194328
  25.8 7.3 %shard_map.46 = f32[2,8,512]{2,1,0:T(8,128)S(1)} custom-call(s32[2]{0:T(128)S(1)} %iota.40.sel_ref, bf16[2,2,2,256,1024]{4,3,2,1,0:T(8,128)(2,1)S(1)} %copy-done, bf16[2,2,2,256,1024]{4,3,2,1,0:T(8,128)(2,1)} %bitcast.87), custom_call_target="tpu_custom_call" | custom-call | flops 4294967296 | bytes 8388608 | tf_op jit(solution)/shard_map/pallas_call | solution.py:42
  33.2 0.0 copy-done.3
  33.2 92.9 %all_gather.3 = s32[16,4,2]{1,2,0:T(2,128)S(1)} all-gather(s32[2,4,2]{1,2,0:T(2,128)S(1)} %copy-done.3), channel_id=1, replica_groups=mesh['inp'=8,'freq'=16] {'inp'}, dimensions={0}, use_global_device_ids=true | all-gather | bytes 576 | tf_op jit(solution)/shard_map/all_gather | solution.py:75
  126.0 0.1 constant_dynamic-slice_fusion.2
  126.1 0.1 copy.65
  126.2 0.1 copy.64
  126.3 0.1 copy.66
  126.5 0.3 slice_reduce_fusion.3
  126.7 0.1 broadcast_and_fusion
  126.8 0.5 convolution_bitcast_fusion
  127.3 0.1 multiply_bitcast_fusion.5
  127.4 0.0 collective-permute-done.1.y_ref
  127.4 4.7 %shard_map.48 = f32[1,8,512]{2,1,0:T(8,128)S(1)} custom-call(s32[1]{0:T(128)} %bitcast.17.sel_ref, bf16[2,2,2,256,1024]{4,3,2,1,0:T(8,128)(2,1)} %convert_bitcast_fusion.x_ref, bf16[1,2,2,256,1024]{4,3,2,1,0:T(8,128)(2,1)} %collective-permute-done.1.y_ref), custom_call_target="tpu_custom_call" | custom-call | flops 2147483648 | bytes 4194304 | tf_op jit(solution)/shard_map/pallas_call | solution.py:42
  132.2 0.0 collective-permute-done.2.y_ref
  132.2 4.8 %shard_map.49 = f32[1,8,512]{2,1,0:T(8,128)S(1)} custom-call(s32[1]{0:T(128)} %bitcast.23.sel_ref, bf16[2,2,2,256,1024]{4,3,2,1,0:T(8,128)(2,1)} %convert_bitcast_fusion.x_ref, bf16[1,2,2,256,1024]{4,3,2,1,0:T(8,128)(2,1)} %collective-permute-done.2.y_ref), custom_call_target="tpu_custom_call" | custom-call | flops 2147483648 | bytes 4194304 | tf_op jit(solution)/shard_map/pallas_call | solution.py:42
  137.0 0.0 collective-permute-done.y_ref
  137.0 4.1 %shard_map.47 = f32[1,8,512]{2,1,0:T(8,128)S(1)} custom-call(s32[1]{0:T(128)} %bitcast.11.sel_ref, bf16[2,2,2,256,1024]{4,3,2,1,0:T(8,128)(2,1)} %convert_bitcast_fusion.x_ref, bf16[1,2,2,256,1024]{4,3,2,1,0:T(8,128)(2,1)S(1)} %collective-permute-done.y_ref), custom_call_target="tpu_custom_call" | custom-call | flops 2147483648 | bytes 4194304 | tf_op jit(solution)/shard_map/pallas_call | solution.py:42
  141.1 0.4 convolution_bitcast_fusion.6
  141.5 0.1 multiply_bitcast_fusion.2
  141.6 0.4 convolution_bitcast_fusion.5
  142.0 0.4 convolution_bitcast_fusion.4
  142.4 0.2 multiply_bitcast_fusion
  142.6 0.2 slice_add_fusion.1
  142.9 0.5 reverse
  143.4 0.4 convolution_bitcast_fusion.2
  143.8 0.4 convolution_bitcast_fusion.3
  144.2 0.4 convolution_bitcast_fusion.1
  144.6 0.2 add_bitcast_fusion
  144.7 1.0 fusion
  145.7 0.0 reduce-scatter.2.cloned.1.call-update
  145.8 37.9 %reduce-scatter.2.cloned.1.call-done = f32[8,2,2,511]{3,0,2,1:T(8,128)} async-done(((f32[64,2,2,511]{3,0,2,1:T(8,128)}), f32[8,2,2,511]{3,0,2,1:T(8,128)}) %reduce-scatter.2.cloned.1.call-update) | async-done | bytes 65424 | tf_op jit(solution)/shard_map/reduce_scatter | solution.py:103
  183.7 1.5 copy.49
  (14 shorter events, 0.1 us)
Async XLA Ops:
  6.5 177.2 %reduce-scatter.2.cloned.1.call-start = ((), (), s32[]{:S(2)}) async-start(), calls=%async_computation.1 | async-start | bytes 589824 | tf_op jit(solution)/shard_map/reduce_scatter | solution.py:103
  11.2 4.8 %copy-start.1 = (bf16[2,256,2,2,1024]{4,1,0,3,2:T(8,128)(2,1)}, bf16[2,256,2,2,1024]{4,1,0,3,2:T(8,128)(2,1)S(1)}, u32[]{:S(2)}) copy-start(bf16[2,256,2,2,1024]{4,1,0,3,2:T(8,128)(2,1)S(1)} %convolution_convert_fusion) | copy-start | bytes 12582916
  11.2 9.2 %copy-start.2 = (bf16[2,2,512,1024]{3,2,1,0:T(8,128)(2,1)S(1)}, bf16[2,2,512,1024]{3,2,1,0:T(8,128)(2,1)}, u32[]{:S(2)}) copy-start(bf16[2,2,512,1024]{3,2,1,0:T(8,128)(2,1)} %param.4) | copy-start | bytes 12582916
  11.2 9.2 %copy-start.4 = (s32[2,256]{1,0:T(2,128)S(1)}, s32[2,256]{1,0:T(2,128)}, u32[]{:S(2)}) copy-start(s32[2,256]{1,0:T(2,128)} %param.5) | copy-start | bytes 6148
  16.0 111.4 %collective-permute-start.1 = (bf16[1,2,2,256,1024]{4,3,2,1,0:T(8,128)(2,1)}, bf16[1,2,2,256,1024]{4,3,2,1,0:T(8,128)(2,1)}, u32[]{:S(2)}, u32[]{:S(2)}) collective-permute-start(bf16[1,2,2,256,1024]{4,3,2,1,0:T(8,128)(2,1)} %get-tuple-element.11), channel_id=1, source_target_pairs={{0,32},{16,48},{32,0},{48,16},{64,96},{80,112},{96,64},{112,80},{1... | collective-permute-start | bytes 6291464 | tf_op jit(solution)/shard_map/ppermute | solution.py:91
  17.5 114.7 %collective-permute-start.2 = (bf16[1,2,2,256,1024]{4,3,2,1,0:T(8,128)(2,1)}, bf16[1,2,2,256,1024]{4,3,2,1,0:T(8,128)(2,1)}, u32[]{:S(2)}, u32[]{:S(2)}) collective-permute-start(bf16[1,2,2,256,1024]{4,3,2,1,0:T(8,128)(2,1)} %get-tuple-element.10), channel_id=1, source_target_pairs={{0,64},{16,80},{32,96},{48,112},{64,0},{80,16},{96,32},{112,48},{1... | collective-permute-start | bytes 6291464 | tf_op jit(solution)/shard_map/ppermute | solution.py:91
  20.2 116.7 %collective-permute-start = (bf16[1,2,2,256,1024]{4,3,2,1,0:T(8,128)(2,1)}, bf16[1,2,2,256,1024]{4,3,2,1,0:T(8,128)(2,1)S(1)}, u32[]{:S(2)}, u32[]{:S(2)}) collective-permute-start(bf16[1,2,2,256,1024]{4,3,2,1,0:T(8,128)(2,1)} %get-tuple-element.9), channel_id=1, source_target_pairs={{0,16},{16,0},{32,48},{48,32},{64,80},{80,64},{96,112},{112,96},{1... | collective-permute-start | bytes 6291464 | tf_op jit(solution)/shard_map/ppermute | solution.py:91
  23.6 2.2 %copy-start = (bf16[2,2,2,256,1024]{4,3,2,1,0:T(8,128)(2,1)S(1)}, bf16[2,2,2,256,1024]{4,3,2,1,0:T(8,128)(2,1)}, u32[]{:S(2)}) copy-start(bf16[2,2,2,256,1024]{4,3,2,1,0:T(8,128)(2,1)} %convert_bitcast_fusion.x_ref) | copy-start | bytes 12582916
  25.8 7.4 %copy-start.3 = (s32[2,4,2]{1,2,0:T(2,128)S(1)}, s32[2,4,2]{1,2,0:T(2,128)}, u32[]{:S(2)}) copy-start(s32[2,4,2]{1,2,0:T(2,128)} %param.6) | copy-start | bytes 196
  25.8 101.5 %copy-start.5 = (f32[2]{0:T(128)S(1)}, f32[2]{0:T(128)}, u32[]{:S(2)}) copy-start(f32[2]{0:T(128)} %constant.36.clone) | copy-start | bytes 28
Sparse Core Ops, SparseCore 0:
  145.9 37.7 reduce-scatter.1
where the time goes:
time: 196 us; the launch traced here: 192 us
  blocking collectives  92.9 us (47%)
  waiting for transfers between devices  38 us (19%)
  Pallas kernels  20.9 us (11%)
  between operations  13.7 us (7%)
  local copies, waits for them, and re-layouts  10.1 us (5%)
  matrix products  9.53 us (5%)
  starting transfers between devices  4.33 us (2%)
  other arithmetic  2.68 us (1%)
    all_gather x1, blocking collectives, on_device(): tg_all = lax.all_gather(tile_group, 'inp', tiled=True)  92.9 us
    reduce_scatter x1, waiting for transfers between devices, on_device(): return lax.psum_scatter(dense, 'inp', scatter_dimension=0, tiled=True)  37.9 us
    pallas_call x4, Pallas kernels, pair_lags(): pl.pallas_call(lag_kernel, out_shape=jax.ShapeDtypeStruct((n, 8, 2 * widt...  20.9 us
    unnamed x13, local copies, waits for them, and re-layouts  4.36 us
    ppermute x3, starting transfers between devices, on_device(): got = lax.ppermute(send, 'inp', [(i, i ^ 1 << bit) for i in range(n_inp)])  4.33 us
  transfers between devices with their start and end apart: 4, of which 1 were waited for; matrix products, arithmetic and copies ran while one was open for 2% of the time, Pallas kernels for 9%

commit v1 on v0

--- a/solution.py
+++ b/solution.py
@@ -8,6 +8,7 @@
 RG_DEV = 8
 HIGH = lax.Precision.HIGHEST
 NT = (((1,), (1,)), ((), ()))
+MESH = pl.DeviceIdType.MESH
 
 
 def lag_kernel(sel_ref, x_ref, y_ref, o_ref):
@@ -55,6 +56,52 @@
     )(sel, x_all, y_all)
 
 
+def scatter_kernel(dense_ref, out_ref, recv, send_sem, recv_sem):
+    n = dense_ref.shape[0]
+    me = lax.axis_index("inp")
+    fq = lax.axis_index("freq")
+    barrier = pltpu.get_barrier_semaphore()
+    for o in range(1, n):
+        pl.semaphore_signal(barrier, inc=1, device_id=(lax.rem(me + o, n), fq), device_id_type=MESH)
+    pl.semaphore_wait(barrier, n - 1)
+    copies = []
+    for o in range(1, n):
+        target = lax.rem(me + o, n)
+        copy = pltpu.make_async_remote_copy(
+            src_ref=dense_ref.at[target],
+            dst_ref=recv.at[o - 1],
+            send_sem=send_sem.at[o - 1],
+            recv_sem=recv_sem.at[o - 1],
+            device_id=(target, fq),
+            device_id_type=MESH,
+        )
+        copy.start()
+        copies.append(copy)
+    for copy in copies:
+        copy.wait()
+    total = dense_ref[me]
+    for o in range(n - 1):
+        total = total + recv[o]
+    out_ref[...] = total
+
+
+def reduce_scatter(dense):
+    n = dense.shape[0]
+    slab = dense.shape[1:]
+    return pl.pallas_call(
+        scatter_kernel,
+        out_shape=jax.ShapeDtypeStruct(slab, jnp.float32),
+        in_specs=[pl.BlockSpec(memory_space=pltpu.VMEM)],
+        out_specs=pl.BlockSpec(memory_space=pltpu.VMEM),
+        scratch_shapes=[
+            pltpu.VMEM((n - 1,) + slab, jnp.float32),
+            pltpu.SemaphoreType.DMA((n - 1,)),
+            pltpu.SemaphoreType.DMA((n - 1,)),
+        ],
+        compiler_params=pltpu.CompilerParams(collective_id=0, has_side_effects=True),
+    )(dense)
+
+
 def on_device(volts, position_input, tile_group):
     blocks, width = position_input.shape
     channels, _, _, samples = volts.shape
@@ -63,16 +110,30 @@
     levels = n_inp.bit_length() - 1
     me = lax.axis_index("inp")
 
+    sent = []
+    for bit in range(levels):
+        mine = (me >> bit) & 1
+        pairs = [(i, i ^ (1 << bit)) for i in range(n_inp)]
+        send = lax.dynamic_index_in_dim(volts, 1 - mine, axis=0, keepdims=True)
+        got = lax.ppermute(send, "inp", pairs)
+        got_pos = lax.ppermute(position_input, "inp", pairs)
+        got_tg = lax.ppermute(tile_group, "inp", pairs)
+        sent.append((mine, got, got_pos, got_tg))
+
     ids = jnp.arange(width, dtype=jnp.int32)
-    perm = (position_input[:, :, None] == ids[None, None, :]).astype(volts.dtype)
-    perm_rev = perm[:, ::-1, :]
-    v5 = volts.reshape(channels, 2, blocks, width, samples)
-    ordered = jnp.einsum("api,fcais->fcaps", perm, v5, preferred_element_type=jnp.float32).astype(volts.dtype)
-    reversed_ = jnp.einsum("api,fcais->fcaps", perm_rev, v5, preferred_element_type=jnp.float32).astype(volts.dtype)
+
+    def reorder(pos, raw, reverse):
+        perm = (pos[:, :, None] == ids[None, None, :]).astype(raw.dtype)
+        if reverse:
+            perm = perm[:, ::-1, :]
+        r5 = raw.reshape(raw.shape[0], 2, blocks, width, samples)
+        return jnp.einsum("api,fcais->fcaps", perm, r5, preferred_element_type=jnp.float32).astype(raw.dtype)
+
+    ordered = reorder(position_input, volts, False)
+    reversed_ = reorder(position_input, volts, True)
 
     groups_all = RG_DEV * n_inp
     group_ids = jnp.arange(groups_all, dtype=jnp.int32)
-    tg_all = lax.all_gather(tile_group, "inp", tiled=True)
 
     lag0 = pair_lags(jnp.arange(channels, dtype=jnp.int32), ordered, reversed_, True)
     lag0 = lag0.reshape(channels, 2, 2, 2, 2 * width)
@@ -85,22 +146,21 @@
     chan_ids = jnp.arange(channels, dtype=jnp.int32)
     sign = jnp.array([1.0, -1.0], jnp.float32)
     for bit in range(levels):
-        partner = me ^ (1 << bit)
-        mine = (me >> bit) & 1
-        send = lax.dynamic_index_in_dim(reversed_, 1 - mine, axis=0, keepdims=True)
-        got = lax.ppermute(send, "inp", [(i, i ^ (1 << bit)) for i in range(n_inp)])
-        lag = pair_lags(mine[None].astype(jnp.int32), ordered, got, False)
+        mine, got, got_pos, got_tg = sent[bit]
+        partner_rev = reorder(got_pos, got, True)
+        lag = pair_lags(mine[None].astype(jnp.int32), ordered, partner_rev, False)
         lag = lag.reshape(2, 2, 2, 2 * width)
         fmask = (chan_ids == mine).astype(jnp.float32)
         w_direct = (tile_group[:, bit + 1, :, None] == group_ids).astype(jnp.float32)
-        tg_partner = lax.dynamic_slice_in_dim(tg_all, partner * blocks, blocks, axis=0)
-        w_trans = (tg_partner[:, bit + 1, :, None] == group_ids).astype(jnp.float32)
+        w_trans = (got_tg[:, bit + 1, :, None] == group_ids).astype(jnp.float32)
         dense_rev = dense_rev + jnp.einsum("abg,f,abcj->gfcj", w_direct, fmask, lag, precision=HIGH)
         term = jnp.einsum("bag,f,c,abcj->gfcj", w_trans, fmask, sign, lag, precision=HIGH)
         dense_fwd = term if dense_fwd is None else dense_fwd + term
     dense = jnp.flip(dense_rev[..., :diffs], axis=-1) + dense_fwd[..., :diffs]
     dense = dense * (1.0 / samples)
-    return lax.psum_scatter(dense, "inp", scatter_dimension=0, tiled=True)
+    dense = jnp.pad(dense, [(0, 0)] * 3 + [(0, 1)])
+    dense = dense.reshape((n_inp, RG_DEV) + dense.shape[1:])
+    return reduce_scatter(dense)[..., :diffs]
 
 
 def solution(mesh):

time: 196 us -> 160 us (0.82); the launches traced: 192 us -> 159 us
  blocking collectives: 92.9 us -> 0 us
  waiting for transfers between devices: 38 us -> 76 us
  between operations: 13.7 us -> 0.34 us
  Pallas kernels: 20.9 us -> 31 us
  matrix products: 9.53 us -> 18.6 us
  starting transfers between devices: 4.33 us -> 12.1 us
  local copies, waits for them, and re-layouts: 10.1 us -> 17.4 us
    all_gather x1 -> x0, blocking collectives: 92.9 us -> none  [on_device(): tg_all = lax.all_gather(tile_group, 'inp', tiled=True)]
    ppermute x3 -> x9, waiting for transfers between devices: 0.01 us -> 76 us  [the longest x3 74.6 us: on_device(): got_tg = lax.ppermute(tile_group, 'inp', pairs)]
    reduce_scatter x1 -> x0, waiting for transfers between devices: 37.9 us -> none  [on_device(): return lax.psum_scatter(dense, 'inp', scatter_dimension=0, tiled=True)]
    pallas_call x0 -> x1, Pallas kernels: none -> 11.4 us  [reduce_scatter(): pl.pallas_call(scatter_kernel, out_shape=jax.ShapeDtypeStruct(slab, jnp.f...]
    dot_general x2 -> x5, matrix products: 6.68 us -> 15.7 us  [reorder(): jnp.einsum('api,fcais->fcaps', perm, r5, preferred_element_type=jnp.float32)]
    ppermute x3 -> x9, starting transfers between devices: 4.33 us -> 12.1 us  [the longest x3 4.62 us: on_device(): got = lax.ppermute(send, 'inp', pairs)]
    rev x1 -> x4, local copies, waits for them, and re-layouts: 0.35 us -> 7.03 us  [reorder(): perm = perm[:, ::-1, :]]
    dynamic_slice x1, local copies, waits for them, and re-layouts: 3.17 us -> 6.18 us  [on_device(): send = lax.dynamic_index_in_dim(volts, 1 - mine, axis=0, keepdims=True)]
  transfers between devices with their start and end apart: 4 -> 9, of which waited for: 1 -> 4; matrix products, arithmetic and copies ran while one was open for 2% -> 15% of each run, Pallas kernels for 9% -> 10%
where the time goes in v1:
time: 160 us; the launch traced here: 159 us
  waiting for transfers between devices  76 us (48%)
  Pallas kernels  31 us (19%)
  matrix products  18.6 us (12%)
  local copies, waits for them, and re-layouts  17.4 us (11%)
  starting transfers between devices  12.1 us (8%)
  other arithmetic  3.03 us (2%)
    ppermute x3, waiting for transfers between devices, on_device(): got_tg = lax.ppermute(tile_group, 'inp', pairs)  74.6 us
    pallas_call x4, Pallas kernels, pair_lags(): pl.pallas_call(lag_kernel, out_shape=jax.ShapeDtypeStruct((n, 8, 2 * widt...  19.6 us
    dot_general x5, matrix products, reorder(): jnp.einsum('api,fcais->fcaps', perm, r5, preferred_element_type=jnp.float32)  15.7 us
    pallas_call x1, Pallas kernels, reduce_scatter(): pl.pallas_call(scatter_kernel, out_shape=jax.ShapeDtypeStruct(slab, jnp.f...  11.4 us
    rev x4, local copies, waits for them, and re-layouts, reorder(): perm = perm[:, ::-1, :]  7.03 us
    dynamic_slice x1, local copies, waits for them, and re-layouts, on_device(): send = lax.dynamic_index_in_dim(volts, 1 - mine, axis=0, keepdims=True)  6.18 us
    ppermute x3, starting transfers between devices, on_device(): got = lax.ppermute(send, 'inp', pairs)  4.62 us
    ppermute x3, starting transfers between devices, on_device(): got_pos = lax.ppermute(position_input, 'inp', pairs)  3.85 us
  transfers between devices with their start and end apart: 9, of which 4 were waited for; matrix products, arithmetic and copies ran while one was open for 15% of the time, Pallas kernels for 10%

profile of v1, /device:TPU:32, one launch (start us, length us, event | category | flops | bytes accessed | tf_op | source)
XLA Modules:
  0.0 158.5 jit_solution(8225329073494457445)
XLA Ops:
  0.0 6.2 %constant_dynamic-slice_fusion.2 = (bf16[1,2,512,1024]{3,2,1,0:T(8,128)(2,1)S(1)}, bf16[1,2,512,1024]{3,2,1,0:T(8,128)(2,1)}, bf16[1,2,512,1024]{3,2,1,0:T(8,128)(2,1)}) fusion(bf16[2,2,512,1024]{3,2,1,0:T(8,128)(2,1)} %param.4, s32[]{:T(128)S(6)} %select_n.15, s32[]{:T(128)S(6)} %select_n.17, s32[]{:T(128)S(6)} %select_n.16), kind=kLoop, calls=%fused_computation.87 | loop fusion | bytes 12582924 | tf_op jit(solution)/shard_map/jit(dynamic_index_in_dim)/dynamic_slice | solution.py:117
  6.2 1.5 collective-permute-start.2
  7.7 0.5 collective-permute-start.3
  8.2 3.0 %collective-permute-start.4 = (bf16[1,2,512,1024]{3,2,1,0:T(8,128)(2,1)}, bf16[1,2,512,1024]{3,2,1,0:T(8,128)(2,1)}, u32[]{:S(2)}, u32[]{:S(2)}) collective-permute-start(bf16[1,2,512,1024]{3,2,1,0:T(8,128)(2,1)} %get-tuple-element.10), channel_id=1, source_target_pairs={{0,64},{16,80},{32,96},{48,112},{64,0},{80,16},{96,32},{112,48},{1... | collective-permute-start | bytes 6291464 | tf_op jit(solution)/shard_map/ppermute | solution.py:118
  11.2 0.1 collective-permute-start
  11.4 0.6 collective-permute-start.7
  12.0 0.1 fusion.1
  12.1 3.2 %convert_bitcast_fusion.1.x_ref = bf16[2,2,2,256,1024]{4,3,2,1,0:T(8,128)(2,1)} fusion(bf16[2,2,2,256,1024]{4,3,2,1,0:T(8,128)(2,1)S(1)} %bitcast.112, s32[2,256]{1,0:T(2,128)S(1)} %copy-done.3), kind=kOutput, calls=%fused_computation.1 | convolution fusion | flops 1075970048 | bytes 8390656 | tf_op jit(solution)/shard_map/api,fcais->fcaps/dot_general | solution.py:130
  15.4 0.3 rev.16
  15.7 5.6 %convert_bitcast_fusion.y_ref = bf16[2,2,2,256,1024]{4,3,2,1,0:T(8,128)(2,1)} fusion(bf16[2,2,2,256,1024]{4,3,2,1,0:T(8,128)(2,1)} %bitcast.111, bf16[2,256,256]{2,1,0:T(8,128)(2,1)S(1)} %rev.16), kind=kOutput, calls=%fused_computation | convolution fusion | flops 1075838976 | bytes 8650752 | tf_op jit(solution)/shard_map/api,fcais->fcaps/dot_general | solution.py:130
  21.3 7.2 %shard_map.46 = f32[2,8,512]{2,1,0:T(8,128)S(1)} custom-call(s32[2]{0:T(128)S(1)} %iota.40.sel_ref, bf16[2,2,2,256,1024]{4,3,2,1,0:T(8,128)(2,1)S(1)} %copy-done, bf16[2,2,2,256,1024]{4,3,2,1,0:T(8,128)(2,1)} %convert_bitcast_fusion.y_ref), custom_call_target="tpu_custom_call" | custom-call | flops 4294967296 | bytes 8388608 | tf_op jit(solution)/shard_map/pallas_call | solution.py:43
  28.6 0.3 slice_reduce_fusion.3
  29.0 0.5 convolution_bitcast_fusion
  29.5 69.3 %collective-permute-done.7 = s32[2,4,2]{1,2,0:T(2,128)S(1)} collective-permute-done((s32[2,4,2]{1,2,0:T(2,128)S(1)}, s32[2,4,2]{1,2,0:T(2,128)S(1)}, u32[]{:S(2)}, u32[]{:S(2)}) %collective-permute-start.7) | collective-permute-done | bytes 96 | tf_op jit(solution)/shard_map/ppermute | solution.py:120
  99.0 3.4 %collective-permute-done.6 = s32[2,4,2]{1,2,0:T(2,128)S(1)} collective-permute-done((s32[2,4,2]{1,2,0:T(2,128)S(1)}, s32[2,4,2]{1,2,0:T(2,128)S(1)}, u32[]{:S(2)}, u32[]{:S(2)}) %collective-permute-start.6) | collective-permute-done | bytes 96 | tf_op jit(solution)/shard_map/ppermute | solution.py:120
  102.4 3.0 %collective-permute-start.8 = (s32[2,4,2]{1,2,0:T(2,128)S(1)}, s32[2,4,2]{1,2,0:T(2,128)S(1)}, u32[]{:S(2)}, u32[]{:S(2)}) collective-permute-start(s32[2,4,2]{1,2,0:T(2,128)S(1)} %copy-done.2), channel_id=1, source_target_pairs={{0,64},{16,80},{32,96},{48,112},{64,0},{80,16},{96,32},{112,48},{1... | collective-permute-start | bytes 200 | tf_op jit(solution)/shard_map/ppermute | solution.py:120
  105.6 1.9 %collective-permute-done.8 = s32[2,4,2]{1,2,0:T(2,128)S(1)} collective-permute-done((s32[2,4,2]{1,2,0:T(2,128)S(1)}, s32[2,4,2]{1,2,0:T(2,128)S(1)}, u32[]{:S(2)}, u32[]{:S(2)}) %collective-permute-start.8) | collective-permute-done | bytes 96 | tf_op jit(solution)/shard_map/ppermute | solution.py:120
  107.5 3.0 %collective-permute-start.5 = (s32[2,256]{1,0:T(2,128)S(1)}, s32[2,256]{1,0:T(2,128)S(1)}, u32[]{:S(2)}, u32[]{:S(2)}) collective-permute-start(s32[2,256]{1,0:T(2,128)S(1)} %copy-done.3), channel_id=1, source_target_pairs={{0,64},{16,80},{32,96},{48,112},{64,0},{80,16},{96,32},{112,48},{1... | collective-permute-start | bytes 6152 | tf_op jit(solution)/shard_map/ppermute | solution.py:119
  110.7 0.3 collective-permute-start.1
  111.0 0.1 fusion.5
  111.1 1.5 collective-permute-done.5
  112.6 0.8 fusion.6
  113.4 0.3 rev.18
  113.7 3.2 %rev.19 = bf16[2,256,256]{2,1,0:T(8,128)(2,1)S(1)} reverse(bf16[2,256,256]{2,1,0:T(8,128)(2,1)} %fusion.6), dimensions={1} | reverse | bytes 524288 | tf_op jit(solution)/shard_map/rev | solution.py:128
  117.0 0.8 fusion.4
  117.8 3.2 %rev.17 = bf16[2,256,256]{2,1,0:T(8,128)(2,1)S(1)} reverse(bf16[2,256,256]{2,1,0:T(8,128)(2,1)} %fusion.4), dimensions={1} | reverse | bytes 524288 | tf_op jit(solution)/shard_map/rev | solution.py:128
  121.0 2.3 %convert_bitcast_fusion.3.y_ref = bf16[1,2,2,256,1024]{4,3,2,1,0:T(8,128)(2,1)S(1)} fusion(bf16[2,2,256,1024]{3,2,1,0:T(8,128)(2,1)} %bitcast.21, bf16[2,256,256]{2,1,0:T(8,128)(2,1)S(1)} %rev.18), kind=kOutput, calls=%fused_computation.3 | convolution fusion | flops 537919488 | bytes 4456448 | tf_op jit(solution)/shard_map/api,fcais->fcaps/dot_general | solution.py:130
  123.3 4.1 %shard_map.48 = f32[1,8,512]{2,1,0:T(8,128)S(1)} custom-call(s32[1]{0:T(128)} %bitcast.20.sel_ref, bf16[2,2,2,256,1024]{4,3,2,1,0:T(8,128)(2,1)} %convert_bitcast_fusion.1.x_ref, bf16[1,2,2,256,1024]{4,3,2,1,0:T(8,128)(2,1)S(1)} %convert_bitcast_fusion.3.y_ref), custom_call_target="tpu_custom_call" | custom-call | flops 2147483648 | bytes 4194304 | tf_op jit(solution)/shard_map/pallas_call | solution.py:43
  127.5 2.3 %convert_bitcast_fusion.2.y_ref = bf16[1,2,2,256,1024]{4,3,2,1,0:T(8,128)(2,1)S(1)} fusion(bf16[2,2,256,1024]{3,2,1,0:T(8,128)(2,1)} %bitcast.30, bf16[2,256,256]{2,1,0:T(8,128)(2,1)S(1)} %rev.19), kind=kOutput, calls=%fused_computation.2 | convolution fusion | flops 537919488 | bytes 4456448 | tf_op jit(solution)/shard_map/api,fcais->fcaps/dot_general | solution.py:130
  129.8 4.1 %shard_map.49 = f32[1,8,512]{2,1,0:T(8,128)S(1)} custom-call(s32[1]{0:T(128)} %bitcast.29.sel_ref, bf16[2,2,2,256,1024]{4,3,2,1,0:T(8,128)(2,1)} %convert_bitcast_fusion.1.x_ref, bf16[1,2,2,256,1024]{4,3,2,1,0:T(8,128)(2,1)S(1)} %convert_bitcast_fusion.2.y_ref), custom_call_target="tpu_custom_call" | custom-call | flops 2147483648 | bytes 4194304 | tf_op jit(solution)/shard_map/pallas_call | solution.py:43
  133.9 2.3 %convert_bitcast_fusion.4.y_ref = bf16[1,2,2,256,1024]{4,3,2,1,0:T(8,128)(2,1)S(1)} fusion(bf16[2,2,256,1024]{3,2,1,0:T(8,128)(2,1)} %bitcast.12, bf16[2,256,256]{2,1,0:T(8,128)(2,1)S(1)} %rev.17), kind=kOutput, calls=%fused_computation.4 | convolution fusion | flops 537919488 | bytes 4456448 | tf_op jit(solution)/shard_map/api,fcais->fcaps/dot_general | solution.py:130
  136.3 4.1 %shard_map.47 = f32[1,8,512]{2,1,0:T(8,128)S(1)} custom-call(s32[1]{0:T(128)} %bitcast.11.sel_ref, bf16[2,2,2,256,1024]{4,3,2,1,0:T(8,128)(2,1)} %convert_bitcast_fusion.1.x_ref, bf16[1,2,2,256,1024]{4,3,2,1,0:T(8,128)(2,1)S(1)} %convert_bitcast_fusion.4.y_ref), custom_call_target="tpu_custom_call" | custom-call | flops 2147483648 | bytes 4194304 | tf_op jit(solution)/shard_map/pallas_call | solution.py:43
  140.4 0.4 convolution_bitcast_fusion.6
  140.8 0.1 multiply_bitcast_fusion.2
  140.9 0.4 convolution_bitcast_fusion.5
  141.3 0.4 convolution_bitcast_fusion.4
  141.7 0.2 multiply_bitcast_fusion
  141.9 0.2 slice_add_fusion.1
  142.1 0.5 reverse
  142.7 0.4 convolution_bitcast_fusion.2
  143.1 0.4 convolution_bitcast_fusion.3
  143.4 0.4 convolution_bitcast_fusion.1
  143.8 0.2 add_bitcast_fusion
  144.0 0.2 fusion
  144.2 0.4 copy.67
  144.6 1.0 pad.4.clone
  145.6 11.4 %shard_map.50 = f32[8,2,2,512]{3,2,1,0:T(2,128)} custom-call(f32[8,8,2,2,512]{4,3,2,1,0:T(2,128)} %bitcast.114), custom_call_target="tpu_custom_call" | custom-call | tf_op jit(solution)/shard_map/pallas_call | solution.py:91
  157.1 1.5 copy.83
  (34 shorter events, 0.8 us)
Async XLA Ops:
  0.0 7.7 %copy-start.3 = (s32[2,256]{1,0:T(2,128)S(1)}, s32[2,256]{1,0:T(2,128)}, u32[]{:S(2)}) copy-start(s32[2,256]{1,0:T(2,128)} %param.5) | copy-start | bytes 6148
  0.0 11.4 %copy-start.2 = (s32[2,4,2]{1,2,0:T(2,128)S(1)}, s32[2,4,2]{1,2,0:T(2,128)}, u32[]{:S(2)}) copy-start(s32[2,4,2]{1,2,0:T(2,128)} %param.6) | copy-start | bytes 196
  0.0 12.1 %copy-start.1 = (bf16[2,2,512,1024]{3,2,1,0:T(8,128)(2,1)S(1)}, bf16[2,2,512,1024]{3,2,1,0:T(8,128)(2,1)}, u32[]{:S(2)}) copy-start(bf16[2,2,512,1024]{3,2,1,0:T(8,128)(2,1)} %param.4) | copy-start | bytes 12582916
  6.2 114.8 %collective-permute-start.2 = (bf16[1,2,512,1024]{3,2,1,0:T(8,128)(2,1)}, bf16[1,2,512,1024]{3,2,1,0:T(8,128)(2,1)}, u32[]{:S(2)}, u32[]{:S(2)}) collective-permute-start(bf16[1,2,512,1024]{3,2,1,0:T(8,128)(2,1)} %get-tuple-element.11), channel_id=1, source_target_pairs={{0,32},{16,48},{32,0},{48,16},{64,96},{80,112},{96,64},{112,80},{1... | collective-permute-start | bytes 6291464 | tf_op jit(solution)/shard_map/ppermute | solution.py:118
  7.7 103.0 %collective-permute-start.3 = (s32[2,256]{1,0:T(2,128)S(1)}, s32[2,256]{1,0:T(2,128)S(1)}, u32[]{:S(2)}, u32[]{:S(2)}) collective-permute-start(s32[2,256]{1,0:T(2,128)S(1)} %copy-done.3), channel_id=1, source_target_pairs={{0,32},{16,48},{32,0},{48,16},{64,96},{80,112},{96,64},{112,80},{1... | collective-permute-start | bytes 6152 | tf_op jit(solution)/shard_map/ppermute | solution.py:119
  8.2 119.3 %collective-permute-start.4 = (bf16[1,2,512,1024]{3,2,1,0:T(8,128)(2,1)}, bf16[1,2,512,1024]{3,2,1,0:T(8,128)(2,1)}, u32[]{:S(2)}, u32[]{:S(2)}) collective-permute-start(bf16[1,2,512,1024]{3,2,1,0:T(8,128)(2,1)} %get-tuple-element.10), channel_id=1, source_target_pairs={{0,64},{16,80},{32,96},{48,112},{64,0},{80,16},{96,32},{112,48},{1... | collective-permute-start | bytes 6291464 | tf_op jit(solution)/shard_map/ppermute | solution.py:118
  11.2 122.7 %collective-permute-start = (bf16[1,2,512,1024]{3,2,1,0:T(8,128)(2,1)S(1)}, bf16[1,2,512,1024]{3,2,1,0:T(8,128)(2,1)}, u32[]{:S(2)}, u32[]{:S(2)}) collective-permute-start(bf16[1,2,512,1024]{3,2,1,0:T(8,128)(2,1)S(1)} %get-tuple-element.9), channel_id=1, source_target_pairs={{0,16},{16,0},{32,48},{48,32},{64,80},{80,64},{96,112},{112,96},{1... | collective-permute-start | bytes 6291464 | tf_op jit(solution)/shard_map/ppermute | solution.py:118
  11.4 87.4 %collective-permute-start.7 = (s32[2,4,2]{1,2,0:T(2,128)S(1)}, s32[2,4,2]{1,2,0:T(2,128)S(1)}, u32[]{:S(2)}, u32[]{:S(2)}) collective-permute-start(s32[2,4,2]{1,2,0:T(2,128)S(1)} %copy-done.2), channel_id=1, source_target_pairs={{0,32},{16,48},{32,0},{48,16},{64,96},{80,112},{96,64},{112,80},{1... | collective-permute-start | bytes 200 | tf_op jit(solution)/shard_map/ppermute | solution.py:120
  15.7 5.6 %copy-start = (bf16[2,2,2,256,1024]{4,3,2,1,0:T(8,128)(2,1)S(1)}, bf16[2,2,2,256,1024]{4,3,2,1,0:T(8,128)(2,1)}, u32[]{:S(2)}) copy-start(bf16[2,2,2,256,1024]{4,3,2,1,0:T(8,128)(2,1)} %convert_bitcast_fusion.1.x_ref) | copy-start | bytes 12582916
  21.3 7.7 %copy-start.4 = (f32[2]{0:T(128)S(1)}, f32[2]{0:T(128)}, u32[]{:S(2)}) copy-start(f32[2]{0:T(128)} %constant.33.clone) | copy-start | bytes 28
  98.8 3.6 %collective-permute-start.6 = (s32[2,4,2]{1,2,0:T(2,128)S(1)}, s32[2,4,2]{1,2,0:T(2,128)S(1)}, u32[]{:S(2)}, u32[]{:S(2)}) collective-permute-start(s32[2,4,2]{1,2,0:T(2,128)S(1)} %copy-done.2), channel_id=1, source_target_pairs={{0,16},{16,0},{32,48},{48,32},{64,80},{80,64},{96,112},{112,96},{1... | collective-permute-start | bytes 200 | tf_op jit(solution)/shard_map/ppermute | solution.py:120
  102.4 5.1 %collective-permute-start.8 = (s32[2,4,2]{1,2,0:T(2,128)S(1)}, s32[2,4,2]{1,2,0:T(2,128)S(1)}, u32[]{:S(2)}, u32[]{:S(2)}) collective-permute-start(s32[2,4,2]{1,2,0:T(2,128)S(1)} %copy-done.2), channel_id=1, source_target_pairs={{0,64},{16,80},{32,96},{48,112},{64,0},{80,16},{96,32},{112,48},{1... | collective-permute-start | bytes 200 | tf_op jit(solution)/shard_map/ppermute | solution.py:120
  107.5 5.1 %collective-permute-start.5 = (s32[2,256]{1,0:T(2,128)S(1)}, s32[2,256]{1,0:T(2,128)S(1)}, u32[]{:S(2)}, u32[]{:S(2)}) collective-permute-start(s32[2,256]{1,0:T(2,128)S(1)} %copy-done.3), channel_id=1, source_target_pairs={{0,64},{16,80},{32,96},{48,112},{64,0},{80,16},{96,32},{112,48},{1... | collective-permute-start | bytes 6152 | tf_op jit(solution)/shard_map/ppermute | solution.py:119
  110.7 6.3 %collective-permute-start.1 = (s32[2,256]{1,0:T(2,128)S(1)}, s32[2,256]{1,0:T(2,128)S(1)}, u32[]{:S(2)}, u32[]{:S(2)}) collective-permute-start(s32[2,256]{1,0:T(2,128)S(1)} %copy-done.3), channel_id=1, source_target_pairs={{0,16},{16,0},{32,48},{48,32},{64,80},{80,64},{96,112},{112,96},{1... | collective-permute-start | bytes 6152 | tf_op jit(solution)/shard_map/ppermute | solution.py:119

commit v2 on v1

--- a/solution.py
+++ b/solution.py
@@ -11,15 +11,24 @@
 MESH = pl.DeviceIdType.MESH
 
 
-def lag_kernel(sel_ref, x_ref, y_ref, o_ref):
-    width = x_ref.shape[3]
+def lag_kernel(sel_ref, xraw_ref, xperm_ref, yraw_ref, yperm_ref, o_ref, xs, ys):
+    width = xperm_ref.shape[1]
+    for blk in range(2):
+        for c in range(2):
+            rows = pl.ds(blk * width, width)
+            xs[blk, c] = jnp.dot(
+                xperm_ref[blk], xraw_ref[0, c, rows, :], preferred_element_type=jnp.float32
+            ).astype(xs.dtype)
+            ys[blk, c] = jnp.dot(
+                yperm_ref[blk], yraw_ref[0, c, rows, :], preferred_element_type=jnp.float32
+            ).astype(ys.dtype)
+    dot = lambda u, v: lax.dot_general(u, v, NT, preferred_element_type=jnp.float32)
     for a in range(2):
-        xre = x_ref[0, 0, a]
-        xim = x_ref[0, 1, a]
+        xre = xs[a, 0]
+        xim = xs[a, 1]
         for b in range(2):
-            yre = y_ref[0, 0, b]
-            yim = y_ref[0, 1, b]
-            dot = lambda u, v: lax.dot_general(u, v, NT, preferred_element_type=jnp.float32)
+            yre = ys[b, 0]
+            yim = ys[b, 1]
             real_part = dot(xre, yre) + dot(xim, yim)
             imag_part = dot(xim, yre) - dot(xre, yim)
             for c, part in enumerate((real_part, imag_part)):
@@ -27,33 +36,39 @@
                 sheared = pltpu.roll(padded, 0, 1, stride=1, stride_axis=0)
                 row = (a * 2 + b) * 2 + c
                 o_ref[0, pl.ds(row, 1), :] = jnp.sum(sheared, axis=0, keepdims=True)
-    del width
 
 
-def pair_lags(sel, x_all, y_all, y_by_sel):
+def pair_lags(sel, x_raw, x_perm, y_raw, y_perm, y_by_sel):
     n = sel.shape[0]
-    _, _, _, width, samples = x_all.shape
-    x_spec = pl.BlockSpec((1, 2, 2, width, samples), lambda i, s: (s[i], 0, 0, 0, 0))
+    _, _, rows_x, samples = x_raw.shape
+    rows_y = y_raw.shape[2]
+    width = x_perm.shape[1]
+    x_spec = pl.BlockSpec((1, 2, rows_x, samples), lambda i, s: (s[i], 0, 0, 0))
     if y_by_sel:
-        y_spec = pl.BlockSpec((1, 2, 2, width, samples), lambda i, s: (s[i], 0, 0, 0, 0))
+        y_spec = pl.BlockSpec((1, 2, rows_y, samples), lambda i, s: (s[i], 0, 0, 0))
     else:
-        y_spec = pl.BlockSpec((1, 2, 2, width, samples), lambda i, s: (i, 0, 0, 0, 0))
+        y_spec = pl.BlockSpec((1, 2, rows_y, samples), lambda i, s: (i, 0, 0, 0))
+    perm_spec = pl.BlockSpec((2, width, width), lambda i, s: (0, 0, 0))
     out_spec = pl.BlockSpec((1, 8, 2 * width), lambda i, s: (i, 0, 0))
-    flops = n * 16 * 2 * width * width * samples
+    flops = n * (16 + 8) * 2 * width * width * samples
     return pl.pallas_call(
         lag_kernel,
         out_shape=jax.ShapeDtypeStruct((n, 8, 2 * width), jnp.float32),
         grid_spec=pltpu.PrefetchScalarGridSpec(
             num_scalar_prefetch=1,
             grid=(n,),
-            in_specs=[x_spec, y_spec],
+            in_specs=[x_spec, perm_spec, y_spec, perm_spec],
             out_specs=out_spec,
+            scratch_shapes=[
+                pltpu.VMEM((2, 2, width, samples), x_raw.dtype),
+                pltpu.VMEM((2, 2, width, samples), x_raw.dtype),
+            ],
         ),
         compiler_params=pltpu.CompilerParams(vmem_limit_bytes=48 * 1024 * 1024),
         cost_estimate=pl.CostEstimate(
             flops=flops, transcendentals=0, bytes_accessed=n * 2 * 4 * width * samples * 2
         ),
-    )(sel, x_all, y_all)
+    )(sel, x_raw, x_perm, y_raw, y_perm)
 
 
 def scatter_kernel(dense_ref, out_ref, recv, send_sem, recv_sem):
@@ -104,38 +119,42 @@
 
 def on_device(volts, position_input, tile_group):
     blocks, width = position_input.shape
-    channels, _, _, samples = volts.shape
+    channels, _, rows, samples = volts.shape
     diffs = 2 * width - 1
     n_inp = lax.axis_size("inp")
     levels = n_inp.bit_length() - 1
     me = lax.axis_index("inp")
 
+    pos_row = jnp.pad(position_input.reshape(-1), (0, samples - blocks * width))
+    tg_flat = tile_group.reshape(-1)
+    tg_row = jnp.pad(tg_flat, (0, samples - tg_flat.shape[0]))
+    meta = jnp.zeros((2, 16, samples), jnp.float32)
+    meta = meta.at[0, 0].set(pos_row.astype(jnp.float32)).at[0, 1].set(tg_row.astype(jnp.float32))
+    meta = meta.astype(volts.dtype)
+
     sent = []
     for bit in range(levels):
         mine = (me >> bit) & 1
         pairs = [(i, i ^ (1 << bit)) for i in range(n_inp)]
-        send = lax.dynamic_index_in_dim(volts, 1 - mine, axis=0, keepdims=True)
+        chan = jnp.where(mine == 1, volts[0], volts[1])
+        send = jnp.concatenate([chan, meta], axis=1)[None]
         got = lax.ppermute(send, "inp", pairs)
-        got_pos = lax.ppermute(position_input, "inp", pairs)
-        got_tg = lax.ppermute(tile_group, "inp", pairs)
-        sent.append((mine, got, got_pos, got_tg))
+        sent.append((mine, got))
 
     ids = jnp.arange(width, dtype=jnp.int32)
 
-    def reorder(pos, raw, reverse):
-        perm = (pos[:, :, None] == ids[None, None, :]).astype(raw.dtype)
+    def one_hot(pos, reverse):
         if reverse:
-            perm = perm[:, ::-1, :]
-        r5 = raw.reshape(raw.shape[0], 2, blocks, width, samples)
-        return jnp.einsum("api,fcais->fcaps", perm, r5, preferred_element_type=jnp.float32).astype(raw.dtype)
+            pos = pos[:, ::-1]
+        return (pos[:, :, None] == ids[None, None, :]).astype(volts.dtype)
 
-    ordered = reorder(position_input, volts, False)
-    reversed_ = reorder(position_input, volts, True)
+    perm = one_hot(position_input, False)
+    perm_rev = one_hot(position_input, True)
 
     groups_all = RG_DEV * n_inp
     group_ids = jnp.arange(groups_all, dtype=jnp.int32)
 
-    lag0 = pair_lags(jnp.arange(channels, dtype=jnp.int32), ordered, reversed_, True)
+    lag0 = pair_lags(jnp.arange(channels, dtype=jnp.int32), volts, perm, volts, perm_rev, True)
     lag0 = lag0.reshape(channels, 2, 2, 2, 2 * width)
     center = (jnp.arange(2 * width) == width - 1)
     same = jnp.eye(2, dtype=bool)
@@ -146,9 +165,10 @@
     chan_ids = jnp.arange(channels, dtype=jnp.int32)
     sign = jnp.array([1.0, -1.0], jnp.float32)
     for bit in range(levels):
-        mine, got, got_pos, got_tg = sent[bit]
-        partner_rev = reorder(got_pos, got, True)
-        lag = pair_lags(mine[None].astype(jnp.int32), ordered, partner_rev, False)
+        mine, got = sent[bit]
+        got_pos = got[0, 0, rows, : blocks * width].astype(jnp.int32).reshape(blocks, width)
+        got_tg = got[0, 0, rows + 1, : tg_flat.shape[0]].astype(jnp.int32).reshape(tile_group.shape)
+        lag = pair_lags(mine[None].astype(jnp.int32), volts, perm, got, one_hot(got_pos, True), False)
         lag = lag.reshape(2, 2, 2, 2 * width)
         fmask = (chan_ids == mine).astype(jnp.float32)
         w_direct = (tile_group[:, bit + 1, :, None] == group_ids).astype(jnp.float32)

time: 160 us -> 155 us (0.969)
  matrix products: 18.6 us -> 2.86 us
  other arithmetic: 3.03 us -> 15.6 us
  starting transfers between devices: 12.1 us -> 4.33 us
  waiting for transfers between devices: 76 us -> 81.8 us
  Pallas kernels: 31 us -> 36 us
  local copies, waits for them, and re-layouts: 17.4 us -> 13.8 us
    ppermute x3, waiting for transfers between devices: 0.01 us -> 81.8 us  [on_device(): got = lax.ppermute(send, 'inp', pairs)]
    ppermute x6 -> x0, waiting for transfers between devices: 76 us -> none  [the longest x3 74.6 us: on_device(): got_tg = lax.ppermute(tile_group, 'inp', pairs)]
    dot_general x5 -> x0, matrix products: 15.7 us -> none  [reorder(): jnp.einsum('api,fcais->fcaps', perm, r5, preferred_element_type=jnp.float32)]
    ppermute x6 -> x0, starting transfers between devices: 7.5 us -> none  [the longest x3 3.85 us: on_device(): got_pos = lax.ppermute(position_input, 'inp', pairs)]
    rev x4, local copies, waits for them, and re-layouts: 7.03 us -> 0.82 us  [one_hot(): pos = pos[:, ::-1]]
    dynamic_slice x1 -> x0, local copies, waits for them, and re-layouts: 6.18 us -> none  [on_device(): send = lax.dynamic_index_in_dim(volts, 1 - mine, axis=0, keepdims=True)]
    unnamed x13 -> x15, local copies, waits for them, and re-layouts: 2.41 us -> 7.67 us
    pallas_call x4, Pallas kernels: 19.6 us -> 24.6 us  [pair_lags(): pl.pallas_call(lag_kernel, out_shape=jax.ShapeDtypeStruct((n, 8, 2 * widt...]
  transfers between devices with their start and end apart: 9 -> 3, of which waited for: 4 -> 2; matrix products, arithmetic and copies ran while one was open for 15% -> 3% of each run, Pallas kernels for 10% -> 12%
where the time goes in v2:
time: 155 us
  waiting for transfers between devices  81.8 us (53%)
  Pallas kernels  36 us (23%)
  other arithmetic  15.6 us (10%)
  local copies, waits for them, and re-layouts  13.8 us (9%)
  starting transfers between devices  4.33 us (3%)
  matrix products  2.86 us (2%)
    ppermute x3, waiting for transfers between devices, on_device(): got = lax.ppermute(send, 'inp', pairs)  81.8 us
    pallas_call x4, Pallas kernels, pair_lags(): pl.pallas_call(lag_kernel, out_shape=jax.ShapeDtypeStruct((n, 8, 2 * widt...  24.6 us
    pallas_call x1, Pallas kernels, reduce_scatter(): pl.pallas_call(scatter_kernel, out_shape=jax.ShapeDtypeStruct(slab, jnp.f...  11.4 us
    unnamed x15, local copies, waits for them, and re-layouts  7.67 us
    select_n x1, other arithmetic, on_device(): chan = jnp.where(mine == 1, volts[0], volts[1])  4.56 us
    broadcast_in_dim x1, other arithmetic, on_device(): send = jnp.concatenate([chan, meta], axis=1)[None]  4.41 us
    ppermute x3, starting transfers between devices, on_device(): got = lax.ppermute(send, 'inp', pairs)  4.33 us
  transfers between devices with their start and end apart: 3, of which 2 were waited for; matrix products, arithmetic and copies ran while one was open for 3% of the time, Pallas kernels for 12%

profile of v2, /device:TPU:32, one launch (start us, length us, event | category | flops | bytes accessed | tf_op | source)
XLA Modules:
  0.0 154.6 jit_solution(12040652113655794453)
XLA Ops:
  0.0 0.6 fusion.49
  0.6 0.7 copy.38
  1.3 0.8 copy.18
  2.2 4.6 %select_bitcast_fusion.2 = (bf16[2,512,1024]{2,1,0:T(8,128)(2,1)S(1)}, bf16[2,512,1024]{2,1,0:T(8,128)(2,1)}, bf16[2,512,1024]{2,1,0:T(8,128)(2,1)}) fusion(pred[]{:T(512)S(6)} %eq.236, bf16[2,2,512,1024]{3,2,1,0:T(8,128)(2,1)} %xraw_ref.7, pred[]{:T(512)S(6)} %eq.256, pred[]{:T(512)S(6)} %eq.246), kind=kLoop, calls=%fused_computation.8 | loop fusion | flops 3145728 | bytes 10485763 | tf_op jit(solution)/shard_map/jit(_where)/select_n | solution.py:139
  6.7 1.3 scatter.9
  8.0 4.4 %fusion = (bf16[1,2,528,1024]{3,2,1,0:T(8,128)(2,1)}, bf16[1,2,528,1024]{3,2,1,0:T(8,128)(2,1)}, bf16[1,2,528,1024]{3,2,1,0:T(8,128)(2,1)}) fusion(bf16[2,16,1024]{2,1,0:T(8,128)(2,1)S(1)} %scatter.9, bf16[2,512,1024]{2,1,0:T(8,128)(2,1)S(1)} %get-tuple-element.33, bf16[2,512,1024]{2,1,0:T(8,128)(2,1)} %get-tuple-element.34, ...), kind=kLoop, calls=%fused_computation.3 | loop fusion | flops 10813440 | bytes 12845056 | tf_op jit(solution)/shard_map/broadcast_in_dim | solution.py:140
  12.4 1.5 collective-permute-start.1
  13.9 2.7 %collective-permute-start.2 = (bf16[1,2,528,1024]{3,2,1,0:T(8,128)(2,1)}, bf16[1,2,528,1024]{3,2,1,0:T(8,128)(2,1)}, u32[]{:S(2)}, u32[]{:S(2)}) collective-permute-start(bf16[1,2,528,1024]{3,2,1,0:T(8,128)(2,1)} %get-tuple-element.37), channel_id=1, source_target_pairs={{0,64},{16,80},{32,96},{48,112},{64,0},{80,16},{96,32},{112,48},{1... | collective-permute-start | bytes 6488072 | tf_op jit(solution)/shard_map/ppermute | solution.py:141
  16.7 0.1 collective-permute-start
  16.8 0.2 rev.16
  17.0 0.1 fusion.4.xperm_ref
  17.1 0.1 fusion.5.yperm_ref
  17.3 2.2 %copy-done = bf16[2,2,512,1024]{3,2,1,0:T(8,128)(2,1)S(1)} copy-done((bf16[2,2,512,1024]{3,2,1,0:T(8,128)(2,1)S(1)}, bf16[2,2,512,1024]{3,2,1,0:T(8,128)(2,1)}, u32[]{:S(2)}) %copy-start) | copy-done | bytes 4194328
  19.4 7.8 %shard_map.46 = f32[2,8,512]{2,1,0:T(8,128)S(1)} custom-call(s32[2]{0:T(128)S(1)} %iota.45.sel_ref, bf16[2,2,512,1024]{3,2,1,0:T(8,128)(2,1)S(1)} %copy-done, bf16[2,256,256]{2,1,0:T(8,128)(2,1)S(1)} %fusion.4.xperm_ref, bf16[2,2,512,1024]{3,2,1,0:T(8,128)(2,1)S(1)} %copy-done, bf16[2,256,256]{2,1,0:T(8,128)(2,1)S(1)} %fusion.5.yperm_ref), custom_call_target="tpu_custom_call" | custom-call | flops 6442450944 | bytes 8388608 | tf_op jit(solution)/shard_map/pallas_call | solution.py:54
  27.3 0.3 slice_reduce_fusion.3
  27.6 0.5 convolution_bitcast_fusion
  28.2 34.3 %collective-permute-done.1.yraw_ref = bf16[1,2,528,1024]{3,2,1,0:T(8,128)(2,1)S(1)} collective-permute-done((bf16[1,2,528,1024]{3,2,1,0:T(8,128)(2,1)}, bf16[1,2,528,1024]{3,2,1,0:T(8,128)(2,1)S(1)}, u32[]{:S(2)}, u32[]{:S(2)}) %collective-permute-start.1) | collective-permute-done | bytes 2162720 | tf_op jit(solution)/shard_map/ppermute | solution.py:141
  62.6 47.5 %collective-permute-done.2.yraw_ref = bf16[1,2,528,1024]{3,2,1,0:T(8,128)(2,1)} collective-permute-done((bf16[1,2,528,1024]{3,2,1,0:T(8,128)(2,1)}, bf16[1,2,528,1024]{3,2,1,0:T(8,128)(2,1)}, u32[]{:S(2)}, u32[]{:S(2)}) %collective-permute-start.2) | collective-permute-done | bytes 2162720 | tf_op jit(solution)/shard_map/ppermute | solution.py:141
  110.1 0.7 fusion.31
  110.8 0.2 rev.18
  111.0 0.1 fusion.7.yperm_ref
  111.2 5.2 %shard_map.48 = f32[1,8,512]{2,1,0:T(8,128)S(1)} custom-call(s32[1]{0:T(128)} %bitcast.15.sel_ref, bf16[2,2,512,1024]{3,2,1,0:T(8,128)(2,1)} %xraw_ref.7, bf16[2,256,256]{2,1,0:T(8,128)(2,1)S(1)} %fusion.4.xperm_ref, bf16[1,2,528,1024]{3,2,1,0:T(8,128)(2,1)S(1)} %collective-permute-done.1.yraw_ref, bf16[2,256,256]{2,1,0:T(8,128)(2,1)S(1)} %fusion.7.yperm_ref), custom_call_target="tpu_custom_call" | custom-call | flops 3221225472 | bytes 4194304 | tf_op jit(solution)/shard_map/pallas_call | solution.py:54
  116.4 0.2 rev.19
  116.6 0.1 fusion.8.yperm_ref
  116.7 5.8 %shard_map.49 = f32[1,8,512]{2,1,0:T(8,128)S(1)} custom-call(s32[1]{0:T(128)} %bitcast.22.sel_ref, bf16[2,2,512,1024]{3,2,1,0:T(8,128)(2,1)} %xraw_ref.7, bf16[2,256,256]{2,1,0:T(8,128)(2,1)S(1)} %fusion.4.xperm_ref, bf16[1,2,528,1024]{3,2,1,0:T(8,128)(2,1)} %collective-permute-done.2.yraw_ref, bf16[2,256,256]{2,1,0:T(8,128)(2,1)S(1)} %fusion.8.yperm_ref), custom_call_target="tpu_custom_call" | custom-call | flops 3221225472 | bytes 4194304 | tf_op jit(solution)/shard_map/pallas_call | solution.py:54
  122.6 0.4 convolution_bitcast_fusion.5
  122.9 0.4 convolution_bitcast_fusion.4
  123.3 0.1 multiply_bitcast_fusion.1
  123.5 0.9 multiply_bitcast_fusion
  124.4 0.7 fusion.33
  125.2 0.2 rev.17
  125.4 0.1 fusion.6.yperm_ref
  125.6 5.8 %shard_map.47 = f32[1,8,512]{2,1,0:T(8,128)S(1)} custom-call(s32[1]{0:T(128)} %bitcast.4.sel_ref, bf16[2,2,512,1024]{3,2,1,0:T(8,128)(2,1)} %xraw_ref.7, bf16[2,256,256]{2,1,0:T(8,128)(2,1)S(1)} %fusion.4.xperm_ref, bf16[1,2,528,1024]{3,2,1,0:T(8,128)(2,1)} %collective-permute-done.yraw_ref, bf16[2,256,256]{2,1,0:T(8,128)(2,1)S(1)} %fusion.6.yperm_ref), custom_call_target="tpu_custom_call" | custom-call | flops 3221225472 | bytes 4194304 | tf_op jit(solution)/shard_map/pallas_call | solution.py:54
  131.4 0.4 convolution_bitcast_fusion.6
  131.8 0.8 multiply_bitcast_fusion.2
  132.6 2.1 %slice_add_fusion.1 = f32[64,2,2,511]{3,0,2,1:T(8,128)} fusion(f32[64,2,2,512]{3,0,2,1:T(8,128)} %multiply_bitcast_fusion, f32[64,2,2,512]{3,0,2,1:T(8,128)S(1)} %multiply_bitcast_fusion.1, f32[64,2,2,512]{3,0,2,1:T(8,128)S(1)} %multiply_bitcast_fusion.2, f32[64,2,2,512]{3,0,2,1:T(8,128)S(1)} %convolution_bitcast_fusion), kind=kLoop, calls=%fused_computation.18 | loop fusion | flops 392448 | bytes 2616320 | tf_op jit(solution)/shard_map/add | solution.py:176
  134.7 2.1 %reverse = f32[64,2,2,512]{3,0,2,1:T(8,128)S(1)} reverse(f32[64,2,2,512]{3,0,2,1:T(8,128)} %bitcast.85), dimensions={3} | reverse | bytes 1048576
  136.8 0.7 slice_reduce_fusion.6
  137.7 0.4 convolution_bitcast_fusion.3
  138.1 0.7 slice_reduce_fusion.4
  139.0 0.4 convolution_bitcast_fusion.2
  139.6 0.4 convolution_bitcast_fusion.1
  140.0 0.2 add_bitcast_fusion
  140.2 0.2 fusion.3
  140.4 0.4 copy.37
  140.8 1.0 pad.21.clone
  141.8 11.4 %shard_map.50 = f32[8,2,2,512]{3,2,1,0:T(2,128)} custom-call(f32[8,8,2,2,512]{4,3,2,1,0:T(2,128)} %bitcast.86), custom_call_target="tpu_custom_call" | custom-call | tf_op jit(solution)/shard_map/pallas_call | solution.py:106
  153.2 1.5 copy.55
  (38 shorter events, 1.0 us)
Async XLA Ops:
  8.0 8.8 %copy-start.2 = (s32[2,256]{1,0:T(2,128)S(1)}, s32[2,256]{1,0:T(2,128)}, u32[]{:S(2)}) copy-start(s32[2,256]{1,0:T(2,128)} %param.9) | copy-start | bytes 6148
  12.4 50.1 %collective-permute-start.1 = (bf16[1,2,528,1024]{3,2,1,0:T(8,128)(2,1)}, bf16[1,2,528,1024]{3,2,1,0:T(8,128)(2,1)S(1)}, u32[]{:S(2)}, u32[]{:S(2)}) collective-permute-start(bf16[1,2,528,1024]{3,2,1,0:T(8,128)(2,1)} %get-tuple-element.38), channel_id=1, source_target_pairs={{0,32},{16,48},{32,0},{48,16},{64,96},{80,112},{96,64},{112,80},{1... | collective-permute-start | bytes 6488072 | tf_op jit(solution)/shard_map/ppermute | solution.py:141
  13.9 96.1 %collective-permute-start.2 = (bf16[1,2,528,1024]{3,2,1,0:T(8,128)(2,1)}, bf16[1,2,528,1024]{3,2,1,0:T(8,128)(2,1)}, u32[]{:S(2)}, u32[]{:S(2)}) collective-permute-start(bf16[1,2,528,1024]{3,2,1,0:T(8,128)(2,1)} %get-tuple-element.37), channel_id=1, source_target_pairs={{0,64},{16,80},{32,96},{48,112},{64,0},{80,16},{96,32},{112,48},{1... | collective-permute-start | bytes 6488072 | tf_op jit(solution)/shard_map/ppermute | solution.py:141
  16.7 107.8 %collective-permute-start = (bf16[1,2,528,1024]{3,2,1,0:T(8,128)(2,1)}, bf16[1,2,528,1024]{3,2,1,0:T(8,128)(2,1)}, u32[]{:S(2)}, u32[]{:S(2)}) collective-permute-start(bf16[1,2,528,1024]{3,2,1,0:T(8,128)(2,1)} %get-tuple-element.36), channel_id=1, source_target_pairs={{0,16},{16,0},{32,48},{48,32},{64,80},{80,64},{96,112},{112,96},{1... | collective-permute-start | bytes 6488072 | tf_op jit(solution)/shard_map/ppermute | solution.py:141
  17.2 2.2 %copy-start = (bf16[2,2,512,1024]{3,2,1,0:T(8,128)(2,1)S(1)}, bf16[2,2,512,1024]{3,2,1,0:T(8,128)(2,1)}, u32[]{:S(2)}) copy-start(bf16[2,2,512,1024]{3,2,1,0:T(8,128)(2,1)} %xraw_ref.7) | copy-start | bytes 12582916
  19.4 7.8 %copy-start.1 = (s32[2,4,2]{1,2,0:T(2,128)S(1)}, s32[2,4,2]{1,2,0:T(2,128)}, u32[]{:S(2)}) copy-start(s32[2,4,2]{1,2,0:T(2,128)} %param.10) | copy-start | bytes 196
  19.4 8.7 %copy-start.4 = (f32[2]{0:T(128)S(1)}, f32[2]{0:T(128)}, u32[]{:S(2)}) copy-start(f32[2]{0:T(128)} %constant.77.clone) | copy-start | bytes 28
  28.2 83.0 %copy-start.3 = (f32[2]{0:T(128)}, f32[2]{0:T(128)S(1)}, u32[]{:S(2)}) copy-start(f32[2]{0:T(128)S(1)} %compare_convert_fusion.2) | copy-start | bytes 28

commit v3 on v2

--- a/solution.py
+++ b/solution.py
@@ -11,16 +11,16 @@
 MESH = pl.DeviceIdType.MESH
 
 
-def lag_kernel(sel_ref, xraw_ref, xperm_ref, yraw_ref, yperm_ref, o_ref, xs, ys):
+def lag_kernel(sel_ref, xraw_ref, xperm_ref, yre_ref, yim_ref, yperm_ref, o_ref, xs, ys):
     width = xperm_ref.shape[1]
     for blk in range(2):
-        for c in range(2):
-            rows = pl.ds(blk * width, width)
+        rows = pl.ds(blk * width, width)
+        for c, y_ref in enumerate((yre_ref, yim_ref)):
             xs[blk, c] = jnp.dot(
                 xperm_ref[blk], xraw_ref[0, c, rows, :], preferred_element_type=jnp.float32
             ).astype(xs.dtype)
             ys[blk, c] = jnp.dot(
-                yperm_ref[blk], yraw_ref[0, c, rows, :], preferred_element_type=jnp.float32
+                yperm_ref[blk], y_ref[0, 0, rows, :], preferred_element_type=jnp.float32
             ).astype(ys.dtype)
     dot = lambda u, v: lax.dot_general(u, v, NT, preferred_element_type=jnp.float32)
     for a in range(2):
@@ -38,16 +38,18 @@
                 o_ref[0, pl.ds(row, 1), :] = jnp.sum(sheared, axis=0, keepdims=True)
 
 
-def pair_lags(sel, x_raw, x_perm, y_raw, y_perm, y_by_sel):
+def pair_lags(sel, x_raw, x_perm, y_re, y_im, y_perm, y_by_sel):
     n = sel.shape[0]
     _, _, rows_x, samples = x_raw.shape
-    rows_y = y_raw.shape[2]
+    rows_y = y_re.shape[2]
     width = x_perm.shape[1]
     x_spec = pl.BlockSpec((1, 2, rows_x, samples), lambda i, s: (s[i], 0, 0, 0))
     if y_by_sel:
-        y_spec = pl.BlockSpec((1, 2, rows_y, samples), lambda i, s: (s[i], 0, 0, 0))
+        re_spec = pl.BlockSpec((1, 1, rows_y, samples), lambda i, s: (s[i], 0, 0, 0))
+        im_spec = pl.BlockSpec((1, 1, rows_y, samples), lambda i, s: (s[i], 1, 0, 0))
     else:
-        y_spec = pl.BlockSpec((1, 2, rows_y, samples), lambda i, s: (i, 0, 0, 0))
+        re_spec = pl.BlockSpec((1, 1, rows_y, samples), lambda i, s: (i, 0, 0, 0))
+        im_spec = pl.BlockSpec((1, 1, rows_y, samples), lambda i, s: (i, 0, 0, 0))
     perm_spec = pl.BlockSpec((2, width, width), lambda i, s: (0, 0, 0))
     out_spec = pl.BlockSpec((1, 8, 2 * width), lambda i, s: (i, 0, 0))
     flops = n * (16 + 8) * 2 * width * width * samples
@@ -57,7 +59,7 @@
         grid_spec=pltpu.PrefetchScalarGridSpec(
             num_scalar_prefetch=1,
             grid=(n,),
-            in_specs=[x_spec, perm_spec, y_spec, perm_spec],
+            in_specs=[x_spec, perm_spec, re_spec, im_spec, perm_spec],
             out_specs=out_spec,
             scratch_shapes=[
                 pltpu.VMEM((2, 2, width, samples), x_raw.dtype),
@@ -68,7 +70,7 @@
         cost_estimate=pl.CostEstimate(
             flops=flops, transcendentals=0, bytes_accessed=n * 2 * 4 * width * samples * 2
         ),
-    )(sel, x_raw, x_perm, y_raw, y_perm)
+    )(sel, x_raw, x_perm, y_re, y_im, y_perm)
 
 
 def scatter_kernel(dense_ref, out_ref, recv, send_sem, recv_sem):
@@ -132,14 +134,21 @@
     meta = meta.at[0, 0].set(pos_row.astype(jnp.float32)).at[0, 1].set(tg_row.astype(jnp.float32))
     meta = meta.astype(volts.dtype)
 
-    sent = []
-    for bit in range(levels):
-        mine = (me >> bit) & 1
-        pairs = [(i, i ^ (1 << bit)) for i in range(n_inp)]
-        chan = jnp.where(mine == 1, volts[0], volts[1])
-        send = jnp.concatenate([chan, meta], axis=1)[None]
-        got = lax.ppermute(send, "inp", pairs)
-        sent.append((mine, got))
+    def exchange(chan, pairs):
+        slab = jnp.concatenate([jnp.where(chan == 1, volts[1], volts[0]), meta], axis=1)
+        return [lax.ppermute(slab[None, c : c + 1], "inp", pairs) for c in range(2)]
+
+    mine = [me & 1] + [((me >> 1) ^ (me >> 2)) & 1] * min(levels - 1, 2)
+    mine += [(me >> bit) & 1 for bit in range(3, levels)]
+    got = {}
+    got[1] = exchange(1 - mine[1], [(i, i ^ 2) for i in range(n_inp)]) if levels > 1 else None
+    got[0] = exchange(1 - mine[0], [(i, i ^ 1) for i in range(n_inp)])
+    relay = [(i, i ^ 6) for i in range(n_inp)]
+    for bit in range(2, levels):
+        if bit == 2:
+            got[2] = [lax.ppermute(part, "inp", relay) for part in got[1]]
+        else:
+            got[bit] = exchange(1 - mine[bit], [(i, i ^ (1 << bit)) for i in range(n_inp)])
 
     ids = jnp.arange(width, dtype=jnp.int32)
 
@@ -153,30 +162,36 @@
 
     groups_all = RG_DEV * n_inp
     group_ids = jnp.arange(groups_all, dtype=jnp.int32)
-
-    lag0 = pair_lags(jnp.arange(channels, dtype=jnp.int32), volts, perm, volts, perm_rev, True)
+    chan_ids = jnp.arange(channels, dtype=jnp.int32)
+
+    lag0 = pair_lags(jnp.arange(channels, dtype=jnp.int32), volts, perm, volts, volts, perm_rev, True)
     lag0 = lag0.reshape(channels, 2, 2, 2, 2 * width)
     center = (jnp.arange(2 * width) == width - 1)
     same = jnp.eye(2, dtype=bool)
     lag0 = jnp.where(same[None, :, :, None, None] & center[None, None, None, None, :], 0.0, lag0)
+    contrib_w = []
+    contrib_v = []
     w0 = (tile_group[:, 0, :, None] == group_ids).astype(jnp.float32)
-    dense_rev = jnp.einsum("abg,fabcj->gfcj", w0, lag0, precision=HIGH)
-    dense_fwd = None
-    chan_ids = jnp.arange(channels, dtype=jnp.int32)
+    f0 = (chan_ids[:, None] == chan_ids[None, :]).astype(jnp.float32)
+    contrib_w.append(jnp.einsum("abg,fh->fabgh", w0, f0).reshape(-1, groups_all, channels))
+    contrib_v.append(jnp.flip(lag0[..., :diffs], axis=-1).reshape(-1, 2, diffs))
     sign = jnp.array([1.0, -1.0], jnp.float32)
     for bit in range(levels):
-        mine, got = sent[bit]
-        got_pos = got[0, 0, rows, : blocks * width].astype(jnp.int32).reshape(blocks, width)
-        got_tg = got[0, 0, rows + 1, : tg_flat.shape[0]].astype(jnp.int32).reshape(tile_group.shape)
-        lag = pair_lags(mine[None].astype(jnp.int32), volts, perm, got, one_hot(got_pos, True), False)
-        lag = lag.reshape(2, 2, 2, 2 * width)
-        fmask = (chan_ids == mine).astype(jnp.float32)
+        yre, yim = got[bit]
+        got_pos = yre[0, 0, rows, : blocks * width].astype(jnp.int32).reshape(blocks, width)
+        got_tg = yre[0, 0, rows + 1, : tg_flat.shape[0]].astype(jnp.int32).reshape(tile_group.shape)
+        lag = pair_lags(mine[bit][None].astype(jnp.int32), volts, perm, yre, yim, one_hot(got_pos, True), False)
+        lag = lag.reshape(2, 2, 2, 2 * width)[..., :diffs]
+        fmask = (chan_ids == mine[bit]).astype(jnp.float32)
         w_direct = (tile_group[:, bit + 1, :, None] == group_ids).astype(jnp.float32)
-        w_trans = (got_tg[:, bit + 1, :, None] == group_ids).astype(jnp.float32)
-        dense_rev = dense_rev + jnp.einsum("abg,f,abcj->gfcj", w_direct, fmask, lag, precision=HIGH)
-        term = jnp.einsum("bag,f,c,abcj->gfcj", w_trans, fmask, sign, lag, precision=HIGH)
-        dense_fwd = term if dense_fwd is None else dense_fwd + term
-    dense = jnp.flip(dense_rev[..., :diffs], axis=-1) + dense_fwd[..., :diffs]
+        w_trans = jnp.swapaxes((got_tg[:, bit + 1, :, None] == group_ids).astype(jnp.float32), 0, 1)
+        contrib_w.append(jnp.einsum("abg,f->abgf", w_direct, fmask).reshape(-1, groups_all, channels))
+        contrib_v.append(jnp.flip(lag, axis=-1).reshape(-1, 2, diffs))
+        contrib_w.append(jnp.einsum("abg,f->abgf", w_trans, fmask).reshape(-1, groups_all, channels))
+        contrib_v.append((lag * sign[:, None]).reshape(-1, 2, diffs))
+    dense = jnp.einsum(
+        "ngf,nck->gfck", jnp.concatenate(contrib_w), jnp.concatenate(contrib_v), precision=HIGH
+    )
     dense = dense * (1.0 / samples)
     dense = jnp.pad(dense, [(0, 0)] * 3 + [(0, 1)])
     dense = dense.reshape((n_inp, RG_DEV) + dense.shape[1:])

time: 155 us -> 120 us (0.77)
  waiting for transfers between devices: 81.8 us -> 44.2 us
  starting transfers between devices: 4.33 us -> 9.61 us
  local copies, waits for them, and re-layouts: 13.8 us -> 17 us
  other arithmetic: 15.6 us -> 12.7 us
  matrix products: 2.86 us -> 0.63 us
    ppermute x3 -> x6, waiting for transfers between devices: 81.8 us -> 44.2 us  [the longest x4 22.2 us: exchange(): return [lax.ppermute(slab[None, c:c + 1], 'inp', pairs) for c in range(2)]]
    ppermute x3 -> x6, starting transfers between devices: 4.33 us -> 9.61 us  [the longest x2 5.56 us: on_device(): got[2] = [lax.ppermute(part, 'inp', relay) for part in got[1]]]
    another operation x2 -> x8, other arithmetic: 0.01 us -> 3.33 us
    dot_general x7 -> x1, matrix products: 2.86 us -> 0.63 us  [on_device(): jnp.einsum('ngf,nck->gfck', jnp.concatenate(contrib_w), jnp.concatenate(c...]
    add x2 -> x0, other arithmetic: 2.22 us -> none  [the longest x1 2.06 us: on_device(): dense_rev + jnp.einsum('abg,f,abcj->gfcj', w_direct, fmask, lag, precisio...]
    transpose x3 -> x0, other arithmetic: 1.86 us -> none  [on_device(): jnp.einsum('abg,f,abcj->gfcj', w_direct, fmask, lag, precision=HIGH)]
    unnamed x15 -> x32, local copies, waits for them, and re-layouts: 7.67 us -> 9.29 us
    select_n x1 -> x2, other arithmetic: 4.56 us -> 4.63 us  [the longest x1 3.85 us: exchange(): jnp.where(chan == 1, volts[1], volts[0])]
  transfers between devices with their start and end apart: 3 -> 6, of which waited for: 2 -> 3; matrix products, arithmetic and copies ran while one was open for 3% -> 10% of each run, Pallas kernels for 12% -> 16%
where the time goes in v3:
time: 120 us
  waiting for transfers between devices  44.2 us (37%)
  Pallas kernels  35.5 us (30%)
  local copies, waits for them, and re-layouts  17 us (14%)
  other arithmetic  12.7 us (11%)
  starting transfers between devices  9.61 us (8%)
    pallas_call x4, Pallas kernels, pair_lags(): pl.pallas_call(lag_kernel, out_shape=jax.ShapeDtypeStruct((n, 8, 2 * widt...  24.1 us
    ppermute x4, waiting for transfers between devices, exchange(): return [lax.ppermute(slab[None, c:c + 1], 'inp', pairs) for c in range(2)]  22.2 us
    ppermute x2, waiting for transfers between devices, on_device(): got[2] = [lax.ppermute(part, 'inp', relay) for part in got[1]]  22 us
    pallas_call x1, Pallas kernels, reduce_scatter(): pl.pallas_call(scatter_kernel, out_shape=jax.ShapeDtypeStruct(slab, jnp.f...  11.4 us
    unnamed x32, local copies, waits for them, and re-layouts  9.29 us
    ppermute x2, starting transfers between devices, on_device(): got[2] = [lax.ppermute(part, 'inp', relay) for part in got[1]]  5.56 us
    ppermute x4, starting transfers between devices, exchange(): return [lax.ppermute(slab[None, c:c + 1], 'inp', pairs) for c in range(2)]  4.05 us
    select_n x1, other arithmetic, exchange(): jnp.where(chan == 1, volts[1], volts[0])  3.85 us
  transfers between devices with their start and end apart: 6, of which 3 were waited for; matrix products, arithmetic and copies ran while one was open for 10% of the time, Pallas kernels for 16%

profile of v3, /device:TPU:32, one launch (start us, length us, event | category | flops | bytes accessed | tf_op | source)
XLA Modules:
  0.0 119.9 jit_solution(1340748213890167443)
XLA Ops:
  0.0 0.6 fusion.17
  0.6 0.7 copy.40
  1.3 0.8 copy.18
  2.2 3.9 %select_bitcast_fusion = (bf16[2,512,1024]{2,1,0:T(8,128)(2,1)S(1)}, bf16[2,512,1024]{2,1,0:T(8,128)(2,1)}) fusion(pred[]{:T(512)S(6)} %eq.268, bf16[2,2,512,1024]{3,2,1,0:T(8,128)(2,1)} %xraw_ref.7, pred[]{:T(512)S(6)} %eq.255), kind=kLoop, calls=%fused_computation.3 | loop fusion | flops 2097152 | bytes 8388610 | tf_op jit(solution)/shard_map/jit(_where)/select_n | solution.py:138
  6.0 1.3 %scatter.9 = bf16[2,16,1024]{2,1,0:T(8,128)(2,1)S(1)} dynamic-update-slice(bf16[2,16,1024]{2,1,0:T(8,128)(2,1)S(1)} %scatter.6, f32[1,1,1024]{2,1,0:T(1,128)S(1)} %bitcast.83, s32[]{:T(128)} %bitcast.6, s32[]{:T(128)} %bitcast.7, s32[]{:T(128)} %constant.72.clone.1) | dynamic-update-slice | bytes 8196 | tf_op jit(solution)/shard_map/scatter | solution.py:134
  7.4 2.9 %fusion.1 = (bf16[1,1,528,1024]{3,2,1,0:T(8,128)(2,1)}, bf16[1,1,528,1024]{3,2,1,0:T(8,128)(2,1)S(1)}, bf16[1,1,528,1024]{3,2,1,0:T(8,128)(2,1)}, bf16[1,1,528,1024]{3,2,1,0:T(8,128)(2,1)}) fusion(bf16[2,16,1024]{2,1,0:T(8,128)(2,1)S(1)} %scatter.9, bf16[2,512,1024]{2,1,0:T(8,128)(2,1)S(1)} %get-tuple-element.33, bf16[2,512,1024]{2,1,0:T(8,128)(2,1)} %get-tuple-element.34), kind=kLoop, calls=%fused_computation.9 | loop fusion | flops 8110080 | bytes 8585216 | tf_op jit(solution)/shard_map/broadcast_in_dim | solution.py:139
  10.3 1.5 %collective-permute-start.1 = (bf16[1,1,528,1024]{3,2,1,0:T(8,128)(2,1)S(1)}, bf16[1,1,528,1024]{3,2,1,0:T(8,128)(2,1)S(1)}, u32[]{:S(2)}, u32[]{:S(2)}) collective-permute-start(bf16[1,1,528,1024]{3,2,1,0:T(8,128)(2,1)S(1)} %get-tuple-element.36), channel_id=1, source_target_pairs={{0,32},{16,48},{32,0},{48,16},{64,96},{80,112},{96,64},{112,80},{1... | collective-permute-start | bytes 3244040 | tf_op jit(solution)/shard_map/ppermute | solution.py:139
  11.9 0.5 collective-permute-start.4
  12.4 2.0 %collective-permute-start.3 = (bf16[1,1,528,1024]{3,2,1,0:T(8,128)(2,1)}, bf16[1,1,528,1024]{3,2,1,0:T(8,128)(2,1)}, u32[]{:S(2)}, u32[]{:S(2)}) collective-permute-start(bf16[1,1,528,1024]{3,2,1,0:T(8,128)(2,1)} %get-tuple-element.40), channel_id=1, source_target_pairs={{0,16},{16,0},{32,48},{48,32},{64,80},{80,64},{96,112},{112,96},{1... | collective-permute-start | bytes 3244040 | tf_op jit(solution)/shard_map/ppermute | solution.py:139
  14.4 0.1 fusion.6.xperm_ref
  14.5 0.2 rev.26
  14.7 0.1 fusion.7.yperm_ref
  14.9 2.2 %copy-done = bf16[2,2,512,1024]{3,2,1,0:T(8,128)(2,1)S(1)} copy-done((bf16[2,2,512,1024]{3,2,1,0:T(8,128)(2,1)S(1)}, bf16[2,2,512,1024]{3,2,1,0:T(8,128)(2,1)}, u32[]{:S(2)}) %copy-start) | copy-done | bytes 4194328
  17.1 7.8 %shard_map.46 = f32[2,8,512]{2,1,0:T(8,128)S(1)} custom-call(s32[2]{0:T(128)S(1)} %iota.49.sel_ref, bf16[2,2,512,1024]{3,2,1,0:T(8,128)(2,1)S(1)} %copy-done, bf16[2,256,256]{2,1,0:T(8,128)(2,1)S(1)} %fusion.6.xperm_ref, bf16[2,2,512,1024]{3,2,1,0:T(8,128)(2,1)S(1)} %copy-done, bf16[2,2,512,1024]{3,2,1,0:T(8,128)(2,1)S(1)} %copy-done, ...), custom_call_target="tpu_custom_call" | custom-call | flops 6442450944 | bytes 8388608 | tf_op jit(solution)/shard_map/pallas_call | solution.py:56
  24.8 0.6 reshape.199
  25.6 0.8 slice_select_fusion
  26.4 1.5 %reverse = f32[2,2,2,2,512]{4,3,2,1,0:T(2,128)} reverse(f32[2,2,2,2,512]{4,3,2,1,0:T(2,128)S(1)} %bitcast.62), dimensions={4} | reverse | bytes 65536
  27.9 0.8 slice.208
  28.8 0.5 compare_convert_fusion.7
  29.3 0.6 compare_convert_fusion.8
  29.9 1.1 slice_reduce_fusion
  31.0 0.7 compare_convert_fusion.1
  31.7 0.7 compare_convert_fusion.5
  32.4 0.7 broadcast_multiply_fusion.3
  33.0 4.0 %collective-permute-done.1.yre_ref = bf16[1,1,528,1024]{3,2,1,0:T(8,128)(2,1)S(1)} collective-permute-done((bf16[1,1,528,1024]{3,2,1,0:T(8,128)(2,1)S(1)}, bf16[1,1,528,1024]{3,2,1,0:T(8,128)(2,1)S(1)}, u32[]{:S(2)}, u32[]{:S(2)}) %collective-permute-start.1) | collective-permute-done | bytes 1081376 | tf_op jit(solution)/shard_map/ppermute | solution.py:139
  37.2 2.8 %collective-permute-start.2 = (bf16[1,1,528,1024]{3,2,1,0:T(8,128)(2,1)S(1)}, bf16[1,1,528,1024]{3,2,1,0:T(8,128)(2,1)S(1)}, u32[]{:S(2)}, u32[]{:S(2)}) collective-permute-start(bf16[1,1,528,1024]{3,2,1,0:T(8,128)(2,1)S(1)} %collective-permute-done.1.yre_ref), channel_id=1, source_target_pairs={{0,96},{16,112},{32,64},{48,80},{64,32},{80,48},{96,0},{112,16},{1... | collective-permute-start | bytes 3244040 | tf_op jit(solution)/shard_map/ppermute | solution.py:149
  40.0 0.7 copy.20
  40.7 0.2 rev.30
  40.9 0.1 fusion.9.yperm_ref
  41.0 18.2 %collective-permute-done.4.yim_ref = bf16[1,1,528,1024]{3,2,1,0:T(8,128)(2,1)} collective-permute-done((bf16[1,1,528,1024]{3,2,1,0:T(8,128)(2,1)}, bf16[1,1,528,1024]{3,2,1,0:T(8,128)(2,1)}, u32[]{:S(2)}, u32[]{:S(2)}) %collective-permute-start.4) | collective-permute-done | bytes 1081376 | tf_op jit(solution)/shard_map/ppermute | solution.py:139
  59.2 5.4 %shard_map.48 = f32[1,8,512]{2,1,0:T(8,128)S(1)} custom-call(s32[1]{0:T(128)} %bitcast.29.sel_ref, bf16[2,2,512,1024]{3,2,1,0:T(8,128)(2,1)} %xraw_ref.7, bf16[2,256,256]{2,1,0:T(8,128)(2,1)S(1)} %fusion.6.xperm_ref, bf16[1,1,528,1024]{3,2,1,0:T(8,128)(2,1)S(1)} %collective-permute-done.1.yre_ref, bf16[1,1,528,1024]{3,2,1,0:T(8,128)(2,1)} %collective-permute-done.4.yim_ref, ...), custom_call_target="tpu_custom_call" | custom-call | flops 3221225472 | bytes 4194304 | tf_op jit(solution)/shard_map/pallas_call | solution.py:56
  64.6 0.6 reshape.204
  65.2 2.8 %collective-permute-start.5 = (bf16[1,1,528,1024]{3,2,1,0:T(8,128)(2,1)}, bf16[1,1,528,1024]{3,2,1,0:T(8,128)(2,1)}, u32[]{:S(2)}, u32[]{:S(2)}) collective-permute-start(bf16[1,1,528,1024]{3,2,1,0:T(8,128)(2,1)} %collective-permute-done.4.yim_ref), channel_id=1, source_target_pairs={{0,96},{16,112},{32,64},{48,80},{64,32},{80,48},{96,0},{112,16},{1... | collective-permute-start | bytes 3244040 | tf_op jit(solution)/shard_map/ppermute | solution.py:149
  68.0 0.7 compare_convert_fusion.2
  69.0 0.2 rev.32
  69.5 22.0 %collective-permute-done.5.yim_ref = bf16[1,1,528,1024]{3,2,1,0:T(8,128)(2,1)} collective-permute-done((bf16[1,1,528,1024]{3,2,1,0:T(8,128)(2,1)}, bf16[1,1,528,1024]{3,2,1,0:T(8,128)(2,1)}, u32[]{:S(2)}, u32[]{:S(2)}) %collective-permute-start.5) | collective-permute-done | bytes 1081376 | tf_op jit(solution)/shard_map/ppermute | solution.py:149
  91.5 5.4 %shard_map.49 = f32[1,8,512]{2,1,0:T(8,128)S(1)} custom-call(s32[1]{0:T(128)} %bitcast.29.sel_ref, bf16[2,2,512,1024]{3,2,1,0:T(8,128)(2,1)} %xraw_ref.7, bf16[2,256,256]{2,1,0:T(8,128)(2,1)S(1)} %fusion.6.xperm_ref, bf16[1,1,528,1024]{3,2,1,0:T(8,128)(2,1)S(1)} %collective-permute-done.2.yre_ref, bf16[1,1,528,1024]{3,2,1,0:T(8,128)(2,1)} %collective-permute-done.5.yim_ref, ...), custom_call_target="tpu_custom_call" | custom-call | flops 3221225472 | bytes 4194304 | tf_op jit(solution)/shard_map/pallas_call | solution.py:56
  97.0 0.2 rev.28
  97.3 0.1 fusion.8.yperm_ref
  97.6 5.4 %shard_map.47 = f32[1,8,512]{2,1,0:T(8,128)S(1)} custom-call(s32[1]{0:T(128)} %bitcast.25.sel_ref, bf16[2,2,512,1024]{3,2,1,0:T(8,128)(2,1)} %xraw_ref.7, bf16[2,256,256]{2,1,0:T(8,128)(2,1)S(1)} %fusion.6.xperm_ref, bf16[1,1,528,1024]{3,2,1,0:T(8,128)(2,1)S(1)} %collective-permute-done.yre_ref, bf16[1,1,528,1024]{3,2,1,0:T(8,128)(2,1)} %collective-permute-done.3.yim_ref, ...), custom_call_target="tpu_custom_call" | custom-call | flops 3221225472 | bytes 4194304 | tf_op jit(solution)/shard_map/pallas_call | solution.py:56
  103.1 0.4 reverse.1
  103.6 0.4 reverse.2
  104.1 0.4 reverse.3
  105.0 0.6 convolution_multiply_fusion
  105.6 0.4 copy.39
  106.0 1.0 pad.21.clone
  107.0 11.4 %shard_map.50 = f32[8,2,2,512]{3,2,1,0:T(2,128)} custom-call(f32[8,8,2,2,512]{4,3,2,1,0:T(2,128)} %bitcast.60), custom_call_target="tpu_custom_call" | custom-call | tf_op jit(solution)/shard_map/pallas_call | solution.py:108
  118.4 1.5 %copy.43 = f32[8,2,2,511]{3,2,1,0:T(2,128)} copy(f32[8,2,2,511]{3,2,1,0:T(2,128)} %bitcast.61) | data formatting | bytes 130816
  (69 shorter events, 2.1 us)
Async XLA Ops:
  7.3 7.0 %copy-start.3 = (s32[2,256]{1,0:T(2,128)S(1)}, s32[2,256]{1,0:T(2,128)}, u32[]{:S(2)}) copy-start(s32[2,256]{1,0:T(2,128)} %param.9) | copy-start | bytes 6148
  10.3 26.7 %collective-permute-start.1 = (bf16[1,1,528,1024]{3,2,1,0:T(8,128)(2,1)S(1)}, bf16[1,1,528,1024]{3,2,1,0:T(8,128)(2,1)S(1)}, u32[]{:S(2)}, u32[]{:S(2)}) collective-permute-start(bf16[1,1,528,1024]{3,2,1,0:T(8,128)(2,1)S(1)} %get-tuple-element.36), channel_id=1, source_target_pairs={{0,32},{16,48},{32,0},{48,16},{64,96},{80,112},{96,64},{112,80},{1... | collective-permute-start | bytes 3244040 | tf_op jit(solution)/shard_map/ppermute | solution.py:139
  11.8 56.9 %collective-permute-start = (bf16[1,1,528,1024]{3,2,1,0:T(8,128)(2,1)}, bf16[1,1,528,1024]{3,2,1,0:T(8,128)(2,1)S(1)}, u32[]{:S(2)}, u32[]{:S(2)}) collective-permute-start(bf16[1,1,528,1024]{3,2,1,0:T(8,128)(2,1)} %get-tuple-element.39), channel_id=1, source_target_pairs={{0,16},{16,0},{32,48},{48,32},{64,80},{80,64},{96,112},{112,96},{1... | collective-permute-start | bytes 3244040 | tf_op jit(solution)/shard_map/ppermute | solution.py:139
  11.9 47.3 %collective-permute-start.4 = (bf16[1,1,528,1024]{3,2,1,0:T(8,128)(2,1)}, bf16[1,1,528,1024]{3,2,1,0:T(8,128)(2,1)}, u32[]{:S(2)}, u32[]{:S(2)}) collective-permute-start(bf16[1,1,528,1024]{3,2,1,0:T(8,128)(2,1)} %get-tuple-element.35), channel_id=1, source_target_pairs={{0,32},{16,48},{32,0},{48,16},{64,96},{80,112},{96,64},{112,80},{1... | collective-permute-start | bytes 3244040 | tf_op jit(solution)/shard_map/ppermute | solution.py:139
  12.4 85.1 %collective-permute-start.3 = (bf16[1,1,528,1024]{3,2,1,0:T(8,128)(2,1)}, bf16[1,1,528,1024]{3,2,1,0:T(8,128)(2,1)}, u32[]{:S(2)}, u32[]{:S(2)}) collective-permute-start(bf16[1,1,528,1024]{3,2,1,0:T(8,128)(2,1)} %get-tuple-element.40), channel_id=1, source_target_pairs={{0,16},{16,0},{32,48},{48,32},{64,80},{80,64},{96,112},{112,96},{1... | collective-permute-start | bytes 3244040 | tf_op jit(solution)/shard_map/ppermute | solution.py:139
  14.9 2.2 %copy-start = (bf16[2,2,512,1024]{3,2,1,0:T(8,128)(2,1)S(1)}, bf16[2,2,512,1024]{3,2,1,0:T(8,128)(2,1)}, u32[]{:S(2)}) copy-start(bf16[2,2,512,1024]{3,2,1,0:T(8,128)(2,1)} %xraw_ref.7) | copy-start | bytes 12582916
  37.2 31.6 %collective-permute-start.2 = (bf16[1,1,528,1024]{3,2,1,0:T(8,128)(2,1)S(1)}, bf16[1,1,528,1024]{3,2,1,0:T(8,128)(2,1)S(1)}, u32[]{:S(2)}, u32[]{:S(2)}) collective-permute-start(bf16[1,1,528,1024]{3,2,1,0:T(8,128)(2,1)S(1)} %collective-permute-done.1.yre_ref), channel_id=1, source_target_pairs={{0,96},{16,112},{32,64},{48,80},{64,32},{80,48},{96,0},{112,16},{1... | collective-permute-start | bytes 3244040 | tf_op jit(solution)/shard_map/ppermute | solution.py:149
  65.2 26.3 %collective-permute-start.5 = (bf16[1,1,528,1024]{3,2,1,0:T(8,128)(2,1)}, bf16[1,1,528,1024]{3,2,1,0:T(8,128)(2,1)}, u32[]{:S(2)}, u32[]{:S(2)}) collective-permute-start(bf16[1,1,528,1024]{3,2,1,0:T(8,128)(2,1)} %collective-permute-done.4.yim_ref), channel_id=1, source_target_pairs={{0,96},{16,112},{32,64},{48,80},{64,32},{80,48},{96,0},{112,16},{1... | collective-permute-start | bytes 3244040 | tf_op jit(solution)/shard_map/ppermute | solution.py:149
  97.5 5.6 %copy-start.1 = (f32[2,2,2,512]{3,2,1,0:T(2,128)S(1)}, f32[2,2,2,512]{3,2,1,0:T(2,128)}, u32[]{:S(2)}) copy-start(f32[2,2,2,512]{3,2,1,0:T(2,128)} %reshape.204) | copy-start | bytes 49156
  97.5 5.6 %copy-start.7 = (f32[2]{0:T(128)S(1)}, f32[2]{0:T(128)}, u32[]{:S(2)}) copy-start(f32[2]{0:T(128)} %constant.77.clone) | copy-start | bytes 28
  97.5 7.1 %copy-start.6 = (f32[2,2,64]{2,1,0:T(2,128)S(1)}, f32[2,2,64]{2,1,0:T(2,128)}, u32[]{:S(2)}) copy-start(f32[2,2,64]{2,1,0:T(2,128)} %get-tuple-element.63) | copy-start | bytes 3076
  97.5 7.1 %copy-start.9 = (f32[2]{0:T(128)S(1)}, f32[2]{0:T(128)}, u32[]{:S(2)}) copy-start(f32[2]{0:T(128)} %compare_convert_fusion.8) | copy-start | bytes 28
  97.5 7.2 %copy-start.4 = (f32[2,2,64]{2,1,0:T(2,128)S(1)}, f32[2,2,64]{2,1,0:T(2,128)}, u32[]{:S(2)}) copy-start(f32[2,2,64]{2,1,0:T(2,128)} %get-tuple-element.61) | copy-start | bytes 3076
  97.5 7.2 %copy-start.5 = (f32[2,2,64]{2,1,0:T(2,128)S(1)}, f32[2,2,64]{2,1,0:T(2,128)}, u32[]{:S(2)}) copy-start(f32[2,2,64]{2,1,0:T(2,128)} %get-tuple-element.62) | copy-start | bytes 3076
  97.5 7.2 %copy-start.8 = (f32[2]{0:T(128)S(1)}, f32[2]{0:T(128)}, u32[]{:S(2)}) copy-start(f32[2]{0:T(128)} %compare_convert_fusion.7) | copy-start | bytes 28
  97.6 7.2 %copy-start.2 = (f32[2,2,2,2,64]{4,3,2,0,1:T(2,128)S(1)}, f32[2,2,2,2,64]{4,3,2,0,1:T(2,128)}, u32[]{:S(2)}) copy-start(f32[2,2,2,2,64]{4,3,2,0,1:T(2,128)} %broadcast_multiply_fusion.3) | copy-start | bytes 12292

commit v4 on v3

--- a/solution.py
+++ b/solution.py
@@ -11,13 +11,13 @@
 MESH = pl.DeviceIdType.MESH
 
 
-def lag_kernel(sel_ref, xraw_ref, xperm_ref, yre_ref, yim_ref, yperm_ref, o_ref, xs, ys):
+def lags_into(x_ref, chan, xperm_ref, yre_ref, yim_ref, yperm_ref, o_ref, slot, xs, ys):
     width = xperm_ref.shape[1]
     for blk in range(2):
         rows = pl.ds(blk * width, width)
         for c, y_ref in enumerate((yre_ref, yim_ref)):
             xs[blk, c] = jnp.dot(
-                xperm_ref[blk], xraw_ref[0, c, rows, :], preferred_element_type=jnp.float32
+                xperm_ref[blk], x_ref[chan, c, rows, :], preferred_element_type=jnp.float32
             ).astype(xs.dtype)
             ys[blk, c] = jnp.dot(
                 yperm_ref[blk], y_ref[0, 0, rows, :], preferred_element_type=jnp.float32
@@ -35,7 +35,62 @@
                 padded = jnp.concatenate([part, jnp.zeros_like(part)], axis=1)
                 sheared = pltpu.roll(padded, 0, 1, stride=1, stride_axis=0)
                 row = (a * 2 + b) * 2 + c
-                o_ref[0, pl.ds(row, 1), :] = jnp.sum(sheared, axis=0, keepdims=True)
+                o_ref[slot, pl.ds(row, 1), :] = jnp.sum(sheared, axis=0, keepdims=True)
+
+
+def lag_kernel(sel_ref, xraw_ref, xperm_ref, yre_ref, yim_ref, yperm_ref, o_ref, xs, ys):
+    lags_into(xraw_ref, 0, xperm_ref, yre_ref, yim_ref, yperm_ref, o_ref, 0, xs, ys)
+
+
+def relay_kernel(x_ref, xperm_ref, yre_ref, yim_ref, yperm_ref, z_ref, zperm_ref,
+                 o_ref, relay_ref, xs, ys, send_sem, recv_sem):
+    me = lax.axis_index("inp")
+    fq = lax.axis_index("freq")
+    onward = lax.bitwise_xor(me, 6)
+    barrier = pltpu.get_barrier_semaphore()
+    pl.semaphore_signal(barrier, inc=1, device_id=(onward, fq), device_id_type=MESH)
+    pl.semaphore_wait(barrier, 1)
+    copy = pltpu.make_async_remote_copy(
+        src_ref=yim_ref,
+        dst_ref=relay_ref,
+        send_sem=send_sem,
+        recv_sem=recv_sem,
+        device_id=(onward, fq),
+        device_id_type=MESH,
+    )
+    copy.start()
+    parity = lax.bitwise_and(lax.bitwise_xor(lax.shift_right_logical(me, 1), lax.shift_right_logical(me, 2)), 1)
+    lags_into(x_ref, parity, xperm_ref, yre_ref, yim_ref, yperm_ref, o_ref, 0, xs, ys)
+    lags_into(x_ref, lax.bitwise_and(me, 1), xperm_ref, z_ref.at[:, 0:1], z_ref.at[:, 1:2], zperm_ref, o_ref, 1, xs, ys)
+    copy.wait()
+
+
+def relay_lags(x_all, x_perm, y_re, y_im, y_perm, z_all, z_perm):
+    width = x_perm.shape[1]
+    samples = x_all.shape[-1]
+    vmem = pl.BlockSpec(memory_space=pltpu.VMEM)
+    return pl.pallas_call(
+        relay_kernel,
+        out_shape=(
+            jax.ShapeDtypeStruct((2, 8, 2 * width), jnp.float32),
+            jax.ShapeDtypeStruct(y_im.shape, y_im.dtype),
+        ),
+        in_specs=[vmem] * 7,
+        out_specs=(vmem, vmem),
+        scratch_shapes=[
+            pltpu.VMEM((2, 2, width, samples), x_all.dtype),
+            pltpu.VMEM((2, 2, width, samples), x_all.dtype),
+            pltpu.SemaphoreType.DMA(()),
+            pltpu.SemaphoreType.DMA(()),
+        ],
+        compiler_params=pltpu.CompilerParams(
+            collective_id=1, has_side_effects=True, vmem_limit_bytes=48 * 1024 * 1024
+        ),
+        cost_estimate=pl.CostEstimate(
+            flops=2 * 4 * 24 * 2 * width * width * samples, transcendentals=0,
+            bytes_accessed=4 * 2 * 4 * width * samples * 2,
+        ),
+    )(x_all, x_perm, y_re, y_im, y_perm, z_all, z_perm)
 
 
 def pair_lags(sel, x_raw, x_perm, y_re, y_im, y_perm, y_by_sel):
@@ -130,25 +185,25 @@
     pos_row = jnp.pad(position_input.reshape(-1), (0, samples - blocks * width))
     tg_flat = tile_group.reshape(-1)
     tg_row = jnp.pad(tg_flat, (0, samples - tg_flat.shape[0]))
-    meta = jnp.zeros((2, 16, samples), jnp.float32)
-    meta = meta.at[0, 0].set(pos_row.astype(jnp.float32)).at[0, 1].set(tg_row.astype(jnp.float32))
-    meta = meta.astype(volts.dtype)
-
-    def exchange(chan, pairs):
+    meta = jnp.stack([pos_row, tg_row]).astype(jnp.float32).astype(volts.dtype)
+    meta = jnp.pad(meta[None], [(0, 1), (0, 14), (0, 0)])
+
+    def exchange(chan, pairs, parts):
         slab = jnp.concatenate([jnp.where(chan == 1, volts[1], volts[0]), meta], axis=1)
+        if parts == 1:
+            got_slab = lax.ppermute(slab[None], "inp", pairs)
+            return [got_slab[:, c : c + 1] for c in range(2)]
         return [lax.ppermute(slab[None, c : c + 1], "inp", pairs) for c in range(2)]
 
     mine = [me & 1] + [((me >> 1) ^ (me >> 2)) & 1] * min(levels - 1, 2)
     mine += [(me >> bit) & 1 for bit in range(3, levels)]
-    got = {}
-    got[1] = exchange(1 - mine[1], [(i, i ^ 2) for i in range(n_inp)]) if levels > 1 else None
-    got[0] = exchange(1 - mine[0], [(i, i ^ 1) for i in range(n_inp)])
-    relay = [(i, i ^ 6) for i in range(n_inp)]
-    for bit in range(2, levels):
-        if bit == 2:
-            got[2] = [lax.ppermute(part, "inp", relay) for part in got[1]]
-        else:
-            got[bit] = exchange(1 - mine[bit], [(i, i ^ (1 << bit)) for i in range(n_inp)])
+    got1 = exchange(1 - mine[1], [(i, i ^ 2) for i in range(n_inp)], 2)
+    got0 = lax.ppermute(
+        jnp.concatenate([jnp.where(mine[0] == 0, volts[1], volts[0]), meta], axis=1)[None],
+        "inp",
+        [(i, i ^ 1) for i in range(n_inp)],
+    )
+    relay_re = lax.ppermute(got1[0], "inp", [(i, i ^ 6) for i in range(n_inp)])
 
     ids = jnp.arange(width, dtype=jnp.int32)
 
@@ -176,11 +231,20 @@
     contrib_w.append(jnp.einsum("abg,fh->fabgh", w0, f0).reshape(-1, groups_all, channels))
     contrib_v.append(jnp.flip(lag0[..., :diffs], axis=-1).reshape(-1, 2, diffs))
     sign = jnp.array([1.0, -1.0], jnp.float32)
+
+    def meta_of(slab):
+        got_pos = slab[0, 0, rows, : blocks * width].astype(jnp.int32).reshape(blocks, width)
+        got_tg = slab[0, 0, rows + 1, : tg_flat.shape[0]].astype(jnp.int32).reshape(tile_group.shape)
+        return one_hot(got_pos, True), got_tg
+
+    perm1, tg1 = meta_of(got1[0])
+    perm0, tg0 = meta_of(got0)
+    lag10, relay_im = relay_lags(volts, perm, got1[0], got1[1], perm1, got0, perm0)
+    perm2, tg2 = meta_of(relay_re)
+    lag2 = pair_lags(mine[2][None].astype(jnp.int32), volts, perm, relay_re, relay_im, perm2, False)
+    level_lags = {0: (lag10[1], tg0), 1: (lag10[0], tg1), 2: (lag2[0], tg2)}
     for bit in range(levels):
-        yre, yim = got[bit]
-        got_pos = yre[0, 0, rows, : blocks * width].astype(jnp.int32).reshape(blocks, width)
-        got_tg = yre[0, 0, rows + 1, : tg_flat.shape[0]].astype(jnp.int32).reshape(tile_group.shape)
-        lag = pair_lags(mine[bit][None].astype(jnp.int32), volts, perm, yre, yim, one_hot(got_pos, True), False)
+        lag, got_tg = level_lags[bit]
         lag = lag.reshape(2, 2, 2, 2 * width)[..., :diffs]
         fmask = (chan_ids == mine[bit]).astype(jnp.float32)
         w_direct = (tile_group[:, bit + 1, :, None] == group_ids).astype(jnp.float32)

time: 120 us -> 111 us (0.925)
  Pallas kernels: 35.5 us -> 51.5 us
  waiting for transfers between devices: 44.2 us -> 34.3 us
  other arithmetic: 12.7 us -> 6.6 us
  starting transfers between devices: 9.61 us -> 4.84 us
  local copies, waits for them, and re-layouts: 17 us -> 12.4 us
    pallas_call x0 -> x1, Pallas kernels: none -> 27.6 us  [relay_lags(): pl.pallas_call(relay_kernel, out_shape=(jax.ShapeDtypeStruct((2, 8, 2 * w...]
    pallas_call x4 -> x2, Pallas kernels: 24.1 us -> 12.9 us  [pair_lags(): pl.pallas_call(lag_kernel, out_shape=jax.ShapeDtypeStruct((n, 8, 2 * widt...]
    ppermute x4 -> x2, waiting for transfers between devices: 22.2 us -> 13 us  [exchange(): return [lax.ppermute(slab[None, c:c + 1], 'inp', pairs) for c in range(2)]]
    another operation x8, other arithmetic: 3.33 us -> 0.37 us
    ppermute x2, starting transfers between devices: 5.56 us -> 2.9 us  [the longest x1 2.79 us: on_device(): relay_re = lax.ppermute(got1[0], 'inp', [(i, i ^ 6) for i in range(n_inp)])]
    ppermute x4 -> x2, starting transfers between devices: 4.05 us -> 1.94 us  [exchange(): return [lax.ppermute(slab[None, c:c + 1], 'inp', pairs) for c in range(2)]]
    unnamed x32 -> x20, local copies, waits for them, and re-layouts: 9.29 us -> 7.44 us
    select_n x1, other arithmetic: 3.85 us -> 2.5 us  [on_device(): jnp.where(mine[0] == 0, volts[1], volts[0])]
  transfers between devices with their start and end apart: 6 -> 4, of which waited for: 3 -> 2; matrix products, arithmetic and copies ran while one was open for 10% -> 5% of each run, Pallas kernels for 16% -> 7%
where the time goes in v4:
time: 111 us
  Pallas kernels  51.5 us (46%)
  waiting for transfers between devices  34.3 us (31%)
  local copies, waits for them, and re-layouts  12.4 us (11%)
  other arithmetic  6.6 us (6%)
  starting transfers between devices  4.84 us (4%)
    pallas_call x1, Pallas kernels, relay_lags(): pl.pallas_call(relay_kernel, out_shape=(jax.ShapeDtypeStruct((2, 8, 2 * w...  27.6 us
    ppermute x1, waiting for transfers between devices, on_device(): relay_re = lax.ppermute(got1[0], 'inp', [(i, i ^ 6) for i in range(n_inp)])  21.4 us
    ppermute x2, waiting for transfers between devices, exchange(): return [lax.ppermute(slab[None, c:c + 1], 'inp', pairs) for c in range(2)]  13 us
    pallas_call x2, Pallas kernels, pair_lags(): pl.pallas_call(lag_kernel, out_shape=jax.ShapeDtypeStruct((n, 8, 2 * widt...  12.9 us
    pallas_call x1, Pallas kernels, reduce_scatter(): pl.pallas_call(scatter_kernel, out_shape=jax.ShapeDtypeStruct(slab, jnp.f...  11 us
    unnamed x20, local copies, waits for them, and re-layouts  7.44 us
    ppermute x1, starting transfers between devices, on_device(): relay_re = lax.ppermute(got1[0], 'inp', [(i, i ^ 6) for i in range(n_inp)])  2.79 us
    select_n x1, other arithmetic, on_device(): jnp.where(mine[0] == 0, volts[1], volts[0])  2.5 us
  transfers between devices with their start and end apart: 4, of which 2 were waited for; matrix products, arithmetic and copies ran while one was open for 5% of the time, Pallas kernels for 7%

profile of v4, /device:TPU:32, one launch (start us, length us, event | category | flops | bytes accessed | tf_op | source)
XLA Modules:
  0.0 110.6 jit_solution(4055469800398635440)
XLA Ops:
  0.0 0.8 copy.18
  0.8 0.1 reshape.149
  0.9 0.7 copy.40
  1.6 2.5 %select_bitcast_fusion.1 = (bf16[2,512,1024]{2,1,0:T(8,128)(2,1)S(1)}, bf16[2,512,1024]{2,1,0:T(8,128)(2,1)S(1)}) fusion(pred[]{:T(512)S(6)} %eq.255, bf16[2,2,512,1024]{3,2,1,0:T(8,128)(2,1)} %xraw_ref.3, pred[]{:T(512)S(6)} %eq.268), kind=kLoop, calls=%fused_computation.6 | loop fusion | flops 2097152 | bytes 8388610 | tf_op jit(solution)/shard_map/jit(_where)/select_n | solution.py:202
  4.1 1.8 %fusion.3 = (bf16[1,2,528,1024]{3,2,1,0:T(8,128)(2,1)}, bf16[2,528,1024]{2,1,0:T(8,128)(2,1)S(1)}) fusion(bf16[1,2,1024]{2,1,0:T(2,128)(2,1)S(1)} %fusion.11, bf16[2,512,1024]{2,1,0:T(8,128)(2,1)S(1)} %get-tuple-element.13, bf16[2,512,1024]{2,1,0:T(8,128)(2,1)S(1)} %get-tuple-element.14), kind=kLoop, calls=%fused_computation.4 | loop fusion | flops 9732096 | bytes 8523776 | tf_op jit(solution)/shard_map/broadcast_in_dim | solution.py:202
  5.9 1.1 %slice_bitcast_fusion = (bf16[1,1,528,1024]{3,2,1,0:T(8,128)(2,1)}, bf16[1,1,528,1024]{3,2,1,0:T(8,128)(2,1)S(1)}) fusion(bf16[2,528,1024]{2,1,0:T(8,128)(2,1)S(1)} %get-tuple-element.26), kind=kLoop, calls=%fused_computation.8 | loop fusion | bytes 4325376 | tf_op jit(solution)/shard_map/broadcast_in_dim | solution.py:196
  7.1 1.5 %collective-permute-start.1 = (bf16[1,1,528,1024]{3,2,1,0:T(8,128)(2,1)S(1)}, bf16[1,1,528,1024]{3,2,1,0:T(8,128)(2,1)S(1)}, u32[]{:S(2)}, u32[]{:S(2)}) collective-permute-start(bf16[1,1,528,1024]{3,2,1,0:T(8,128)(2,1)S(1)} %get-tuple-element.16), channel_id=1, source_target_pairs={{0,32},{16,48},{32,0},{48,16},{64,96},{80,112},{96,64},{112,80},{1... | collective-permute-start | bytes 3244040 | tf_op jit(solution)/shard_map/ppermute | solution.py:196
  8.6 0.1 collective-permute-start
  8.7 0.5 collective-permute-start.3
  9.1 0.1 fusion.4.xperm_ref
  9.3 0.2 rev.26
  9.5 0.1 fusion.5.yperm_ref
  9.6 2.2 %copy-done = bf16[2,2,512,1024]{3,2,1,0:T(8,128)(2,1)S(1)} copy-done((bf16[2,2,512,1024]{3,2,1,0:T(8,128)(2,1)S(1)}, bf16[2,2,512,1024]{3,2,1,0:T(8,128)(2,1)}, u32[]{:S(2)}) %copy-start) | copy-done | bytes 4194328
  11.8 7.7 %shard_map.46 = f32[2,8,512]{2,1,0:T(8,128)S(1)} custom-call(s32[2]{0:T(128)S(1)} %iota.43.sel_ref, bf16[2,2,512,1024]{3,2,1,0:T(8,128)(2,1)S(1)} %copy-done, bf16[2,256,256]{2,1,0:T(8,128)(2,1)S(1)} %fusion.4.xperm_ref, bf16[2,2,512,1024]{3,2,1,0:T(8,128)(2,1)S(1)} %copy-done, bf16[2,2,512,1024]{3,2,1,0:T(8,128)(2,1)S(1)} %copy-done, ...), custom_call_target="tpu_custom_call" | custom-call | flops 6442450944 | bytes 8388608 | tf_op jit(solution)/shard_map/pallas_call | solution.py:111
  19.6 0.1 copy.22
  19.7 0.1 broadcast_and_fusion
  19.8 0.4 reverse
  20.3 0.1 slice.146
  20.4 0.3 slice_reduce_fusion
  20.9 12.9 %collective-permute-done.1.yre_ref = bf16[1,1,528,1024]{3,2,1,0:T(8,128)(2,1)S(1)} collective-permute-done((bf16[1,1,528,1024]{3,2,1,0:T(8,128)(2,1)S(1)}, bf16[1,1,528,1024]{3,2,1,0:T(8,128)(2,1)S(1)}, u32[]{:S(2)}, u32[]{:S(2)}) %collective-permute-start.1) | collective-permute-done | bytes 1081376 | tf_op jit(solution)/shard_map/ppermute | solution.py:196
  33.8 2.8 %collective-permute-start.2 = (bf16[1,1,528,1024]{3,2,1,0:T(8,128)(2,1)S(1)}, bf16[1,1,528,1024]{3,2,1,0:T(8,128)(2,1)S(1)}, u32[]{:S(2)}, u32[]{:S(2)}) collective-permute-start(bf16[1,1,528,1024]{3,2,1,0:T(8,128)(2,1)S(1)} %collective-permute-done.1.yre_ref), channel_id=1, source_target_pairs={{0,96},{16,112},{32,64},{48,80},{64,32},{80,48},{96,0},{112,16},{1... | collective-permute-start | bytes 3244040 | tf_op jit(solution)/shard_map/ppermute | solution.py:206
  36.7 0.1 convert_element_type.89
  36.8 0.1 copy.20
  36.9 0.2 rev.28
  37.2 0.1 fusion.6.yperm_ref
  37.4 21.4 %collective-permute-done.2.yre_ref = bf16[1,1,528,1024]{3,2,1,0:T(8,128)(2,1)S(1)} collective-permute-done((bf16[1,1,528,1024]{3,2,1,0:T(8,128)(2,1)S(1)}, bf16[1,1,528,1024]{3,2,1,0:T(8,128)(2,1)S(1)}, u32[]{:S(2)}, u32[]{:S(2)}) %collective-permute-start.2) | collective-permute-done | bytes 1081376 | tf_op jit(solution)/shard_map/ppermute | solution.py:206
  58.7 0.7 slice_reduce_fusion.4
  59.4 0.1 convert_element_type.90
  59.5 0.1 convert_element_type.88
  59.6 0.1 copy.21
  59.7 0.1 copy.19
  59.8 0.7 fusion.12
  60.6 0.2 rev.29
  60.8 0.2 rev.32
  61.1 0.1 fusion.7.zperm_ref
  61.2 0.1 fusion.8.yperm_ref
  61.4 27.6 %shard_map.47 = (f32[2,8,512]{2,1,0:T(8,128)S(1)}, bf16[1,1,528,1024]{3,2,1,0:T(8,128)(2,1)S(1)}) custom-call(bf16[2,2,512,1024]{3,2,1,0:T(8,128)(2,1)} %xraw_ref.3, bf16[2,256,256]{2,1,0:T(8,128)(2,1)S(1)} %fusion.4.xperm_ref, bf16[1,1,528,1024]{3,2,1,0:T(8,128)(2,1)S(1)} %collective-permute-done.1.yre_ref, ...), custom_call_target="tpu_custom_call" | custom-call | flops 25769803776 | bytes 16777216 | tf_op jit(solution)/shard_map/pallas_call | solution.py:72
  89.0 5.2 %shard_map.48 = f32[1,8,512]{2,1,0:T(8,128)S(1)} custom-call(s32[1]{0:T(128)} %bitcast.28.sel_ref, bf16[2,2,512,1024]{3,2,1,0:T(8,128)(2,1)} %xraw_ref.3, bf16[2,256,256]{2,1,0:T(8,128)(2,1)S(1)} %fusion.4.xperm_ref, bf16[1,1,528,1024]{3,2,1,0:T(8,128)(2,1)S(1)} %collective-permute-done.2.yre_ref, bf16[1,1,528,1024]{3,2,1,0:T(8,128)(2,1)S(1)} %get-tuple-element.8.yim_ref, ...), custom_call_target="tpu_custom_call" | custom-call | flops 3221225472 | bytes 4194304 | tf_op jit(solution)/shard_map/pallas_call | solution.py:111
  94.2 0.1 broadcast_multiply_fusion
  94.3 0.4 reverse.1
  94.8 0.4 reverse.2
  95.3 0.4 reverse.3
  96.0 0.1 concatenate.22
  96.1 0.6 convolution_multiply_fusion
  96.7 0.4 copy.39
  97.1 1.0 pad.19.clone
  98.1 11.0 %shard_map.49 = f32[8,2,2,512]{3,2,1,0:T(2,128)} custom-call(f32[8,8,2,2,512]{4,3,2,1,0:T(2,128)} %bitcast.55), custom_call_target="tpu_custom_call" | custom-call | tf_op jit(solution)/shard_map/pallas_call | solution.py:163
  109.1 1.5 %copy.42 = f32[8,2,2,511]{3,2,1,0:T(2,128)} copy(f32[8,2,2,511]{3,2,1,0:T(2,128)} %bitcast.56) | data formatting | bytes 130816
  (51 shorter events, 1.2 us)
Async XLA Ops:
  5.9 3.2 %copy-start.2 = (s32[2,256]{1,0:T(2,128)S(1)}, s32[2,256]{1,0:T(2,128)}, u32[]{:S(2)}) copy-start(s32[2,256]{1,0:T(2,128)} %param.5) | copy-start | bytes 6148
  7.1 26.7 %collective-permute-start.1 = (bf16[1,1,528,1024]{3,2,1,0:T(8,128)(2,1)S(1)}, bf16[1,1,528,1024]{3,2,1,0:T(8,128)(2,1)S(1)}, u32[]{:S(2)}, u32[]{:S(2)}) collective-permute-start(bf16[1,1,528,1024]{3,2,1,0:T(8,128)(2,1)S(1)} %get-tuple-element.16), channel_id=1, source_target_pairs={{0,32},{16,48},{32,0},{48,16},{64,96},{80,112},{96,64},{112,80},{1... | collective-permute-start | bytes 3244040 | tf_op jit(solution)/shard_map/ppermute | solution.py:196
  8.6 50.2 %collective-permute-start = (bf16[1,2,528,1024]{3,2,1,0:T(8,128)(2,1)}, bf16[1,2,528,1024]{3,2,1,0:T(8,128)(2,1)}, u32[]{:S(2)}, u32[]{:S(2)}) collective-permute-start(bf16[1,2,528,1024]{3,2,1,0:T(8,128)(2,1)} %get-tuple-element.25), channel_id=1, source_target_pairs={{0,16},{16,0},{32,48},{48,32},{64,80},{80,64},{96,112},{112,96},{1... | collective-permute-start | bytes 6488072 | tf_op jit(solution)/shard_map/ppermute | solution.py:201
  8.7 52.7 %collective-permute-start.3 = (bf16[1,1,528,1024]{3,2,1,0:T(8,128)(2,1)}, bf16[1,1,528,1024]{3,2,1,0:T(8,128)(2,1)}, u32[]{:S(2)}, u32[]{:S(2)}) collective-permute-start(bf16[1,1,528,1024]{3,2,1,0:T(8,128)(2,1)} %get-tuple-element.15), channel_id=1, source_target_pairs={{0,32},{16,48},{32,0},{48,16},{64,96},{80,112},{96,64},{112,80},{1... | collective-permute-start | bytes 3244040 | tf_op jit(solution)/shard_map/ppermute | solution.py:196
  9.6 2.2 %copy-start = (bf16[2,2,512,1024]{3,2,1,0:T(8,128)(2,1)S(1)}, bf16[2,2,512,1024]{3,2,1,0:T(8,128)(2,1)}, u32[]{:S(2)}) copy-start(bf16[2,2,512,1024]{3,2,1,0:T(8,128)(2,1)} %xraw_ref.3) | copy-start | bytes 12582916
  11.8 8.6 %copy-start.1 = (s32[2,4,2]{1,2,0:T(2,128)S(1)}, s32[2,4,2]{1,2,0:T(2,128)}, u32[]{:S(2)}) copy-start(s32[2,4,2]{1,2,0:T(2,128)} %param.6) | copy-start | bytes 196
  33.8 24.9 %collective-permute-start.2 = (bf16[1,1,528,1024]{3,2,1,0:T(8,128)(2,1)S(1)}, bf16[1,1,528,1024]{3,2,1,0:T(8,128)(2,1)S(1)}, u32[]{:S(2)}, u32[]{:S(2)}) collective-permute-start(bf16[1,1,528,1024]{3,2,1,0:T(8,128)(2,1)S(1)} %collective-permute-done.1.yre_ref), channel_id=1, source_target_pairs={{0,96},{16,112},{32,64},{48,80},{64,32},{80,48},{96,0},{112,16},{1... | collective-permute-start | bytes 3244040 | tf_op jit(solution)/shard_map/ppermute | solution.py:206
  88.9 5.3 %copy-start.3 = (f32[2]{0:T(128)S(1)}, f32[2]{0:T(128)}, u32[]{:S(2)}) copy-start(f32[2]{0:T(128)} %constant.23.clone) | copy-start | bytes 28

commit v5 on v4

--- a/solution.py
+++ b/solution.py
@@ -11,17 +11,11 @@
 MESH = pl.DeviceIdType.MESH
 
 
-def lags_into(x_ref, chan, xperm_ref, yre_ref, yim_ref, yperm_ref, o_ref, slot, xs, ys):
-    width = xperm_ref.shape[1]
+def lags_into(get_x, get_y, xperm_ref, yperm_ref, o_ref, slot, xs, ys):
     for blk in range(2):
-        rows = pl.ds(blk * width, width)
-        for c, y_ref in enumerate((yre_ref, yim_ref)):
-            xs[blk, c] = jnp.dot(
-                xperm_ref[blk], x_ref[chan, c, rows, :], preferred_element_type=jnp.float32
-            ).astype(xs.dtype)
-            ys[blk, c] = jnp.dot(
-                yperm_ref[blk], y_ref[0, 0, rows, :], preferred_element_type=jnp.float32
-            ).astype(ys.dtype)
+        for c in range(2):
+            xs[blk, c] = jnp.dot(xperm_ref[blk], get_x(blk, c), preferred_element_type=jnp.float32).astype(xs.dtype)
+            ys[blk, c] = jnp.dot(yperm_ref[blk], get_y(blk, c), preferred_element_type=jnp.float32).astype(ys.dtype)
     dot = lambda u, v: lax.dot_general(u, v, NT, preferred_element_type=jnp.float32)
     for a in range(2):
         xre = xs[a, 0]
@@ -38,12 +32,23 @@
                 o_ref[slot, pl.ds(row, 1), :] = jnp.sum(sheared, axis=0, keepdims=True)
 
 
-def lag_kernel(sel_ref, xraw_ref, xperm_ref, yre_ref, yim_ref, yperm_ref, o_ref, xs, ys):
-    lags_into(xraw_ref, 0, xperm_ref, yre_ref, yim_ref, yperm_ref, o_ref, 0, xs, ys)
-
-
-def relay_kernel(x_ref, xperm_ref, yre_ref, yim_ref, yperm_ref, z_ref, zperm_ref,
+def block_rows(ref, chan, c, blk, width):
+    return ref[chan, c, pl.ds(blk * width, width), :]
+
+
+def lag_kernel(sel_ref, xraw_ref, xperm_ref, y00, y01, y10, y11, yperm_ref, o_ref, xs, ys):
+    width = xperm_ref.shape[1]
+    ys_in = ((y00, y01), (y10, y11))
+    lags_into(
+        lambda a, c: block_rows(xraw_ref, 0, c, a, width),
+        lambda b, c: ys_in[b][c][0, 0, pl.ds(0, width), :],
+        xperm_ref, yperm_ref, o_ref, 0, xs, ys,
+    )
+
+
+def relay_kernel(x_ref, xperm_ref, y00, y01, y10, y11, yperm_ref, z_ref, zperm_ref,
                  o_ref, relay_ref, xs, ys, send_sem, recv_sem):
+    width = xperm_ref.shape[1]
     me = lax.axis_index("inp")
     fq = lax.axis_index("freq")
     onward = lax.bitwise_xor(me, 6)
@@ -51,7 +56,7 @@
     pl.semaphore_signal(barrier, inc=1, device_id=(onward, fq), device_id_type=MESH)
     pl.semaphore_wait(barrier, 1)
     copy = pltpu.make_async_remote_copy(
-        src_ref=yim_ref,
+        src_ref=y11,
         dst_ref=relay_ref,
         send_sem=send_sem,
         recv_sem=recv_sem,
@@ -60,12 +65,21 @@
     )
     copy.start()
     parity = lax.bitwise_and(lax.bitwise_xor(lax.shift_right_logical(me, 1), lax.shift_right_logical(me, 2)), 1)
-    lags_into(x_ref, parity, xperm_ref, yre_ref, yim_ref, yperm_ref, o_ref, 0, xs, ys)
-    lags_into(x_ref, lax.bitwise_and(me, 1), xperm_ref, z_ref.at[:, 0:1], z_ref.at[:, 1:2], zperm_ref, o_ref, 1, xs, ys)
+    ys_in = ((y00, y01), (y10, y11))
+    lags_into(
+        lambda a, c: block_rows(x_ref, parity, c, a, width),
+        lambda b, c: ys_in[b][c][0, 0, pl.ds(0, width), :],
+        xperm_ref, yperm_ref, o_ref, 0, xs, ys,
+    )
+    lags_into(
+        lambda a, c: block_rows(x_ref, lax.bitwise_and(me, 1), c, a, width),
+        lambda b, c: block_rows(z_ref, 0, c, b, width),
+        xperm_ref, zperm_ref, o_ref, 1, xs, ys,
+    )
     copy.wait()
 
 
-def relay_lags(x_all, x_perm, y_re, y_im, y_perm, z_all, z_perm):
+def relay_lags(x_all, x_perm, y_parts, y_perm, z_all, z_perm):
     width = x_perm.shape[1]
     samples = x_all.shape[-1]
     vmem = pl.BlockSpec(memory_space=pltpu.VMEM)
@@ -73,9 +87,9 @@
         relay_kernel,
         out_shape=(
             jax.ShapeDtypeStruct((2, 8, 2 * width), jnp.float32),
-            jax.ShapeDtypeStruct(y_im.shape, y_im.dtype),
-        ),
-        in_specs=[vmem] * 7,
+            jax.ShapeDtypeStruct(y_parts[3].shape, y_parts[3].dtype),
+        ),
+        in_specs=[vmem] * 9,
         out_specs=(vmem, vmem),
         scratch_shapes=[
             pltpu.VMEM((2, 2, width, samples), x_all.dtype),
@@ -90,21 +104,25 @@
             flops=2 * 4 * 24 * 2 * width * width * samples, transcendentals=0,
             bytes_accessed=4 * 2 * 4 * width * samples * 2,
         ),
-    )(x_all, x_perm, y_re, y_im, y_perm, z_all, z_perm)
-
-
-def pair_lags(sel, x_raw, x_perm, y_re, y_im, y_perm, y_by_sel):
+    )(x_all, x_perm, *y_parts, y_perm, z_all, z_perm)
+
+
+def pair_lags(sel, x_raw, x_perm, y_parts, y_perm, y_by_sel):
     n = sel.shape[0]
     _, _, rows_x, samples = x_raw.shape
-    rows_y = y_re.shape[2]
     width = x_perm.shape[1]
     x_spec = pl.BlockSpec((1, 2, rows_x, samples), lambda i, s: (s[i], 0, 0, 0))
     if y_by_sel:
-        re_spec = pl.BlockSpec((1, 1, rows_y, samples), lambda i, s: (s[i], 0, 0, 0))
-        im_spec = pl.BlockSpec((1, 1, rows_y, samples), lambda i, s: (s[i], 1, 0, 0))
+        y_specs = [
+            pl.BlockSpec((1, 1, width, samples), lambda i, s, b=b, c=c: (s[i], c, b, 0))
+            for b in range(2) for c in range(2)
+        ]
+        y_args = [y_parts] * 4
     else:
-        re_spec = pl.BlockSpec((1, 1, rows_y, samples), lambda i, s: (i, 0, 0, 0))
-        im_spec = pl.BlockSpec((1, 1, rows_y, samples), lambda i, s: (i, 0, 0, 0))
+        y_specs = [
+            pl.BlockSpec((1, 1) + part.shape[2:], lambda i, s: (0, 0, 0, 0)) for part in y_parts
+        ]
+        y_args = list(y_parts)
     perm_spec = pl.BlockSpec((2, width, width), lambda i, s: (0, 0, 0))
     out_spec = pl.BlockSpec((1, 8, 2 * width), lambda i, s: (i, 0, 0))
     flops = n * (16 + 8) * 2 * width * width * samples
@@ -114,7 +132,7 @@
         grid_spec=pltpu.PrefetchScalarGridSpec(
             num_scalar_prefetch=1,
             grid=(n,),
-            in_specs=[x_spec, perm_spec, re_spec, im_spec, perm_spec],
+            in_specs=[x_spec, perm_spec] + y_specs + [perm_spec],
             out_specs=out_spec,
             scratch_shapes=[
                 pltpu.VMEM((2, 2, width, samples), x_raw.dtype),
@@ -125,7 +143,7 @@
         cost_estimate=pl.CostEstimate(
             flops=flops, transcendentals=0, bytes_accessed=n * 2 * 4 * width * samples * 2
         ),
-    )(sel, x_raw, x_perm, y_re, y_im, y_perm)
+    )(sel, x_raw, x_perm, *y_args, y_perm)
 
 
 def scatter_kernel(dense_ref, out_ref, recv, send_sem, recv_sem):
@@ -188,22 +206,22 @@
     meta = jnp.stack([pos_row, tg_row]).astype(jnp.float32).astype(volts.dtype)
     meta = jnp.pad(meta[None], [(0, 1), (0, 14), (0, 0)])
 
-    def exchange(chan, pairs, parts):
-        slab = jnp.concatenate([jnp.where(chan == 1, volts[1], volts[0]), meta], axis=1)
-        if parts == 1:
-            got_slab = lax.ppermute(slab[None], "inp", pairs)
-            return [got_slab[:, c : c + 1] for c in range(2)]
-        return [lax.ppermute(slab[None, c : c + 1], "inp", pairs) for c in range(2)]
+    def chunks(chan):
+        pick = lambda c, blk: jnp.where(chan == 1, volts[1, c, blk * width:(blk + 1) * width],
+                                        volts[0, c, blk * width:(blk + 1) * width])
+        parts = [pick(c, blk) for blk in range(2) for c in range(2)]
+        parts[0] = jnp.concatenate([parts[0], meta[0]], axis=0)
+        return [part[None, None] for part in parts]
 
     mine = [me & 1] + [((me >> 1) ^ (me >> 2)) & 1] * min(levels - 1, 2)
     mine += [(me >> bit) & 1 for bit in range(3, levels)]
-    got1 = exchange(1 - mine[1], [(i, i ^ 2) for i in range(n_inp)], 2)
+    got1 = [lax.ppermute(part, "inp", [(i, i ^ 2) for i in range(n_inp)]) for part in chunks(1 - mine[1])]
     got0 = lax.ppermute(
         jnp.concatenate([jnp.where(mine[0] == 0, volts[1], volts[0]), meta], axis=1)[None],
         "inp",
         [(i, i ^ 1) for i in range(n_inp)],
     )
-    relay_re = lax.ppermute(got1[0], "inp", [(i, i ^ 6) for i in range(n_inp)])
+    relayed = [lax.ppermute(part, "inp", [(i, i ^ 6) for i in range(n_inp)]) for part in got1[:3]]
 
     ids = jnp.arange(width, dtype=jnp.int32)
 
@@ -219,7 +237,7 @@
     group_ids = jnp.arange(groups_all, dtype=jnp.int32)
     chan_ids = jnp.arange(channels, dtype=jnp.int32)
 
-    lag0 = pair_lags(jnp.arange(channels, dtype=jnp.int32), volts, perm, volts, volts, perm_rev, True)
+    lag0 = pair_lags(jnp.arange(channels, dtype=jnp.int32), volts, perm, volts, perm_rev, True)
     lag0 = lag0.reshape(channels, 2, 2, 2, 2 * width)
     center = (jnp.arange(2 * width) == width - 1)
     same = jnp.eye(2, dtype=bool)
@@ -232,16 +250,16 @@
     contrib_v.append(jnp.flip(lag0[..., :diffs], axis=-1).reshape(-1, 2, diffs))
     sign = jnp.array([1.0, -1.0], jnp.float32)
 
-    def meta_of(slab):
-        got_pos = slab[0, 0, rows, : blocks * width].astype(jnp.int32).reshape(blocks, width)
-        got_tg = slab[0, 0, rows + 1, : tg_flat.shape[0]].astype(jnp.int32).reshape(tile_group.shape)
+    def meta_of(slab, row):
+        got_pos = slab[0, 0, row, : blocks * width].astype(jnp.int32).reshape(blocks, width)
+        got_tg = slab[0, 0, row + 1, : tg_flat.shape[0]].astype(jnp.int32).reshape(tile_group.shape)
         return one_hot(got_pos, True), got_tg
 
-    perm1, tg1 = meta_of(got1[0])
-    perm0, tg0 = meta_of(got0)
-    lag10, relay_im = relay_lags(volts, perm, got1[0], got1[1], perm1, got0, perm0)
-    perm2, tg2 = meta_of(relay_re)
-    lag2 = pair_lags(mine[2][None].astype(jnp.int32), volts, perm, relay_re, relay_im, perm2, False)
+    perm1, tg1 = meta_of(got1[0], width)
+    perm0, tg0 = meta_of(got0, rows)
+    lag10, relay_last = relay_lags(volts, perm, got1, perm1, got0, perm0)
+    perm2, tg2 = meta_of(relayed[0], width)
+    lag2 = pair_lags(mine[2][None].astype(jnp.int32), volts, perm, relayed + [relay_last], perm2, False)
     level_lags = {0: (lag10[1], tg0), 1: (lag10[0], tg1), 2: (lag2[0], tg2)}
     for bit in range(levels):
         lag, got_tg = level_lags[bit]

time: 111 us -> 110 us (level)
  Pallas kernels: 51.5 us -> 39.6 us
  starting transfers between devices: 4.84 us -> 10.3 us
  other arithmetic: 6.6 us -> 9.61 us
  waiting for transfers between devices: 34.3 us -> 36.2 us
    pallas_call x1, Pallas kernels: 27.6 us -> 15 us  [relay_lags(): pl.pallas_call(relay_kernel, out_shape=(jax.ShapeDtypeStruct((2, 8, 2 * w...]
    ppermute x3 -> x7, starting transfers between devices: 4.73 us -> 10.2 us  [the longest x3 6.17 us: on_device(): lax.ppermute(part, 'inp', [(i, i ^ 6) for i in range(n_inp)])]
    select_n x0 -> x1, other arithmetic: none -> 3.35 us  [chunks(): jnp.where(chan == 1, volts[1, c, blk * width:(blk + 1) * width], volts[0,...]
    ppermute x3 -> x7, waiting for transfers between devices: 34.3 us -> 36.2 us  [the longest x3 20.8 us: on_device(): lax.ppermute(part, 'inp', [(i, i ^ 6) for i in range(n_inp)])]
    unnamed x20 -> x24, local copies, waits for them, and re-layouts: 7.44 us -> 9.26 us
    broadcast_in_dim x1 -> x0, local copies, waits for them, and re-layouts: 1.15 us -> none  [exchange(): return [lax.ppermute(slab[None, c:c + 1], 'inp', pairs) for c in range(2)]]
  transfers between devices with their start and end apart: 4 -> 8, of which waited for: 2 -> 3; matrix products, arithmetic and copies ran while one was open for 5% -> 8% of each run, Pallas kernels for 7% -> 21%
where the time goes in v5:
time: 110 us
  Pallas kernels  39.6 us (36%)
  waiting for transfers between devices  36.2 us (33%)
  local copies, waits for them, and re-layouts  13.1 us (12%)
  starting transfers between devices  10.3 us (9%)
  other arithmetic  9.61 us (9%)
    ppermute x3, waiting for transfers between devices, on_device(): lax.ppermute(part, 'inp', [(i, i ^ 6) for i in range(n_inp)])  20.8 us
    ppermute x4, waiting for transfers between devices, on_device(): lax.ppermute(part, 'inp', [(i, i ^ 2) for i in range(n_inp)])  15.4 us
    pallas_call x1, Pallas kernels, relay_lags(): pl.pallas_call(relay_kernel, out_shape=(jax.ShapeDtypeStruct((2, 8, 2 * w...  15 us
    pallas_call x2, Pallas kernels, pair_lags(): pl.pallas_call(lag_kernel, out_shape=jax.ShapeDtypeStruct((n, 8, 2 * widt...  13.1 us
    pallas_call x1, Pallas kernels, reduce_scatter(): pl.pallas_call(scatter_kernel, out_shape=jax.ShapeDtypeStruct(slab, jnp.f...  11.4 us
    unnamed x24, local copies, waits for them, and re-layouts  9.26 us
    ppermute x3, starting transfers between devices, on_device(): lax.ppermute(part, 'inp', [(i, i ^ 6) for i in range(n_inp)])  6.17 us
    ppermute x4, starting transfers between devices, on_device(): lax.ppermute(part, 'inp', [(i, i ^ 2) for i in range(n_inp)])  4.05 us
  transfers between devices with their start and end apart: 8, of which 3 were waited for; matrix products, arithmetic and copies ran while one was open for 8% of the time, Pallas kernels for 21%

profile of v5, /device:TPU:32, one launch (start us, length us, event | category | flops | bytes accessed | tf_op | source)
XLA Modules:
  0.0 109.8 jit_solution(10020236435534340122)
XLA Ops:
  0.0 0.8 copy.18
  0.9 0.7 copy.40
  1.6 3.4 %slice_select_fusion = (bf16[1,1,256,1024]{3,2,1,0:T(8,128)(2,1)}, bf16[1,1,256,1024]{3,2,1,0:T(8,128)(2,1)}, bf16[256,1024]{1,0:T(8,128)(2,1)S(1)}, bf16[1,1,256,1024]{3,2,1,0:T(8,128)(2,1)}) fusion(bf16[2,2,512,1024]{3,2,1,0:T(8,128)(2,1)} %xraw_ref.3, pred[]{:T(512)S(6)} %eq.271), kind=kLoop, calls=%fused_computation.7 | loop fusion | flops 1048576 | bytes 6291457 | tf_op jit(solution)/shard_map/jit(_where)/select_n | solution.py:210
  5.0 1.6 %collective-permute-start.1 = (bf16[1,1,272,1024]{3,2,1,0:T(8,128)(2,1)S(1)}, bf16[1,1,272,1024]{3,2,1,0:T(8,128)(2,1)S(1)}, u32[]{:S(2)}, u32[]{:S(2)}) collective-permute-start(bf16[1,1,272,1024]{3,2,1,0:T(8,128)(2,1)S(1)} %maximum_bitcast_fusion.1), channel_id=1, source_target_pairs={{0,32},{16,48},{32,0},{48,16},{64,96},{80,112},{96,64},{112,80},{1... | collective-permute-start | bytes 1671176 | tf_op jit(solution)/shard_map/ppermute | solution.py:218
  6.6 2.4 %select_bitcast_fusion = bf16[2,512,1024]{2,1,0:T(8,128)(2,1)S(1)} fusion(bf16[2,2,512,1024]{3,2,1,0:T(8,128)(2,1)} %xraw_ref.3, pred[]{:T(512)S(6)} %eq.258), kind=kLoop, calls=%fused_computation.1 | loop fusion | flops 1048576 | bytes 6291457 | tf_op jit(solution)/shard_map/jit(_where)/select_n | solution.py:220
  9.0 1.5 %maximum_bitcast_fusion = bf16[1,2,528,1024]{3,2,1,0:T(8,128)(2,1)} fusion(bf16[2,16,1024]{2,1,0:T(8,128)(2,1)S(1)} %pad.18, bf16[2,512,1024]{2,1,0:T(8,128)(2,1)S(1)} %select_bitcast_fusion), kind=kLoop, calls=%fused_computation | loop fusion | flops 4325376 | bytes 4325376 | tf_op jit(solution)/shard_map/broadcast_in_dim | solution.py:220
  10.5 0.1 collective-permute-start
  10.7 0.5 collective-permute-start.3
  11.1 1.6 %collective-permute-start.4 = (bf16[1,1,256,1024]{3,2,1,0:T(8,128)(2,1)}, bf16[1,1,256,1024]{3,2,1,0:T(8,128)(2,1)S(1)}, u32[]{:S(2)}, u32[]{:S(2)}) collective-permute-start(bf16[1,1,256,1024]{3,2,1,0:T(8,128)(2,1)} %get-tuple-element.14), channel_id=1, source_target_pairs={{0,32},{16,48},{32,0},{48,16},{64,96},{80,112},{96,64},{112,80},{1... | collective-permute-start | bytes 1572872 | tf_op jit(solution)/shard_map/ppermute | solution.py:218
  12.7 0.5 collective-permute-start.5
  13.1 0.1 fusion.xperm_ref
  13.3 0.2 rev.26
  13.5 0.1 fusion.1.yperm_ref
  13.7 2.2 %copy-done = bf16[2,2,512,1024]{3,2,1,0:T(8,128)(2,1)S(1)} copy-done((bf16[2,2,512,1024]{3,2,1,0:T(8,128)(2,1)S(1)}, bf16[2,2,512,1024]{3,2,1,0:T(8,128)(2,1)}, u32[]{:S(2)}) %copy-start) | copy-done | bytes 4194328
  15.8 7.7 %shard_map.46 = f32[2,8,512]{2,1,0:T(8,128)S(1)} custom-call(s32[2]{0:T(128)S(1)} %iota.43.sel_ref, bf16[2,2,512,1024]{3,2,1,0:T(8,128)(2,1)S(1)} %copy-done, bf16[2,256,256]{2,1,0:T(8,128)(2,1)S(1)} %fusion.xperm_ref, bf16[2,2,512,1024]{3,2,1,0:T(8,128)(2,1)S(1)} %copy-done, bf16[2,2,512,1024]{3,2,1,0:T(8,128)(2,1)S(1)} %copy-done, ...), custom_call_target="tpu_custom_call" | custom-call | flops 6442450944 | bytes 8388608 | tf_op jit(solution)/shard_map/pallas_call | solution.py:129
  23.6 0.1 copy.22
  23.8 0.4 reverse
  24.3 0.1 slice.175
  24.4 0.3 slice_reduce_fusion
  24.9 6.9 %collective-permute-done.3.y01 = bf16[1,1,256,1024]{3,2,1,0:T(8,128)(2,1)S(1)} collective-permute-done((bf16[1,1,256,1024]{3,2,1,0:T(8,128)(2,1)}, bf16[1,1,256,1024]{3,2,1,0:T(8,128)(2,1)S(1)}, u32[]{:S(2)}, u32[]{:S(2)}) %collective-permute-start.3) | collective-permute-done | bytes 524320 | tf_op jit(solution)/shard_map/ppermute | solution.py:218
  31.8 2.8 %collective-permute-start.6 = (bf16[1,1,256,1024]{3,2,1,0:T(8,128)(2,1)S(1)}, bf16[1,1,256,1024]{3,2,1,0:T(8,128)(2,1)}, u32[]{:S(2)}, u32[]{:S(2)}) collective-permute-start(bf16[1,1,256,1024]{3,2,1,0:T(8,128)(2,1)S(1)} %collective-permute-done.3.y01), channel_id=1, source_target_pairs={{0,96},{16,112},{32,64},{48,80},{64,32},{80,48},{96,0},{112,16},{1... | collective-permute-start | bytes 1572872 | tf_op jit(solution)/shard_map/ppermute | solution.py:224
  34.6 8.5 %collective-permute-done.4.y10 = bf16[1,1,256,1024]{3,2,1,0:T(8,128)(2,1)S(1)} collective-permute-done((bf16[1,1,256,1024]{3,2,1,0:T(8,128)(2,1)}, bf16[1,1,256,1024]{3,2,1,0:T(8,128)(2,1)S(1)}, u32[]{:S(2)}, u32[]{:S(2)}) %collective-permute-start.4) | collective-permute-done | bytes 524320 | tf_op jit(solution)/shard_map/ppermute | solution.py:218
  43.0 2.8 %collective-permute-start.7 = (bf16[1,1,256,1024]{3,2,1,0:T(8,128)(2,1)S(1)}, bf16[1,1,256,1024]{3,2,1,0:T(8,128)(2,1)}, u32[]{:S(2)}, u32[]{:S(2)}) collective-permute-start(bf16[1,1,256,1024]{3,2,1,0:T(8,128)(2,1)S(1)} %collective-permute-done.4.y10), channel_id=1, source_target_pairs={{0,96},{16,112},{32,64},{48,80},{64,32},{80,48},{96,0},{112,16},{1... | collective-permute-start | bytes 1572872 | tf_op jit(solution)/shard_map/ppermute | solution.py:224
  45.9 0.1 copy.20
  46.0 0.7 collective-permute-start.2
  46.7 0.2 rev.28
  47.0 0.1 fusion.2.yperm_ref
  47.1 20.8 %collective-permute-done.2.y00 = bf16[1,1,272,1024]{3,2,1,0:T(8,128)(2,1)S(1)} collective-permute-done((bf16[1,1,272,1024]{3,2,1,0:T(8,128)(2,1)S(1)}, bf16[1,1,272,1024]{3,2,1,0:T(8,128)(2,1)S(1)}, u32[]{:S(2)}, u32[]{:S(2)}) %collective-permute-start.2) | collective-permute-done | bytes 557088 | tf_op jit(solution)/shard_map/ppermute | solution.py:224
  68.0 0.7 slice_reduce_fusion.4
  68.7 0.1 copy.21
  68.9 0.7 fusion.8
  69.7 0.2 rev.29
  69.9 0.1 fusion.3.zperm_ref
  70.1 15.0 %shard_map.47 = (f32[2,8,512]{2,1,0:T(8,128)S(1)}, bf16[1,1,256,1024]{3,2,1,0:T(8,128)(2,1)S(1)}) custom-call(bf16[2,2,512,1024]{3,2,1,0:T(8,128)(2,1)} %xraw_ref.3, bf16[2,256,256]{2,1,0:T(8,128)(2,1)S(1)} %fusion.xperm_ref, bf16[1,1,272,1024]{3,2,1,0:T(8,128)(2,1)S(1)} %collective-permute-done.1.y00, ...), custom_call_target="tpu_custom_call" | custom-call | flops 25769803776 | bytes 16777216 | tf_op jit(solution)/shard_map/pallas_call | solution.py:86
  85.1 0.8 copy-done.1
  85.9 0.1 copy.19
  86.0 0.2 rev.32
  86.3 0.1 fusion.4.yperm_ref
  86.5 1.0 copy-done.2
  87.5 5.4 %shard_map.48 = f32[1,8,512]{2,1,0:T(8,128)S(1)} custom-call(s32[1]{0:T(128)} %bitcast.28.sel_ref, bf16[2,2,512,1024]{3,2,1,0:T(8,128)(2,1)} %xraw_ref.3, bf16[2,256,256]{2,1,0:T(8,128)(2,1)S(1)} %fusion.xperm_ref, bf16[1,1,272,1024]{3,2,1,0:T(8,128)(2,1)S(1)} %collective-permute-done.2.y00, bf16[1,1,256,1024]{3,2,1,0:T(8,128)(2,1)} %collective-permute-done.6.y01, ...), custom_call_target="tpu_custom_call" | custom-call | flops 3221225472 | bytes 4194304 | tf_op jit(solution)/shard_map/pallas_call | solution.py:129
  93.1 0.4 reverse.1
  93.6 0.4 reverse.2
  94.0 0.4 reverse.3
  94.8 0.6 convolution_multiply_fusion
  95.5 0.4 copy.39
  95.9 1.0 pad.19.clone
  96.9 11.4 %shard_map.49 = f32[8,2,2,512]{3,2,1,0:T(2,128)} custom-call(f32[8,8,2,2,512]{4,3,2,1,0:T(2,128)} %bitcast.55), custom_call_target="tpu_custom_call" | custom-call | tf_op jit(solution)/shard_map/pallas_call | solution.py:181
  108.3 1.5 %copy.42 = f32[8,2,2,511]{3,2,1,0:T(2,128)} copy(f32[8,2,2,511]{3,2,1,0:T(2,128)} %bitcast.56) | data formatting | bytes 130816
  (66 shorter events, 1.9 us)
Async XLA Ops:
  5.0 40.8 %collective-permute-start.1 = (bf16[1,1,272,1024]{3,2,1,0:T(8,128)(2,1)S(1)}, bf16[1,1,272,1024]{3,2,1,0:T(8,128)(2,1)S(1)}, u32[]{:S(2)}, u32[]{:S(2)}) collective-permute-start(bf16[1,1,272,1024]{3,2,1,0:T(8,128)(2,1)S(1)} %maximum_bitcast_fusion.1), channel_id=1, source_target_pairs={{0,32},{16,48},{32,0},{48,16},{64,96},{80,112},{96,64},{112,80},{1... | collective-permute-start | bytes 1671176 | tf_op jit(solution)/shard_map/ppermute | solution.py:218
  9.0 4.1 %copy-start.4 = (s32[2,256]{1,0:T(2,128)S(1)}, s32[2,256]{1,0:T(2,128)}, u32[]{:S(2)}) copy-start(s32[2,256]{1,0:T(2,128)} %param.5) | copy-start | bytes 6148
  10.5 57.4 %collective-permute-start = (bf16[1,2,528,1024]{3,2,1,0:T(8,128)(2,1)}, bf16[1,2,528,1024]{3,2,1,0:T(8,128)(2,1)}, u32[]{:S(2)}, u32[]{:S(2)}) collective-permute-start(bf16[1,2,528,1024]{3,2,1,0:T(8,128)(2,1)} %maximum_bitcast_fusion), channel_id=1, source_target_pairs={{0,16},{16,0},{32,48},{48,32},{64,80},{80,64},{96,112},{112,96},{1... | collective-permute-start | bytes 6488072 | tf_op jit(solution)/shard_map/ppermute | solution.py:219
  10.7 21.2 %collective-permute-start.3 = (bf16[1,1,256,1024]{3,2,1,0:T(8,128)(2,1)}, bf16[1,1,256,1024]{3,2,1,0:T(8,128)(2,1)S(1)}, u32[]{:S(2)}, u32[]{:S(2)}) collective-permute-start(bf16[1,1,256,1024]{3,2,1,0:T(8,128)(2,1)} %get-tuple-element.16), channel_id=1, source_target_pairs={{0,32},{16,48},{32,0},{48,16},{64,96},{80,112},{96,64},{112,80},{1... | collective-permute-start | bytes 1572872 | tf_op jit(solution)/shard_map/ppermute | solution.py:218
  11.1 31.9 %collective-permute-start.4 = (bf16[1,1,256,1024]{3,2,1,0:T(8,128)(2,1)}, bf16[1,1,256,1024]{3,2,1,0:T(8,128)(2,1)S(1)}, u32[]{:S(2)}, u32[]{:S(2)}) collective-permute-start(bf16[1,1,256,1024]{3,2,1,0:T(8,128)(2,1)} %get-tuple-element.14), channel_id=1, source_target_pairs={{0,32},{16,48},{32,0},{48,16},{64,96},{80,112},{96,64},{112,80},{1... | collective-permute-start | bytes 1572872 | tf_op jit(solution)/shard_map/ppermute | solution.py:218
  12.7 57.4 %collective-permute-start.5 = (bf16[1,1,256,1024]{3,2,1,0:T(8,128)(2,1)}, bf16[1,1,256,1024]{3,2,1,0:T(8,128)(2,1)S(1)}, u32[]{:S(2)}, u32[]{:S(2)}) collective-permute-start(bf16[1,1,256,1024]{3,2,1,0:T(8,128)(2,1)} %get-tuple-element.13), channel_id=1, source_target_pairs={{0,32},{16,48},{32,0},{48,16},{64,96},{80,112},{96,64},{112,80},{1... | collective-permute-start | bytes 1572872 | tf_op jit(solution)/shard_map/ppermute | solution.py:218
  13.6 2.2 %copy-start = (bf16[2,2,512,1024]{3,2,1,0:T(8,128)(2,1)S(1)}, bf16[2,2,512,1024]{3,2,1,0:T(8,128)(2,1)}, u32[]{:S(2)}) copy-start(bf16[2,2,512,1024]{3,2,1,0:T(8,128)(2,1)} %xraw_ref.3) | copy-start | bytes 12582916
  15.8 8.6 %copy-start.3 = (s32[2,4,2]{1,2,0:T(2,128)S(1)}, s32[2,4,2]{1,2,0:T(2,128)}, u32[]{:S(2)}) copy-start(s32[2,4,2]{1,2,0:T(2,128)} %param.6) | copy-start | bytes 196
  31.8 54.6 %collective-permute-start.6 = (bf16[1,1,256,1024]{3,2,1,0:T(8,128)(2,1)S(1)}, bf16[1,1,256,1024]{3,2,1,0:T(8,128)(2,1)}, u32[]{:S(2)}, u32[]{:S(2)}) collective-permute-start(bf16[1,1,256,1024]{3,2,1,0:T(8,128)(2,1)S(1)} %collective-permute-done.3.y01), channel_id=1, source_target_pairs={{0,96},{16,112},{32,64},{48,80},{64,32},{80,48},{96,0},{112,16},{1... | collective-permute-start | bytes 1572872 | tf_op jit(solution)/shard_map/ppermute | solution.py:224
  43.0 43.4 %collective-permute-start.7 = (bf16[1,1,256,1024]{3,2,1,0:T(8,128)(2,1)S(1)}, bf16[1,1,256,1024]{3,2,1,0:T(8,128)(2,1)}, u32[]{:S(2)}, u32[]{:S(2)}) collective-permute-start(bf16[1,1,256,1024]{3,2,1,0:T(8,128)(2,1)S(1)} %collective-permute-done.4.y10), channel_id=1, source_target_pairs={{0,96},{16,112},{32,64},{48,80},{64,32},{80,48},{96,0},{112,16},{1... | collective-permute-start | bytes 1572872 | tf_op jit(solution)/shard_map/ppermute | solution.py:224
  46.0 21.9 %collective-permute-start.2 = (bf16[1,1,272,1024]{3,2,1,0:T(8,128)(2,1)S(1)}, bf16[1,1,272,1024]{3,2,1,0:T(8,128)(2,1)S(1)}, u32[]{:S(2)}, u32[]{:S(2)}) collective-permute-start(bf16[1,1,272,1024]{3,2,1,0:T(8,128)(2,1)S(1)} %collective-permute-done.1.y00), channel_id=1, source_target_pairs={{0,96},{16,112},{32,64},{48,80},{64,32},{80,48},{96,0},{112,16},{1... | collective-permute-start | bytes 1671176 | tf_op jit(solution)/shard_map/ppermute | solution.py:224
  85.1 0.8 copy-start.1
  86.4 1.0 copy-start.2
  87.5 5.5 %copy-start.5 = (f32[2]{0:T(128)S(1)}, f32[2]{0:T(128)}, u32[]{:S(2)}) copy-start(f32[2]{0:T(128)} %constant.23.clone) | copy-start | bytes 28

commit v6 on v5

--- a/solution.py
+++ b/solution.py
@@ -46,9 +46,7 @@
     )
 
 
-def relay_kernel(x_ref, xperm_ref, y00, y01, y10, y11, yperm_ref, z_ref, zperm_ref,
-                 o_ref, relay_ref, xs, ys, send_sem, recv_sem):
-    width = xperm_ref.shape[1]
+def start_relay(src_ref, dst_ref, send_sem, recv_sem):
     me = lax.axis_index("inp")
     fq = lax.axis_index("freq")
     onward = lax.bitwise_xor(me, 6)
@@ -56,14 +54,40 @@
     pl.semaphore_signal(barrier, inc=1, device_id=(onward, fq), device_id_type=MESH)
     pl.semaphore_wait(barrier, 1)
     copy = pltpu.make_async_remote_copy(
-        src_ref=y11,
-        dst_ref=relay_ref,
+        src_ref=src_ref,
+        dst_ref=dst_ref,
         send_sem=send_sem,
         recv_sem=recv_sem,
         device_id=(onward, fq),
         device_id_type=MESH,
     )
     copy.start()
+    return copy
+
+
+def relay_only_kernel(chunk_ref, prev_ref, relay_ref, send_sem, recv_sem):
+    del prev_ref
+    start_relay(chunk_ref, relay_ref, send_sem, recv_sem).wait()
+
+
+def relay_own_kernel(chunk_ref, x_ref, xperm_ref, yperm_ref, o_ref, relay_ref, xs, ys, send_sem, recv_sem):
+    width = xperm_ref.shape[1]
+    copy = start_relay(chunk_ref, relay_ref, send_sem, recv_sem)
+    for f in range(x_ref.shape[0]):
+        lags_into(
+            lambda a, c, f=f: block_rows(x_ref, f, c, a, width),
+            lambda b, c, f=f: block_rows(x_ref, f, c, b, width),
+            xperm_ref, yperm_ref, o_ref, f, xs, ys,
+        )
+    copy.wait()
+
+
+def relay_kernel(x_ref, xperm_ref, y00, y01, y10, y11, yperm_ref, z_ref, zperm_ref, prev_ref,
+                 o_ref, relay_ref, xs, ys, send_sem, recv_sem):
+    del prev_ref
+    width = xperm_ref.shape[1]
+    me = lax.axis_index("inp")
+    copy = start_relay(y11, relay_ref, send_sem, recv_sem)
     parity = lax.bitwise_and(lax.bitwise_xor(lax.shift_right_logical(me, 1), lax.shift_right_logical(me, 2)), 1)
     ys_in = ((y00, y01), (y10, y11))
     lags_into(
@@ -79,32 +103,26 @@
     copy.wait()
 
 
-def relay_lags(x_all, x_perm, y_parts, y_perm, z_all, z_perm):
-    width = x_perm.shape[1]
-    samples = x_all.shape[-1]
+def relay_call(kernel, args, outs, n_lags, width, samples, collective_id):
     vmem = pl.BlockSpec(memory_space=pltpu.VMEM)
+    scratch = []
+    if n_lags:
+        outs = (jax.ShapeDtypeStruct((n_lags, 8, 2 * width), jnp.float32),) + outs
+        scratch = [pltpu.VMEM((2, 2, width, samples), jnp.bfloat16)] * 2
     return pl.pallas_call(
-        relay_kernel,
-        out_shape=(
-            jax.ShapeDtypeStruct((2, 8, 2 * width), jnp.float32),
-            jax.ShapeDtypeStruct(y_parts[3].shape, y_parts[3].dtype),
-        ),
-        in_specs=[vmem] * 9,
-        out_specs=(vmem, vmem),
-        scratch_shapes=[
-            pltpu.VMEM((2, 2, width, samples), x_all.dtype),
-            pltpu.VMEM((2, 2, width, samples), x_all.dtype),
-            pltpu.SemaphoreType.DMA(()),
-            pltpu.SemaphoreType.DMA(()),
-        ],
+        kernel,
+        out_shape=outs,
+        in_specs=[vmem] * len(args),
+        out_specs=tuple(vmem for _ in outs),
+        scratch_shapes=scratch + [pltpu.SemaphoreType.DMA(()), pltpu.SemaphoreType.DMA(())],
         compiler_params=pltpu.CompilerParams(
-            collective_id=1, has_side_effects=True, vmem_limit_bytes=48 * 1024 * 1024
+            collective_id=collective_id, has_side_effects=True, vmem_limit_bytes=48 * 1024 * 1024
         ),
         cost_estimate=pl.CostEstimate(
-            flops=2 * 4 * 24 * 2 * width * width * samples, transcendentals=0,
+            flops=max(n_lags, 1) * 4 * 24 * 2 * width * width * samples, transcendentals=0,
             bytes_accessed=4 * 2 * 4 * width * samples * 2,
         ),
-    )(x_all, x_perm, *y_parts, y_perm, z_all, z_perm)
+    )(*args)
 
 
 def pair_lags(sel, x_raw, x_perm, y_parts, y_perm, y_by_sel):
@@ -221,8 +239,6 @@
         "inp",
         [(i, i ^ 1) for i in range(n_inp)],
     )
-    relayed = [lax.ppermute(part, "inp", [(i, i ^ 6) for i in range(n_inp)]) for part in got1[:3]]
-
     ids = jnp.arange(width, dtype=jnp.int32)
 
     def one_hot(pos, reverse):
@@ -237,7 +253,13 @@
     group_ids = jnp.arange(groups_all, dtype=jnp.int32)
     chan_ids = jnp.arange(channels, dtype=jnp.int32)
 
-    lag0 = pair_lags(jnp.arange(channels, dtype=jnp.int32), volts, perm, volts, perm_rev, True)
+    chunk_shape = lambda k: (jax.ShapeDtypeStruct(got1[k].shape, got1[k].dtype),)
+    lag0, relay0 = relay_call(
+        relay_own_kernel, (got1[0], volts, perm, perm_rev), chunk_shape(0), channels, width, samples, 1
+    )
+    (relay1,) = relay_call(relay_only_kernel, (got1[1], relay0), chunk_shape(1), 0, width, samples, 2)
+    (relay2,) = relay_call(relay_only_kernel, (got1[2], relay1), chunk_shape(2), 0, width, samples, 3)
+    relayed = [relay0, relay1, relay2]
     lag0 = lag0.reshape(channels, 2, 2, 2, 2 * width)
     center = (jnp.arange(2 * width) == width - 1)
     same = jnp.eye(2, dtype=bool)
@@ -257,7 +279,9 @@
 
     perm1, tg1 = meta_of(got1[0], width)
     perm0, tg0 = meta_of(got0, rows)
-    lag10, relay_last = relay_lags(volts, perm, got1, perm1, got0, perm0)
+    lag10, relay_last = relay_call(
+        relay_kernel, (volts, perm, *got1, perm1, got0, perm0, relay2), chunk_shape(3), 2, width, samples, 4
+    )
     perm2, tg2 = meta_of(relayed[0], width)
     lag2 = pair_lags(mine[2][None].astype(jnp.int32), volts, perm, relayed + [relay_last], perm2, False)
     level_lags = {0: (lag10[1], tg0), 1: (lag10[0], tg1), 2: (lag2[0], tg2)}

time: 110 us -> 103 us (0.936)
  waiting for transfers between devices: 36.2 us -> 6.22 us
  Pallas kernels: 39.6 us -> 66.9 us
  starting transfers between devices: 10.3 us -> 4.16 us
  local copies, waits for them, and re-layouts: 13.1 us -> 15 us
    pallas_call x1 -> x4, Pallas kernels: 15 us -> 50.3 us  [relay_call(): pl.pallas_call(kernel, out_shape=outs, in_specs=[vmem] * len(args), out_s...]
    ppermute x3 -> x0, waiting for transfers between devices: 20.8 us -> none  [on_device(): lax.ppermute(part, 'inp', [(i, i ^ 6) for i in range(n_inp)])]
    ppermute x4, waiting for transfers between devices: 15.4 us -> 6.22 us  [on_device(): lax.ppermute(part, 'inp', [(i, i ^ 2) for i in range(n_inp)])]
    pallas_call x2 -> x1, Pallas kernels: 13.1 us -> 5.17 us  [pair_lags(): pl.pallas_call(lag_kernel, out_shape=jax.ShapeDtypeStruct((n, 8, 2 * widt...]
    ppermute x3 -> x0, starting transfers between devices: 6.17 us -> none  [on_device(): lax.ppermute(part, 'inp', [(i, i ^ 6) for i in range(n_inp)])]
    unnamed x24 -> x32, local copies, waits for them, and re-layouts: 9.26 us -> 11.2 us
  transfers between devices with their start and end apart: 8 -> 5, of which waited for: 3 -> 1; matrix products, arithmetic and copies ran while one was open for 8% -> 9% of each run, Pallas kernels for 21% -> 36%
where the time goes in v6:
time: 103 us
  Pallas kernels  66.9 us (65%)
  local copies, waits for them, and re-layouts  15 us (15%)
  other arithmetic  9.61 us (9%)
  waiting for transfers between devices  6.22 us (6%)
  starting transfers between devices  4.16 us (4%)
    pallas_call x4, Pallas kernels, relay_call(): pl.pallas_call(kernel, out_shape=outs, in_specs=[vmem] * len(args), out_s...  50.3 us
    pallas_call x1, Pallas kernels, reduce_scatter(): pl.pallas_call(scatter_kernel, out_shape=jax.ShapeDtypeStruct(slab, jnp.f...  11.4 us
    unnamed x32, local copies, waits for them, and re-layouts  11.2 us
    ppermute x4, waiting for transfers between devices, on_device(): lax.ppermute(part, 'inp', [(i, i ^ 2) for i in range(n_inp)])  6.22 us
    pallas_call x1, Pallas kernels, pair_lags(): pl.pallas_call(lag_kernel, out_shape=jax.ShapeDtypeStruct((n, 8, 2 * widt...  5.17 us
    ppermute x4, starting transfers between devices, on_device(): lax.ppermute(part, 'inp', [(i, i ^ 2) for i in range(n_inp)])  4.05 us
    select_n x1, other arithmetic, chunks(): jnp.where(chan == 1, volts[1, c, blk * width:(blk + 1) * width], volts[0,...  3.35 us
    select_n x1, other arithmetic, on_device(): jnp.where(mine[0] == 0, volts[1], volts[0])  2.44 us
  transfers between devices with their start and end apart: 5, of which 1 were waited for; matrix products, arithmetic and copies ran while one was open for 9% of the time, Pallas kernels for 36%

profile of v6, /device:TPU:32, one launch (start us, length us, event | category | flops | bytes accessed | tf_op | source)
XLA Modules:
  0.0 102.9 jit_solution(1159688424726948025)
XLA Ops:
  0.0 0.8 copy.18
  0.9 0.7 copy.40
  1.6 3.4 %slice_select_fusion = (bf16[1,1,256,1024]{3,2,1,0:T(8,128)(2,1)}, bf16[1,1,256,1024]{3,2,1,0:T(8,128)(2,1)}, bf16[256,1024]{1,0:T(8,128)(2,1)S(1)}, bf16[1,1,256,1024]{3,2,1,0:T(8,128)(2,1)}) fusion(bf16[2,2,512,1024]{3,2,1,0:T(8,128)(2,1)} %xraw_ref.1, pred[]{:T(512)S(6)} %eq.271), kind=kLoop, calls=%fused_computation.7 | loop fusion | flops 1048576 | bytes 6291457 | tf_op jit(solution)/shard_map/jit(_where)/select_n | solution.py:228
  5.0 1.6 %collective-permute-start.1 = (bf16[1,1,272,1024]{3,2,1,0:T(8,128)(2,1)S(1)}, bf16[1,1,272,1024]{3,2,1,0:T(8,128)(2,1)S(1)}, u32[]{:S(2)}, u32[]{:S(2)}) collective-permute-start(bf16[1,1,272,1024]{3,2,1,0:T(8,128)(2,1)S(1)} %maximum_bitcast_fusion.1), channel_id=1, source_target_pairs={{0,32},{16,48},{32,0},{48,16},{64,96},{80,112},{96,64},{112,80},{1... | collective-permute-start | bytes 1671176 | tf_op jit(solution)/shard_map/ppermute | solution.py:236
  6.6 2.4 %select_bitcast_fusion = bf16[2,512,1024]{2,1,0:T(8,128)(2,1)S(1)} fusion(bf16[2,2,512,1024]{3,2,1,0:T(8,128)(2,1)} %xraw_ref.1, pred[]{:T(512)S(6)} %eq.258), kind=kLoop, calls=%fused_computation.1 | loop fusion | flops 1048576 | bytes 6291457 | tf_op jit(solution)/shard_map/jit(_where)/select_n | solution.py:238
  9.0 1.5 %maximum_bitcast_fusion = bf16[1,2,528,1024]{3,2,1,0:T(8,128)(2,1)} fusion(bf16[2,16,1024]{2,1,0:T(8,128)(2,1)S(1)} %pad.18, bf16[2,512,1024]{2,1,0:T(8,128)(2,1)S(1)} %select_bitcast_fusion), kind=kLoop, calls=%fused_computation | loop fusion | flops 4325376 | bytes 4325376 | tf_op jit(solution)/shard_map/broadcast_in_dim | solution.py:238
  10.6 0.1 collective-permute-start
  10.7 0.5 collective-permute-start.2
  11.1 1.6 %collective-permute-start.3 = (bf16[1,1,256,1024]{3,2,1,0:T(8,128)(2,1)}, bf16[1,1,256,1024]{3,2,1,0:T(8,128)(2,1)S(1)}, u32[]{:S(2)}, u32[]{:S(2)}) collective-permute-start(bf16[1,1,256,1024]{3,2,1,0:T(8,128)(2,1)} %get-tuple-element.18), channel_id=1, source_target_pairs={{0,32},{16,48},{32,0},{48,16},{64,96},{80,112},{96,64},{112,80},{1... | collective-permute-start | bytes 1572872 | tf_op jit(solution)/shard_map/ppermute | solution.py:236
  12.7 0.5 collective-permute-start.4
  13.2 0.2 rev.26
  13.3 0.3 slice_reduce_fusion
  13.7 0.1 copy.22
  14.1 0.1 fusion.xperm_ref
  14.2 0.1 fusion.1.yperm_ref
  14.4 6.2 %collective-permute-done.1.chunk_ref.y00 = bf16[1,1,272,1024]{3,2,1,0:T(8,128)(2,1)S(1)} collective-permute-done((bf16[1,1,272,1024]{3,2,1,0:T(8,128)(2,1)S(1)}, bf16[1,1,272,1024]{3,2,1,0:T(8,128)(2,1)S(1)}, u32[]{:S(2)}, u32[]{:S(2)}) %collective-permute-start.1) | collective-permute-done | bytes 557088 | tf_op jit(solution)/shard_map/ppermute | solution.py:236
  20.6 2.2 %copy-done = bf16[2,2,512,1024]{3,2,1,0:T(8,128)(2,1)S(1)} copy-done((bf16[2,2,512,1024]{3,2,1,0:T(8,128)(2,1)S(1)}, bf16[2,2,512,1024]{3,2,1,0:T(8,128)(2,1)}, u32[]{:S(2)}) %copy-start) | copy-done | bytes 4194328
  22.8 13.7 %shard_map.46 = (f32[2,8,512]{2,1,0:T(8,128)S(1)}, bf16[1,1,272,1024]{3,2,1,0:T(8,128)(2,1)S(1)}) custom-call(bf16[1,1,272,1024]{3,2,1,0:T(8,128)(2,1)S(1)} %collective-permute-done.1.chunk_ref.y00, bf16[2,2,512,1024]{3,2,1,0:T(8,128)(2,1)S(1)} %copy-done, bf16[2,256,256]{2,1,0:T(8,128)(2,1)S(1)} %fusion.xperm_ref, bf16[2,256,256]{2,1,0:T(8,128)(2,1)S(1)} %fusion.1.yperm_ref), custom_call_target="tpu_custom_call" | custom-call | flops 25769803776 | bytes 16777216 | tf_op jit(solution)/shard_map/pallas_call | solution.py:112
  36.5 0.1 convert_element_type.92
  36.6 12.1 %shard_map.47.prev_ref.y01 = bf16[1,1,256,1024]{3,2,1,0:T(8,128)(2,1)S(1)} custom-call(bf16[1,1,256,1024]{3,2,1,0:T(8,128)(2,1)S(1)} %collective-permute-done.2.chunk_ref.y01, bf16[1,1,272,1024]{3,2,1,0:T(8,128)(2,1)S(1)} %get-tuple-element.9.prev_ref.y00), custom_call_target="tpu_custom_call" | custom-call | flops 12884901888 | bytes 16777216 | tf_op jit(solution)/shard_map/pallas_call | solution.py:112
  48.7 0.8 copy-done.1
  49.5 0.1 copy.21
  49.7 0.2 rev.32
  49.9 0.4 reverse
  50.3 0.1 slice.171
  50.5 0.1 fusion.4.yperm_ref
  50.7 1.0 %copy-done.2 = bf16[1,1,256,1024]{3,2,1,0:T(8,128)(2,1)S(1)} copy-done((bf16[1,1,256,1024]{3,2,1,0:T(8,128)(2,1)S(1)}, bf16[1,1,256,1024]{3,2,1,0:T(8,128)(2,1)}, u32[]{:S(2)}) %copy-start.2) | copy-done | bytes 524312
  51.7 11.1 %shard_map.48.prev_ref.y10 = bf16[1,1,256,1024]{3,2,1,0:T(8,128)(2,1)S(1)} custom-call(bf16[1,1,256,1024]{3,2,1,0:T(8,128)(2,1)S(1)} %collective-permute-done.3.chunk_ref.y10, bf16[1,1,256,1024]{3,2,1,0:T(8,128)(2,1)S(1)} %copy-done.2), custom_call_target="tpu_custom_call" | custom-call | flops 12884901888 | bytes 16777216 | tf_op jit(solution)/shard_map/pallas_call | solution.py:112
  62.9 0.8 copy-done.4
  63.7 0.7 slice_reduce_fusion.4
  64.5 0.1 copy.20
  64.7 0.1 copy.19
  64.9 0.7 fusion.8
  65.6 0.2 rev.28
  65.9 0.2 rev.29
  66.1 0.1 fusion.2.yperm_ref
  66.2 0.1 fusion.3.zperm_ref
  66.4 1.1 %copy-done.5 = bf16[1,1,256,1024]{3,2,1,0:T(8,128)(2,1)S(1)} copy-done((bf16[1,1,256,1024]{3,2,1,0:T(8,128)(2,1)S(1)}, bf16[1,1,256,1024]{3,2,1,0:T(8,128)(2,1)}, u32[]{:S(2)}) %copy-start.5) | copy-done | bytes 524312
  67.5 13.3 %shard_map.49 = (f32[2,8,512]{2,1,0:T(8,128)S(1)}, bf16[1,1,256,1024]{3,2,1,0:T(8,128)(2,1)S(1)}) custom-call(bf16[2,2,512,1024]{3,2,1,0:T(8,128)(2,1)} %xraw_ref.1, bf16[2,256,256]{2,1,0:T(8,128)(2,1)S(1)} %fusion.xperm_ref, bf16[1,1,272,1024]{3,2,1,0:T(8,128)(2,1)S(1)} %collective-permute-done.1.chunk_ref.y00, ...), custom_call_target="tpu_custom_call" | custom-call | flops 25769803776 | bytes 16777216 | tf_op jit(solution)/shard_map/pallas_call | solution.py:112
  80.9 5.2 %shard_map.50 = f32[1,8,512]{2,1,0:T(8,128)S(1)} custom-call(s32[1]{0:T(128)} %bitcast.28.sel_ref, bf16[2,2,512,1024]{3,2,1,0:T(8,128)(2,1)} %xraw_ref.1, bf16[2,256,256]{2,1,0:T(8,128)(2,1)S(1)} %fusion.xperm_ref, bf16[1,1,272,1024]{3,2,1,0:T(8,128)(2,1)S(1)} %get-tuple-element.9.prev_ref.y00, bf16[1,1,256,1024]{3,2,1,0:T(8,128)(2,1)S(1)} %copy-done.3, ...), custom_call_target="tpu_custom_call" | custom-call | flops 3221225472 | bytes 4194304 | tf_op jit(solution)/shard_map/pallas_call | solution.py:147
  86.2 0.4 reverse.1
  86.7 0.4 reverse.2
  87.2 0.4 reverse.3
  88.0 0.6 convolution_multiply_fusion
  88.6 0.4 copy.39
  89.0 1.0 pad.19.clone
  90.0 11.4 %shard_map.51 = f32[8,2,2,512]{3,2,1,0:T(2,128)} custom-call(f32[8,8,2,2,512]{4,3,2,1,0:T(2,128)} %bitcast.55), custom_call_target="tpu_custom_call" | custom-call | tf_op jit(solution)/shard_map/pallas_call | solution.py:199
  101.5 1.5 %copy.42 = f32[8,2,2,511]{3,2,1,0:T(2,128)} copy(f32[8,2,2,511]{3,2,1,0:T(2,128)} %bitcast.56) | data formatting | bytes 130816
  (69 shorter events, 1.8 us)
Async XLA Ops:
  5.0 15.6 %collective-permute-start.1 = (bf16[1,1,272,1024]{3,2,1,0:T(8,128)(2,1)S(1)}, bf16[1,1,272,1024]{3,2,1,0:T(8,128)(2,1)S(1)}, u32[]{:S(2)}, u32[]{:S(2)}) collective-permute-start(bf16[1,1,272,1024]{3,2,1,0:T(8,128)(2,1)S(1)} %maximum_bitcast_fusion.1), channel_id=1, source_target_pairs={{0,32},{16,48},{32,0},{48,16},{64,96},{80,112},{96,64},{112,80},{1... | collective-permute-start | bytes 1671176 | tf_op jit(solution)/shard_map/ppermute | solution.py:236
  9.0 4.1 %copy-start.8 = (s32[2,256]{1,0:T(2,128)S(1)}, s32[2,256]{1,0:T(2,128)}, u32[]{:S(2)}) copy-start(s32[2,256]{1,0:T(2,128)} %param.5) | copy-start | bytes 6148
  9.0 4.3 %copy-start.7 = (s32[2,4,2]{1,2,0:T(2,128)S(1)}, s32[2,4,2]{1,2,0:T(2,128)}, u32[]{:S(2)}) copy-start(s32[2,4,2]{1,2,0:T(2,128)} %param.6) | copy-start | bytes 196
  10.6 53.1 %collective-permute-start = (bf16[1,2,528,1024]{3,2,1,0:T(8,128)(2,1)}, bf16[1,2,528,1024]{3,2,1,0:T(8,128)(2,1)}, u32[]{:S(2)}, u32[]{:S(2)}) collective-permute-start(bf16[1,2,528,1024]{3,2,1,0:T(8,128)(2,1)} %maximum_bitcast_fusion), channel_id=1, source_target_pairs={{0,16},{16,0},{32,48},{48,32},{64,80},{80,64},{96,112},{112,96},{1... | collective-permute-start | bytes 6488072 | tf_op jit(solution)/shard_map/ppermute | solution.py:237
  10.7 25.9 %collective-permute-start.2 = (bf16[1,1,256,1024]{3,2,1,0:T(8,128)(2,1)}, bf16[1,1,256,1024]{3,2,1,0:T(8,128)(2,1)S(1)}, u32[]{:S(2)}, u32[]{:S(2)}) collective-permute-start(bf16[1,1,256,1024]{3,2,1,0:T(8,128)(2,1)} %get-tuple-element.20), channel_id=1, source_target_pairs={{0,32},{16,48},{32,0},{48,16},{64,96},{80,112},{96,64},{112,80},{1... | collective-permute-start | bytes 1572872 | tf_op jit(solution)/shard_map/ppermute | solution.py:236
  11.1 39.5 %collective-permute-start.3 = (bf16[1,1,256,1024]{3,2,1,0:T(8,128)(2,1)}, bf16[1,1,256,1024]{3,2,1,0:T(8,128)(2,1)S(1)}, u32[]{:S(2)}, u32[]{:S(2)}) collective-permute-start(bf16[1,1,256,1024]{3,2,1,0:T(8,128)(2,1)} %get-tuple-element.18), channel_id=1, source_target_pairs={{0,32},{16,48},{32,0},{48,16},{64,96},{80,112},{96,64},{112,80},{1... | collective-permute-start | bytes 1572872 | tf_op jit(solution)/shard_map/ppermute | solution.py:236
  12.7 53.7 %collective-permute-start.4 = (bf16[1,1,256,1024]{3,2,1,0:T(8,128)(2,1)}, bf16[1,1,256,1024]{3,2,1,0:T(8,128)(2,1)S(1)}, u32[]{:S(2)}, u32[]{:S(2)}) collective-permute-start(bf16[1,1,256,1024]{3,2,1,0:T(8,128)(2,1)} %get-tuple-element.17), channel_id=1, source_target_pairs={{0,32},{16,48},{32,0},{48,16},{64,96},{80,112},{96,64},{112,80},{1... | collective-permute-start | bytes 1572872 | tf_op jit(solution)/shard_map/ppermute | solution.py:236
  20.6 2.2 %copy-start = (bf16[2,2,512,1024]{3,2,1,0:T(8,128)(2,1)S(1)}, bf16[2,2,512,1024]{3,2,1,0:T(8,128)(2,1)}, u32[]{:S(2)}) copy-start(bf16[2,2,512,1024]{3,2,1,0:T(8,128)(2,1)} %xraw_ref.1) | copy-start | bytes 12582916
  48.7 0.8 copy-start.1
  50.7 1.0 %copy-start.2 = (bf16[1,1,256,1024]{3,2,1,0:T(8,128)(2,1)S(1)}, bf16[1,1,256,1024]{3,2,1,0:T(8,128)(2,1)}, u32[]{:S(2)}) copy-start(bf16[1,1,256,1024]{3,2,1,0:T(8,128)(2,1)} %copy-done.1) | copy-start | bytes 1572868
  62.9 0.8 copy-start.4
  66.4 14.5 %copy-start.3 = (bf16[1,1,256,1024]{3,2,1,0:T(8,128)(2,1)S(1)}, bf16[1,1,256,1024]{3,2,1,0:T(8,128)(2,1)}, u32[]{:S(2)}) copy-start(bf16[1,1,256,1024]{3,2,1,0:T(8,128)(2,1)} %copy-done.1) | copy-start | bytes 1572868
  66.4 1.1 %copy-start.5 = (bf16[1,1,256,1024]{3,2,1,0:T(8,128)(2,1)S(1)}, bf16[1,1,256,1024]{3,2,1,0:T(8,128)(2,1)}, u32[]{:S(2)}) copy-start(bf16[1,1,256,1024]{3,2,1,0:T(8,128)(2,1)} %copy-done.4) | copy-start | bytes 1572868
  67.5 13.4 %copy-start.6 = (bf16[1,1,256,1024]{3,2,1,0:T(8,128)(2,1)S(1)}, bf16[1,1,256,1024]{3,2,1,0:T(8,128)(2,1)}, u32[]{:S(2)}) copy-start(bf16[1,1,256,1024]{3,2,1,0:T(8,128)(2,1)} %copy-done.4) | copy-start | bytes 1572868
  80.9 5.3 %copy-start.9 = (f32[2]{0:T(128)S(1)}, f32[2]{0:T(128)}, u32[]{:S(2)}) copy-start(f32[2]{0:T(128)} %constant.23.clone) | copy-start | bytes 28

commit v7 on v6

--- a/solution.py
+++ b/solution.py
@@ -1,3 +1,5 @@
+import functools
+
 import jax
 import jax.numpy as jnp
 from jax import lax
@@ -11,16 +13,17 @@
 MESH = pl.DeviceIdType.MESH
 
 
-def lags_into(get_x, get_y, xperm_ref, yperm_ref, o_ref, slot, xs, ys):
+def lags_into(get_x, get_y, xperm_ref, yperm_ref, o_ref, slot, xs, ys, b_list=(0, 1)):
     for blk in range(2):
         for c in range(2):
             xs[blk, c] = jnp.dot(xperm_ref[blk], get_x(blk, c), preferred_element_type=jnp.float32).astype(xs.dtype)
-            ys[blk, c] = jnp.dot(yperm_ref[blk], get_y(blk, c), preferred_element_type=jnp.float32).astype(ys.dtype)
+            if blk in b_list:
+                ys[blk, c] = jnp.dot(yperm_ref[blk], get_y(blk, c), preferred_element_type=jnp.float32).astype(ys.dtype)
     dot = lambda u, v: lax.dot_general(u, v, NT, preferred_element_type=jnp.float32)
     for a in range(2):
         xre = xs[a, 0]
         xim = xs[a, 1]
-        for b in range(2):
+        for b_at, b in enumerate(b_list):
             yre = ys[b, 0]
             yim = ys[b, 1]
             real_part = dot(xre, yre) + dot(xim, yim)
@@ -28,7 +31,7 @@
             for c, part in enumerate((real_part, imag_part)):
                 padded = jnp.concatenate([part, jnp.zeros_like(part)], axis=1)
                 sheared = pltpu.roll(padded, 0, 1, stride=1, stride_axis=0)
-                row = (a * 2 + b) * 2 + c
+                row = (a * len(b_list) + b_at) * 2 + c
                 o_ref[slot, pl.ds(row, 1), :] = jnp.sum(sheared, axis=0, keepdims=True)
 
 
@@ -36,13 +39,13 @@
     return ref[chan, c, pl.ds(blk * width, width), :]
 
 
-def lag_kernel(sel_ref, xraw_ref, xperm_ref, y00, y01, y10, y11, yperm_ref, o_ref, xs, ys):
+def lag_kernel(b_list, sel_ref, xraw_ref, xperm_ref, y00, y01, y10, y11, yperm_ref, o_ref, xs, ys):
     width = xperm_ref.shape[1]
     ys_in = ((y00, y01), (y10, y11))
     lags_into(
         lambda a, c: block_rows(xraw_ref, 0, c, a, width),
         lambda b, c: ys_in[b][c][0, 0, pl.ds(0, width), :],
-        xperm_ref, yperm_ref, o_ref, 0, xs, ys,
+        xperm_ref, yperm_ref, o_ref, 0, xs, ys, b_list,
     )
 
 
@@ -82,32 +85,48 @@
     copy.wait()
 
 
-def relay_kernel(x_ref, xperm_ref, y00, y01, y10, y11, yperm_ref, z_ref, zperm_ref, prev_ref,
-                 o_ref, relay_ref, xs, ys, send_sem, recv_sem):
+def relay_mid_kernel(chunk_ref, prev_ref, x_ref, xperm_ref, y00, y01, yperm_ref, r00, r01, rperm_ref,
+                     o_ref, relay_ref, xs, ys, send_sem, recv_sem):
     del prev_ref
     width = xperm_ref.shape[1]
     me = lax.axis_index("inp")
+    copy = start_relay(chunk_ref, relay_ref, send_sem, recv_sem)
+    parity = lax.bitwise_and(lax.bitwise_xor(lax.shift_right_logical(me, 1), lax.shift_right_logical(me, 2)), 1)
+    for slot, parts in enumerate(((y00, y01), (r00, r01))):
+        lags_into(
+            lambda a, c: block_rows(x_ref, parity, c, a, width),
+            lambda b, c, parts=parts: parts[c][0, 0, pl.ds(0, width), :],
+            xperm_ref, (yperm_ref, rperm_ref)[slot], o_ref, slot, xs, ys, (0,),
+        )
+    copy.wait()
+
+
+def relay_kernel(x_ref, xperm_ref, y10, y11, yperm_ref, z_ref, zperm_ref, prev_ref,
+                 o_ref, p_ref, relay_ref, xs, ys, send_sem, recv_sem):
+    del prev_ref
+    width = xperm_ref.shape[1]
+    me = lax.axis_index("inp")
     copy = start_relay(y11, relay_ref, send_sem, recv_sem)
     parity = lax.bitwise_and(lax.bitwise_xor(lax.shift_right_logical(me, 1), lax.shift_right_logical(me, 2)), 1)
-    ys_in = ((y00, y01), (y10, y11))
+    parts = (y10, y11)
     lags_into(
         lambda a, c: block_rows(x_ref, parity, c, a, width),
-        lambda b, c: ys_in[b][c][0, 0, pl.ds(0, width), :],
-        xperm_ref, yperm_ref, o_ref, 0, xs, ys,
+        lambda b, c: parts[c][0, 0, pl.ds(0, width), :],
+        xperm_ref, yperm_ref, o_ref, 0, xs, ys, (1,),
     )
     lags_into(
         lambda a, c: block_rows(x_ref, lax.bitwise_and(me, 1), c, a, width),
         lambda b, c: block_rows(z_ref, 0, c, b, width),
-        xperm_ref, zperm_ref, o_ref, 1, xs, ys,
+        xperm_ref, zperm_ref, p_ref, 0, xs, ys,
     )
     copy.wait()
 
 
-def relay_call(kernel, args, outs, n_lags, width, samples, collective_id):
+def relay_call(kernel, args, outs, lag_shapes, width, samples, collective_id):
     vmem = pl.BlockSpec(memory_space=pltpu.VMEM)
     scratch = []
-    if n_lags:
-        outs = (jax.ShapeDtypeStruct((n_lags, 8, 2 * width), jnp.float32),) + outs
+    if lag_shapes:
+        outs = tuple(jax.ShapeDtypeStruct(s + (2 * width,), jnp.float32) for s in lag_shapes) + outs
         scratch = [pltpu.VMEM((2, 2, width, samples), jnp.bfloat16)] * 2
     return pl.pallas_call(
         kernel,
@@ -119,13 +138,13 @@
             collective_id=collective_id, has_side_effects=True, vmem_limit_bytes=48 * 1024 * 1024
         ),
         cost_estimate=pl.CostEstimate(
-            flops=max(n_lags, 1) * 4 * 24 * 2 * width * width * samples, transcendentals=0,
+            flops=max(len(lag_shapes), 1) * 4 * 24 * 2 * width * width * samples, transcendentals=0,
             bytes_accessed=4 * 2 * 4 * width * samples * 2,
         ),
     )(*args)
 
 
-def pair_lags(sel, x_raw, x_perm, y_parts, y_perm, y_by_sel):
+def pair_lags(sel, x_raw, x_perm, y_parts, y_perm, y_by_sel, b_list=(0, 1)):
     n = sel.shape[0]
     _, _, rows_x, samples = x_raw.shape
     width = x_perm.shape[1]
@@ -142,11 +161,12 @@
         ]
         y_args = list(y_parts)
     perm_spec = pl.BlockSpec((2, width, width), lambda i, s: (0, 0, 0))
-    out_spec = pl.BlockSpec((1, 8, 2 * width), lambda i, s: (i, 0, 0))
-    flops = n * (16 + 8) * 2 * width * width * samples
+    n_rows = 4 * len(b_list)
+    out_spec = pl.BlockSpec((1, n_rows, 2 * width), lambda i, s: (i, 0, 0))
+    flops = n * (8 * len(b_list) + 8) * 2 * width * width * samples
     return pl.pallas_call(
-        lag_kernel,
-        out_shape=jax.ShapeDtypeStruct((n, 8, 2 * width), jnp.float32),
+        functools.partial(lag_kernel, b_list),
+        out_shape=jax.ShapeDtypeStruct((n, n_rows, 2 * width), jnp.float32),
         grid_spec=pltpu.PrefetchScalarGridSpec(
             num_scalar_prefetch=1,
             grid=(n,),
@@ -255,11 +275,9 @@
 
     chunk_shape = lambda k: (jax.ShapeDtypeStruct(got1[k].shape, got1[k].dtype),)
     lag0, relay0 = relay_call(
-        relay_own_kernel, (got1[0], volts, perm, perm_rev), chunk_shape(0), channels, width, samples, 1
-    )
-    (relay1,) = relay_call(relay_only_kernel, (got1[1], relay0), chunk_shape(1), 0, width, samples, 2)
-    (relay2,) = relay_call(relay_only_kernel, (got1[2], relay1), chunk_shape(2), 0, width, samples, 3)
-    relayed = [relay0, relay1, relay2]
+        relay_own_kernel, (got1[0], volts, perm, perm_rev), chunk_shape(0), [(channels, 8)], width, samples, 1
+    )
+    (relay1,) = relay_call(relay_only_kernel, (got1[1], relay0), chunk_shape(1), [], width, samples, 2)
     lag0 = lag0.reshape(channels, 2, 2, 2, 2 * width)
     center = (jnp.arange(2 * width) == width - 1)
     same = jnp.eye(2, dtype=bool)
@@ -278,13 +296,23 @@
         return one_hot(got_pos, True), got_tg
 
     perm1, tg1 = meta_of(got1[0], width)
+    perm2, tg2 = meta_of(relay0, width)
+    lag_b0, relay2 = relay_call(
+        relay_mid_kernel, (got1[2], relay1, volts, perm, got1[0], got1[1], perm1, relay0, relay1, perm2),
+        chunk_shape(2), [(2, 4)], width, samples, 3,
+    )
+    got0, _ = lax.optimization_barrier((got0, relay2))
     perm0, tg0 = meta_of(got0, rows)
-    lag10, relay_last = relay_call(
-        relay_kernel, (volts, perm, *got1, perm1, got0, perm0, relay2), chunk_shape(3), 2, width, samples, 4
-    )
-    perm2, tg2 = meta_of(relayed[0], width)
-    lag2 = pair_lags(mine[2][None].astype(jnp.int32), volts, perm, relayed + [relay_last], perm2, False)
-    level_lags = {0: (lag10[1], tg0), 1: (lag10[0], tg1), 2: (lag2[0], tg2)}
+    lag1_b1, lag_bit0, relay3 = relay_call(
+        relay_kernel, (volts, perm, got1[2], got1[3], perm1, got0, perm0, relay2),
+        chunk_shape(3), [(1, 4), (1, 8)], width, samples, 4,
+    )
+    lag2_b1 = pair_lags(
+        mine[2][None].astype(jnp.int32), volts, perm, [relay0, relay1, relay2, relay3], perm2, False, (1,)
+    )
+    lag1 = jnp.stack([lag_b0[0].reshape(2, 2, -1), lag1_b1[0].reshape(2, 2, -1)], axis=1)
+    lag2 = jnp.stack([lag_b0[1].reshape(2, 2, -1), lag2_b1[0].reshape(2, 2, -1)], axis=1)
+    level_lags = {0: (lag_bit0[0], tg0), 1: (lag1, tg1), 2: (lag2, tg2)}
     for bit in range(levels):
         lag, got_tg = level_lags[bit]
         lag = lag.reshape(2, 2, 2, 2 * width)[..., :diffs]

time: 103 us -> 142 us (1.38)
  waiting for transfers between devices: 6.22 us -> 37 us
  Pallas kernels: 66.9 us -> 72 us
  other arithmetic: 9.61 us -> 12.4 us
    ppermute x4, waiting for transfers between devices: 6.22 us -> 37 us  [on_device(): lax.ppermute(part, 'inp', [(i, i ^ 2) for i in range(n_inp)])]
    pallas_call x4, Pallas kernels: 50.3 us -> 56.8 us  [relay_call(): pl.pallas_call(kernel, out_shape=outs, in_specs=[vmem] * len(args), out_s...]
    another operation x8, other arithmetic: 0.37 us -> 2.06 us
    unnamed x32 -> x36, local copies, waits for them, and re-layouts: 11.2 us -> 9.82 us
  transfers between devices with their start and end apart: 5 -> 5, of which waited for: 1 -> 1; matrix products, arithmetic and copies ran while one was open for 9% -> 9% of each run, Pallas kernels for 36% -> 30%
where the time goes in v7:
time: 142 us
  Pallas kernels  72 us (51%)
  waiting for transfers between devices  37 us (26%)
  local copies, waits for them, and re-layouts  15.1 us (11%)
  other arithmetic  12.4 us (9%)
  starting transfers between devices  4.16 us (3%)
    pallas_call x4, Pallas kernels, relay_call(): pl.pallas_call(kernel, out_shape=outs, in_specs=[vmem] * len(args), out_s...  56.8 us
    ppermute x4, waiting for transfers between devices, on_device(): lax.ppermute(part, 'inp', [(i, i ^ 2) for i in range(n_inp)])  37 us
    pallas_call x1, Pallas kernels, reduce_scatter(): pl.pallas_call(scatter_kernel, out_shape=jax.ShapeDtypeStruct(slab, jnp.f...  11.3 us
    unnamed x36, local copies, waits for them, and re-layouts  9.82 us
    ppermute x4, starting transfers between devices, on_device(): lax.ppermute(part, 'inp', [(i, i ^ 2) for i in range(n_inp)])  4.13 us
    pallas_call x1, Pallas kernels, pair_lags(): pl.pallas_call(functools.partial(lag_kernel, b_list), out_shape=jax.Shape...  3.82 us
    select_n x1, other arithmetic, chunks(): jnp.where(chan == 1, volts[1, c, blk * width:(blk + 1) * width], volts[0,...  3.37 us
  transfers between devices with their start and end apart: 5, of which 1 were waited for; matrix products, arithmetic and copies ran while one was open for 9% of the time, Pallas kernels for 30%

profile of v7, /device:TPU:32, one launch (start us, length us, event | category | flops | bytes accessed | tf_op | source)
XLA Modules:
  0.0 141.7 jit_solution(1982601769795667264)
XLA Ops:
  0.0 3.4 %slice_select_fusion.1 = (bf16[1,1,256,1024]{3,2,1,0:T(8,128)(2,1)}, bf16[1,1,256,1024]{3,2,1,0:T(8,128)(2,1)}, bf16[256,1024]{1,0:T(8,128)(2,1)S(1)}, bf16[1,1,256,1024]{3,2,1,0:T(8,128)(2,1)}) fusion(bf16[2,2,512,1024]{3,2,1,0:T(8,128)(2,1)} %xraw_ref.1, pred[]{:T(512)S(6)} %eq.259), kind=kLoop, calls=%fused_computation.11 | loop fusion | flops 1048576 | bytes 6291457 | tf_op jit(solution)/shard_map/jit(_where)/select_n | solution.py:248
  3.4 1.5 %collective-permute-start.2 = (bf16[1,1,256,1024]{3,2,1,0:T(8,128)(2,1)}, bf16[1,1,256,1024]{3,2,1,0:T(8,128)(2,1)S(1)}, u32[]{:S(2)}, u32[]{:S(2)}) collective-permute-start(bf16[1,1,256,1024]{3,2,1,0:T(8,128)(2,1)} %get-tuple-element.25), channel_id=1, source_target_pairs={{0,32},{16,48},{32,0},{48,16},{64,96},{80,112},{96,64},{112,80},{1... | collective-permute-start | bytes 1572872 | tf_op jit(solution)/shard_map/ppermute | solution.py:256
  4.9 0.5 collective-permute-start.1
  5.4 1.5 %collective-permute-start.4 = (bf16[1,1,256,1024]{3,2,1,0:T(8,128)(2,1)}, bf16[1,1,256,1024]{3,2,1,0:T(8,128)(2,1)S(1)}, u32[]{:S(2)}, u32[]{:S(2)}) collective-permute-start(bf16[1,1,256,1024]{3,2,1,0:T(8,128)(2,1)} %get-tuple-element.28), channel_id=1, source_target_pairs={{0,32},{16,48},{32,0},{48,16},{64,96},{80,112},{96,64},{112,80},{1... | collective-permute-start | bytes 1572872 | tf_op jit(solution)/shard_map/ppermute | solution.py:256
  6.9 0.1 copy.19
  7.2 0.6 collective-permute-start.3
  7.8 2.4 %select_bitcast_fusion = bf16[2,512,1024]{2,1,0:T(8,128)(2,1)S(1)} fusion(bf16[2,2,512,1024]{3,2,1,0:T(8,128)(2,1)} %xraw_ref.1, pred[]{:T(512)S(6)} %eq.258), kind=kLoop, calls=%fused_computation.1 | loop fusion | flops 1048576 | bytes 6291457 | tf_op jit(solution)/shard_map/jit(_where)/select_n | solution.py:258
  10.3 1.5 %maximum_bitcast_fusion = bf16[1,2,528,1024]{3,2,1,0:T(8,128)(2,1)} fusion(bf16[2,16,1024]{2,1,0:T(8,128)(2,1)S(1)} %pad.18, bf16[2,512,1024]{2,1,0:T(8,128)(2,1)S(1)} %select_bitcast_fusion), kind=kLoop, calls=%fused_computation | loop fusion | flops 4325376 | bytes 4325376 | tf_op jit(solution)/shard_map/broadcast_in_dim | solution.py:258
  11.8 0.6 compare_convert_fusion.8
  12.4 0.2 rev.26
  12.6 0.3 slice_reduce_fusion
  12.9 0.1 copy.23
  13.1 0.7 compare_convert_fusion.1
  13.9 0.5 compare_convert_fusion.7
  14.4 0.1 fusion.xperm_ref
  14.6 0.1 fusion.1.yperm_ref
  14.7 37.0 %collective-permute-done.3.chunk_ref.y00 = bf16[1,1,272,1024]{3,2,1,0:T(8,128)(2,1)S(1)} collective-permute-done((bf16[1,1,272,1024]{3,2,1,0:T(8,128)(2,1)S(1)}, bf16[1,1,272,1024]{3,2,1,0:T(8,128)(2,1)S(1)}, u32[]{:S(2)}, u32[]{:S(2)}) %collective-permute-start.3) | collective-permute-done | bytes 557088 | tf_op jit(solution)/shard_map/ppermute | solution.py:256
  51.7 2.2 %copy-done = bf16[2,2,512,1024]{3,2,1,0:T(8,128)(2,1)S(1)} copy-done((bf16[2,2,512,1024]{3,2,1,0:T(8,128)(2,1)S(1)}, bf16[2,2,512,1024]{3,2,1,0:T(8,128)(2,1)}, u32[]{:S(2)}) %copy-start) | copy-done | bytes 4194328
  53.9 14.8 %shard_map.46 = (f32[2,8,512]{2,1,0:T(8,128)S(1)}, bf16[1,1,272,1024]{3,2,1,0:T(8,128)(2,1)S(1)}) custom-call(bf16[1,1,272,1024]{3,2,1,0:T(8,128)(2,1)S(1)} %collective-permute-done.3.chunk_ref.y00, bf16[2,2,512,1024]{3,2,1,0:T(8,128)(2,1)S(1)} %copy-done, bf16[2,256,256]{2,1,0:T(8,128)(2,1)S(1)} %fusion.xperm_ref, bf16[2,256,256]{2,1,0:T(8,128)(2,1)S(1)} %fusion.1.yperm_ref), custom_call_target="tpu_custom_call" | custom-call | flops 12884901888 | bytes 16777216 | tf_op jit(solution)/shard_map/pallas_call | solution.py:131
  68.9 0.2 rev.28
  69.1 0.1 fusion.3.rperm_ref.yperm_ref
  69.2 13.3 %shard_map.47.prev_ref.r01.y01 = bf16[1,1,256,1024]{3,2,1,0:T(8,128)(2,1)S(1)} custom-call(bf16[1,1,256,1024]{3,2,1,0:T(8,128)(2,1)S(1)} %collective-permute-done.2.chunk_ref.y01, bf16[1,1,272,1024]{3,2,1,0:T(8,128)(2,1)S(1)} %get-tuple-element.13.prev_ref.r00.y00), custom_call_target="tpu_custom_call" | custom-call | flops 12884901888 | bytes 16777216 | tf_op jit(solution)/shard_map/pallas_call | solution.py:131
  82.5 0.8 copy-done.1
  83.4 0.5 slice_convert_fusion.2
  84.0 0.2 rev.27
  84.2 0.1 fusion.2.yperm_ref
  84.3 0.5 slice_convert_fusion.1
  84.9 0.4 reverse
  85.4 0.7 copy.21
  86.1 0.7 copy.22
  86.8 1.0 copy-done.2
  87.9 14.5 %shard_map.48 = (f32[2,4,512]{2,1,0:T(4,128)S(1)}, bf16[1,1,256,1024]{3,2,1,0:T(8,128)(2,1)S(1)}) custom-call(bf16[1,1,256,1024]{3,2,1,0:T(8,128)(2,1)S(1)} %collective-permute-done.1.chunk_ref.y10, bf16[1,1,256,1024]{3,2,1,0:T(8,128)(2,1)S(1)} %copy-done.2, bf16[2,2,512,1024]{3,2,1,0:T(8,128)(2,1)} %xraw_ref.1, bf16[2,256,256]{2,1,0:T(8,128)(2,1)S(1)} %fusion.xperm_ref, ...), custom_call_target="tpu_custom_call" | custom-call | flops 12884901888 | bytes 16777216 | tf_op jit(solution)/shard_map/pallas_call | solution.py:131
  102.4 0.8 copy-done.4
  103.4 0.7 slice_reduce_fusion.6
  104.3 0.7 convert_reduce_fusion
  105.1 0.2 rev.30
  105.4 0.1 fusion.4.zperm_ref
  105.6 1.1 copy-done.5
  106.7 14.2 %shard_map.49 = (f32[1,4,512]{2,1,0:T(4,128)S(1)}, f32[1,8,512]{2,1,0:T(8,128)S(1)}, bf16[1,1,256,1024]{3,2,1,0:T(8,128)(2,1)S(1)}) custom-call(bf16[2,2,512,1024]{3,2,1,0:T(8,128)(2,1)} %xraw_ref.1, bf16[2,256,256]{2,1,0:T(8,128)(2,1)S(1)} %fusion.xperm_ref, bf16[1,1,256,1024]{3,2,1,0:T(8,128)(2,1)S(1)} %collective-permute-done.1.chunk_ref.y10, ...), custom_call_target="tpu_custom_call" | custom-call | flops 25769803776 | bytes 16777216 | tf_op jit(solution)/shard_map/pallas_call | solution.py:131
  120.9 3.8 %shard_map.50 = f32[1,4,512]{2,1,0:T(4,128)S(1)} custom-call(s32[1]{0:T(128)} %bitcast.24.sel_ref, bf16[2,2,512,1024]{3,2,1,0:T(8,128)(2,1)} %xraw_ref.1, bf16[2,256,256]{2,1,0:T(8,128)(2,1)S(1)} %fusion.xperm_ref, bf16[1,1,272,1024]{3,2,1,0:T(8,128)(2,1)S(1)} %get-tuple-element.13.prev_ref.r00.y00, bf16[1,1,256,1024]{3,2,1,0:T(8,128)(2,1)S(1)} %copy-done.3, ...), custom_call_target="tpu_custom_call" | custom-call | flops 2147483648 | bytes 4194304 | tf_op jit(solution)/shard_map/pallas_call | solution.py:167
  125.0 0.4 reverse.3
  125.5 0.4 reverse.2
  126.0 0.4 reverse.1
  126.8 0.6 convolution_multiply_fusion
  127.5 0.4 copy.36
  127.9 1.0 pad.19.clone
  128.8 11.3 %shard_map.51 = f32[8,2,2,512]{3,2,1,0:T(2,128)} custom-call(f32[8,8,2,2,512]{4,3,2,1,0:T(2,128)} %bitcast.61), custom_call_target="tpu_custom_call" | custom-call | tf_op jit(solution)/shard_map/pallas_call | solution.py:219
  140.2 1.5 %copy.41 = f32[8,2,2,511]{3,2,1,0:T(2,128)} copy(f32[8,2,2,511]{3,2,1,0:T(2,128)} %bitcast.62) | data formatting | bytes 130816
  (81 shorter events, 2.2 us)
Async XLA Ops:
  0.0 6.9 %copy-start.7 = (s32[2,256]{1,0:T(2,128)S(1)}, s32[2,256]{1,0:T(2,128)}, u32[]{:S(2)}) copy-start(s32[2,256]{1,0:T(2,128)} %param.5) | copy-start | bytes 6148
  0.0 6.9 %copy-start.6 = (s32[2,4,2]{1,2,0:T(2,128)S(1)}, s32[2,4,2]{1,2,0:T(2,128)}, u32[]{:S(2)}) copy-start(s32[2,4,2]{1,2,0:T(2,128)} %param.6) | copy-start | bytes 196
  3.4 65.9 %collective-permute-start.2 = (bf16[1,1,256,1024]{3,2,1,0:T(8,128)(2,1)}, bf16[1,1,256,1024]{3,2,1,0:T(8,128)(2,1)S(1)}, u32[]{:S(2)}, u32[]{:S(2)}) collective-permute-start(bf16[1,1,256,1024]{3,2,1,0:T(8,128)(2,1)} %get-tuple-element.25), channel_id=1, source_target_pairs={{0,32},{16,48},{32,0},{48,16},{64,96},{80,112},{96,64},{112,80},{1... | collective-permute-start | bytes 1572872 | tf_op jit(solution)/shard_map/ppermute | solution.py:256
  4.9 82.0 %collective-permute-start.1 = (bf16[1,1,256,1024]{3,2,1,0:T(8,128)(2,1)}, bf16[1,1,256,1024]{3,2,1,0:T(8,128)(2,1)S(1)}, u32[]{:S(2)}, u32[]{:S(2)}) collective-permute-start(bf16[1,1,256,1024]{3,2,1,0:T(8,128)(2,1)} %get-tuple-element.26), channel_id=1, source_target_pairs={{0,32},{16,48},{32,0},{48,16},{64,96},{80,112},{96,64},{112,80},{1... | collective-permute-start | bytes 1572872 | tf_op jit(solution)/shard_map/ppermute | solution.py:256
  5.4 100.1 %collective-permute-start.4 = (bf16[1,1,256,1024]{3,2,1,0:T(8,128)(2,1)}, bf16[1,1,256,1024]{3,2,1,0:T(8,128)(2,1)S(1)}, u32[]{:S(2)}, u32[]{:S(2)}) collective-permute-start(bf16[1,1,256,1024]{3,2,1,0:T(8,128)(2,1)} %get-tuple-element.28), channel_id=1, source_target_pairs={{0,32},{16,48},{32,0},{48,16},{64,96},{80,112},{96,64},{112,80},{1... | collective-permute-start | bytes 1572872 | tf_op jit(solution)/shard_map/ppermute | solution.py:256
  7.2 44.5 %collective-permute-start.3 = (bf16[1,1,272,1024]{3,2,1,0:T(8,128)(2,1)S(1)}, bf16[1,1,272,1024]{3,2,1,0:T(8,128)(2,1)S(1)}, u32[]{:S(2)}, u32[]{:S(2)}) collective-permute-start(bf16[1,1,272,1024]{3,2,1,0:T(8,128)(2,1)S(1)} %maximum_bitcast_fusion.1), channel_id=1, source_target_pairs={{0,32},{16,48},{32,0},{48,16},{64,96},{80,112},{96,64},{112,80},{1... | collective-permute-start | bytes 1671176 | tf_op jit(solution)/shard_map/ppermute | solution.py:256
  11.8 91.7 %collective-permute-start = (bf16[1,2,528,1024]{3,2,1,0:T(8,128)(2,1)}, bf16[1,2,528,1024]{3,2,1,0:T(8,128)(2,1)}, u32[]{:S(2)}, u32[]{:S(2)}) collective-permute-start(bf16[1,2,528,1024]{3,2,1,0:T(8,128)(2,1)} %maximum_bitcast_fusion), channel_id=1, source_target_pairs={{0,16},{16,0},{32,48},{48,32},{64,80},{80,64},{96,112},{112,96},{1... | collective-permute-start | bytes 6488072 | tf_op jit(solution)/shard_map/ppermute | solution.py:257
  51.7 2.2 %copy-start = (bf16[2,2,512,1024]{3,2,1,0:T(8,128)(2,1)S(1)}, bf16[2,2,512,1024]{3,2,1,0:T(8,128)(2,1)}, u32[]{:S(2)}) copy-start(bf16[2,2,512,1024]{3,2,1,0:T(8,128)(2,1)} %xraw_ref.1) | copy-start | bytes 12582916
  82.5 0.8 copy-start.1
  86.8 1.0 copy-start.2
  87.9 15.5 %copy-start.8 = (f32[2,2,64]{2,1,0:T(2,128)S(1)}, f32[2,2,64]{2,1,0:T(2,128)}, u32[]{:S(2)}) copy-start(f32[2,2,64]{2,1,0:T(2,128)} %get-tuple-element.50) | copy-start | bytes 3076
  87.9 15.5 %copy-start.11 = (f32[2]{0:T(128)S(1)}, f32[2]{0:T(128)}, u32[]{:S(2)}) copy-start(f32[2]{0:T(128)} %compare_convert_fusion.7) | copy-start | bytes 28
  102.4 0.8 copy-start.4
  105.5 15.4 %copy-start.3 = (bf16[1,1,256,1024]{3,2,1,0:T(8,128)(2,1)S(1)}, bf16[1,1,256,1024]{3,2,1,0:T(8,128)(2,1)}, u32[]{:S(2)}) copy-start(bf16[1,1,256,1024]{3,2,1,0:T(8,128)(2,1)} %copy-done.1) | copy-start | bytes 1572868
  105.6 1.1 copy-start.5
  120.9 3.9 %copy-start.9 = (f32[2]{0:T(128)S(1)}, f32[2]{0:T(128)}, u32[]{:S(2)}) copy-start(f32[2]{0:T(128)} %constant.23.clone) | copy-start | bytes 28
  120.9 5.7 %copy-start.10 = (f32[2]{0:T(128)S(1)}, f32[2]{0:T(128)}, u32[]{:S(2)}) copy-start(f32[2]{0:T(128)} %compare_convert_fusion.8) | copy-start | bytes 28

commit v8 on v7

--- a/solution.py
+++ b/solution.py
@@ -249,7 +249,7 @@
                                         volts[0, c, blk * width:(blk + 1) * width])
         parts = [pick(c, blk) for blk in range(2) for c in range(2)]
         parts[0] = jnp.concatenate([parts[0], meta[0]], axis=0)
-        return [part[None, None] for part in parts]
+        return [part[None, None] for part in lax.optimization_barrier(tuple(parts))]
 
     mine = [me & 1] + [((me >> 1) ^ (me >> 2)) & 1] * min(levels - 1, 2)
     mine += [(me >> bit) & 1 for bit in range(3, levels)]

time: 142 us -> 108 us (0.76)
  waiting for transfers between devices: 37 us -> 3.97 us
  Pallas kernels: 72 us -> 67.5 us
  local copies, waits for them, and re-layouts: 15.1 us -> 17.1 us
    ppermute x4, waiting for transfers between devices: 37 us -> 3.96 us  [on_device(): lax.ppermute(part, 'inp', [(i, i ^ 2) for i in range(n_inp)])]
    pallas_call x4, Pallas kernels: 56.8 us -> 52.4 us  [relay_call(): pl.pallas_call(kernel, out_shape=outs, in_specs=[vmem] * len(args), out_s...]
    unnamed x36 -> x50, local copies, waits for them, and re-layouts: 9.82 us -> 13 us
  transfers between devices with their start and end apart: 5 -> 5, of which waited for: 1 -> 1; matrix products, arithmetic and copies ran while one was open for 9% -> 12% of each run, Pallas kernels for 30% -> 37%
where the time goes in v8:
time: 108 us; the launch traced here: 107 us
  Pallas kernels  67.5 us (62%)
  local copies, waits for them, and re-layouts  17.1 us (16%)
  other arithmetic  13.1 us (12%)
  starting transfers between devices  4.16 us (4%)
  waiting for transfers between devices  3.97 us (4%)
    pallas_call x4, Pallas kernels, relay_call(): pl.pallas_call(kernel, out_shape=outs, in_specs=[vmem] * len(args), out_s...  52.4 us
    unnamed x50, local copies, waits for them, and re-layouts  13 us
    pallas_call x1, Pallas kernels, reduce_scatter(): pl.pallas_call(scatter_kernel, out_shape=jax.ShapeDtypeStruct(slab, jnp.f...  11.3 us
    ppermute x4, starting transfers between devices, on_device(): lax.ppermute(part, 'inp', [(i, i ^ 2) for i in range(n_inp)])  4.05 us
    ppermute x4, waiting for transfers between devices, on_device(): lax.ppermute(part, 'inp', [(i, i ^ 2) for i in range(n_inp)])  3.96 us
    pallas_call x1, Pallas kernels, pair_lags(): pl.pallas_call(functools.partial(lag_kernel, b_list), out_shape=jax.Shape...  3.82 us
    select_n x1, other arithmetic, chunks(): jnp.where(chan == 1, volts[1, c, blk * width:(blk + 1) * width], volts[0,...  3.36 us
    select_n x1, other arithmetic, on_device(): jnp.where(mine[0] == 0, volts[1], volts[0])  2.44 us
  transfers between devices with their start and end apart: 5, of which 1 were waited for; matrix products, arithmetic and copies ran while one was open for 12% of the time, Pallas kernels for 37%

profile of v8, /device:TPU:32, one launch (start us, length us, event | category | flops | bytes accessed | tf_op | source)
XLA Modules:
  0.0 107.0 jit_solution(3167235263411705726)
XLA Ops:
  0.0 0.8 copy.19
  0.9 0.7 copy.37
  1.6 3.4 %select_bitcast_fusion.1 = (bf16[256,1024]{1,0:T(8,128)(2,1)}, bf16[256,1024]{1,0:T(8,128)(2,1)}, bf16[256,1024]{1,0:T(8,128)(2,1)S(1)}, bf16[256,1024]{1,0:T(8,128)(2,1)}) fusion(bf16[2,2,512,1024]{3,2,1,0:T(8,128)(2,1)} %xraw_ref.1, pred[]{:T(512)S(6)} %eq.259), kind=kLoop, calls=%fused_computation.9 | loop fusion | flops 1048576 | bytes 6291457 | tf_op jit(solution)/shard_map/jit(_where)/select_n | solution.py:248
  5.0 1.6 %collective-permute-start.3 = (bf16[1,1,272,1024]{3,2,1,0:T(8,128)(2,1)S(1)}, bf16[1,1,272,1024]{3,2,1,0:T(8,128)(2,1)S(1)}, u32[]{:S(2)}, u32[]{:S(2)}) collective-permute-start(bf16[1,1,272,1024]{3,2,1,0:T(8,128)(2,1)S(1)} %bitcast.70), channel_id=1, source_target_pairs={{0,32},{16,48},{32,0},{48,16},{64,96},{80,112},{96,64},{112,80},{1... | collective-permute-start | bytes 1671176 | tf_op jit(solution)/shard_map/ppermute | solution.py:256
  6.6 0.5 collective-permute-start.2
  7.1 1.5 %collective-permute-start.1 = (bf16[1,1,256,1024]{3,2,1,0:T(8,128)(2,1)}, bf16[1,1,256,1024]{3,2,1,0:T(8,128)(2,1)S(1)}, u32[]{:S(2)}, u32[]{:S(2)}) collective-permute-start(bf16[1,1,256,1024]{3,2,1,0:T(8,128)(2,1)} %bitcast.12), channel_id=1, source_target_pairs={{0,32},{16,48},{32,0},{48,16},{64,96},{80,112},{96,64},{112,80},{1... | collective-permute-start | bytes 1572872 | tf_op jit(solution)/shard_map/ppermute | solution.py:256
  8.6 2.4 %select_bitcast_fusion = bf16[2,512,1024]{2,1,0:T(8,128)(2,1)S(1)} fusion(bf16[2,2,512,1024]{3,2,1,0:T(8,128)(2,1)} %xraw_ref.1, pred[]{:T(512)S(6)} %eq.258), kind=kLoop, calls=%fused_computation.1 | loop fusion | flops 1048576 | bytes 6291457 | tf_op jit(solution)/shard_map/jit(_where)/select_n | solution.py:258
  11.1 1.5 %maximum_bitcast_fusion = bf16[1,2,528,1024]{3,2,1,0:T(8,128)(2,1)} fusion(bf16[2,16,1024]{2,1,0:T(8,128)(2,1)S(1)} %pad.18, bf16[2,512,1024]{2,1,0:T(8,128)(2,1)S(1)} %select_bitcast_fusion), kind=kLoop, calls=%fused_computation | loop fusion | flops 4325376 | bytes 4325376 | tf_op jit(solution)/shard_map/broadcast_in_dim | solution.py:258
  12.7 0.5 collective-permute-start.4
  13.2 0.2 rev.26
  13.4 0.3 slice_reduce_fusion
  13.6 0.5 compare_convert_fusion.7
  14.4 0.6 compare_convert_fusion.5
  15.0 0.7 broadcast_multiply_fusion.3
  15.8 0.6 compare_convert_fusion.8
  16.3 0.1 fusion.xperm_ref
  16.5 0.1 fusion.1.yperm_ref
  16.6 4.0 %collective-permute-done.3.chunk_ref.y00 = bf16[1,1,272,1024]{3,2,1,0:T(8,128)(2,1)S(1)} collective-permute-done((bf16[1,1,272,1024]{3,2,1,0:T(8,128)(2,1)S(1)}, bf16[1,1,272,1024]{3,2,1,0:T(8,128)(2,1)S(1)}, u32[]{:S(2)}, u32[]{:S(2)}) %collective-permute-start.3) | collective-permute-done | bytes 557088 | tf_op jit(solution)/shard_map/ppermute | solution.py:256
  20.6 2.2 %copy-done = bf16[2,2,512,1024]{3,2,1,0:T(8,128)(2,1)S(1)} copy-done((bf16[2,2,512,1024]{3,2,1,0:T(8,128)(2,1)S(1)}, bf16[2,2,512,1024]{3,2,1,0:T(8,128)(2,1)}, u32[]{:S(2)}) %copy-start) | copy-done | bytes 4194328
  22.8 13.7 %shard_map.46 = (f32[2,8,512]{2,1,0:T(8,128)S(1)}, bf16[1,1,272,1024]{3,2,1,0:T(8,128)(2,1)S(1)}) custom-call(bf16[1,1,272,1024]{3,2,1,0:T(8,128)(2,1)S(1)} %collective-permute-done.3.chunk_ref.y00, bf16[2,2,512,1024]{3,2,1,0:T(8,128)(2,1)S(1)} %copy-done, bf16[2,256,256]{2,1,0:T(8,128)(2,1)S(1)} %fusion.xperm_ref, bf16[2,256,256]{2,1,0:T(8,128)(2,1)S(1)} %fusion.1.yperm_ref), custom_call_target="tpu_custom_call" | custom-call | flops 12884901888 | bytes 16777216 | tf_op jit(solution)/shard_map/pallas_call | solution.py:131
  36.9 12.1 %shard_map.47.prev_ref.r01.y01 = bf16[1,1,256,1024]{3,2,1,0:T(8,128)(2,1)S(1)} custom-call(bf16[1,1,256,1024]{3,2,1,0:T(8,128)(2,1)S(1)} %collective-permute-done.2.chunk_ref.y01, bf16[1,1,272,1024]{3,2,1,0:T(8,128)(2,1)S(1)} %get-tuple-element.20.prev_ref.r00.y00), custom_call_target="tpu_custom_call" | custom-call | flops 12884901888 | bytes 16777216 | tf_op jit(solution)/shard_map/pallas_call | solution.py:131
  49.0 0.8 copy-done.1
  49.8 0.2 rev.27
  50.0 0.2 rev.28
  50.2 0.1 fusion.2.yperm_ref
  50.3 0.1 fusion.3.rperm_ref.yperm_ref
  50.5 1.0 copy-done.2
  51.5 13.3 %shard_map.48 = (f32[2,4,512]{2,1,0:T(4,128)S(1)}, bf16[1,1,256,1024]{3,2,1,0:T(8,128)(2,1)S(1)}) custom-call(bf16[1,1,256,1024]{3,2,1,0:T(8,128)(2,1)S(1)} %collective-permute-done.1.chunk_ref.y10, bf16[1,1,256,1024]{3,2,1,0:T(8,128)(2,1)S(1)} %copy-done.2, bf16[2,2,512,1024]{3,2,1,0:T(8,128)(2,1)} %xraw_ref.1, bf16[2,256,256]{2,1,0:T(8,128)(2,1)S(1)} %fusion.xperm_ref, ...), custom_call_target="tpu_custom_call" | custom-call | flops 12884901888 | bytes 16777216 | tf_op jit(solution)/shard_map/pallas_call | solution.py:131
  64.9 0.8 copy-done.4
  65.8 0.4 reverse
  66.5 1.3 %broadcast_multiply_fusion.4 = (f32[2,2,64,2]{2,1,0,3:T(2,128)}, f32[2,2,64,2]{2,1,0,3:T(2,128)}, f32[2,2,64,2]{2,1,0,3:T(2,128)}, f32[2,2,64,2]{2,1,0,3:T(2,128)}) fusion(f32[2,2,64]{2,1,0:T(2,128)S(1)} %compare_convert_fusion, f32[2]{0:T(128)} %compare_convert_fusion.7, f32[2,2,64]{2,1,0:T(2,128)S(1)} %compare_convert_fusion.2, ...), kind=kLoop, calls=%fused_computation.43 | loop fusion | flops 2048 | bytes 12296 | tf_op jit(solution)/shard_map/abg,f->abgf/dot_general | solution.py:324
  67.8 0.7 slice_reduce_fusion.6
  68.7 0.7 convert_reduce_fusion
  69.4 0.2 rev.30
  69.7 0.1 fusion.4.zperm_ref
  69.9 1.1 %copy-done.5 = bf16[1,1,256,1024]{3,2,1,0:T(8,128)(2,1)S(1)} copy-done((bf16[1,1,256,1024]{3,2,1,0:T(8,128)(2,1)S(1)}, bf16[1,1,256,1024]{3,2,1,0:T(8,128)(2,1)}, u32[]{:S(2)}) %copy-start.5) | copy-done | bytes 524312
  71.0 13.3 %shard_map.49 = (f32[1,4,512]{2,1,0:T(4,128)S(1)}, f32[1,8,512]{2,1,0:T(8,128)S(1)}, bf16[1,1,256,1024]{3,2,1,0:T(8,128)(2,1)S(1)}) custom-call(bf16[2,2,512,1024]{3,2,1,0:T(8,128)(2,1)} %xraw_ref.1, bf16[2,256,256]{2,1,0:T(8,128)(2,1)S(1)} %fusion.xperm_ref, bf16[1,1,256,1024]{3,2,1,0:T(8,128)(2,1)S(1)} %collective-permute-done.1.chunk_ref.y10, ...), custom_call_target="tpu_custom_call" | custom-call | flops 25769803776 | bytes 16777216 | tf_op jit(solution)/shard_map/pallas_call | solution.py:131
  84.4 0.8 copy-done.7
  85.2 1.0 copy-done.8
  86.3 3.8 %shard_map.50 = f32[1,4,512]{2,1,0:T(4,128)S(1)} custom-call(s32[1]{0:T(128)} %bitcast.30.sel_ref, bf16[2,2,512,1024]{3,2,1,0:T(8,128)(2,1)} %xraw_ref.1, bf16[2,256,256]{2,1,0:T(8,128)(2,1)S(1)} %fusion.xperm_ref, bf16[1,1,272,1024]{3,2,1,0:T(8,128)(2,1)S(1)} %get-tuple-element.20.prev_ref.r00.y00, bf16[1,1,256,1024]{3,2,1,0:T(8,128)(2,1)S(1)} %copy-done.3, ...), custom_call_target="tpu_custom_call" | custom-call | flops 2147483648 | bytes 4194304 | tf_op jit(solution)/shard_map/pallas_call | solution.py:167
  90.2 0.4 reverse.1
  90.7 0.4 reverse.2
  91.2 0.4 reverse.3
  92.2 0.6 convolution_multiply_fusion
  92.8 0.4 copy.36
  93.2 1.0 pad.19.clone
  94.2 11.3 %shard_map.51 = f32[8,2,2,512]{3,2,1,0:T(2,128)} custom-call(f32[8,8,2,2,512]{4,3,2,1,0:T(2,128)} %bitcast.69), custom_call_target="tpu_custom_call" | custom-call | tf_op jit(solution)/shard_map/pallas_call | solution.py:219
  105.5 1.5 %copy.41 = f32[8,2,2,511]{3,2,1,0:T(2,128)} copy(f32[8,2,2,511]{3,2,1,0:T(2,128)} %bitcast.71) | data formatting | bytes 130816
  (95 shorter events, 2.5 us)
Async XLA Ops:
  5.0 15.6 %collective-permute-start.3 = (bf16[1,1,272,1024]{3,2,1,0:T(8,128)(2,1)S(1)}, bf16[1,1,272,1024]{3,2,1,0:T(8,128)(2,1)S(1)}, u32[]{:S(2)}, u32[]{:S(2)}) collective-permute-start(bf16[1,1,272,1024]{3,2,1,0:T(8,128)(2,1)S(1)} %bitcast.70), channel_id=1, source_target_pairs={{0,32},{16,48},{32,0},{48,16},{64,96},{80,112},{96,64},{112,80},{1... | collective-permute-start | bytes 1671176 | tf_op jit(solution)/shard_map/ppermute | solution.py:256
  6.6 30.3 %collective-permute-start.2 = (bf16[1,1,256,1024]{3,2,1,0:T(8,128)(2,1)}, bf16[1,1,256,1024]{3,2,1,0:T(8,128)(2,1)S(1)}, u32[]{:S(2)}, u32[]{:S(2)}) collective-permute-start(bf16[1,1,256,1024]{3,2,1,0:T(8,128)(2,1)} %bitcast.13), channel_id=1, source_target_pairs={{0,32},{16,48},{32,0},{48,16},{64,96},{80,112},{96,64},{112,80},{1... | collective-permute-start | bytes 1572872 | tf_op jit(solution)/shard_map/ppermute | solution.py:256
  7.1 43.4 %collective-permute-start.1 = (bf16[1,1,256,1024]{3,2,1,0:T(8,128)(2,1)}, bf16[1,1,256,1024]{3,2,1,0:T(8,128)(2,1)S(1)}, u32[]{:S(2)}, u32[]{:S(2)}) collective-permute-start(bf16[1,1,256,1024]{3,2,1,0:T(8,128)(2,1)} %bitcast.12), channel_id=1, source_target_pairs={{0,32},{16,48},{32,0},{48,16},{64,96},{80,112},{96,64},{112,80},{1... | collective-permute-start | bytes 1572872 | tf_op jit(solution)/shard_map/ppermute | solution.py:256
  11.1 2.1 %copy-start.11 = (s32[2,256]{1,0:T(2,128)S(1)}, s32[2,256]{1,0:T(2,128)}, u32[]{:S(2)}) copy-start(s32[2,256]{1,0:T(2,128)} %param.5) | copy-start | bytes 6148
  11.1 2.3 %copy-start.9 = (s32[2,4,2]{1,2,0:T(2,128)S(1)}, s32[2,4,2]{1,2,0:T(2,128)}, u32[]{:S(2)}) copy-start(s32[2,4,2]{1,2,0:T(2,128)} %param.6) | copy-start | bytes 196
  12.6 55.2 %collective-permute-start = (bf16[1,2,528,1024]{3,2,1,0:T(8,128)(2,1)}, bf16[1,2,528,1024]{3,2,1,0:T(8,128)(2,1)}, u32[]{:S(2)}, u32[]{:S(2)}) collective-permute-start(bf16[1,2,528,1024]{3,2,1,0:T(8,128)(2,1)} %maximum_bitcast_fusion), channel_id=1, source_target_pairs={{0,16},{16,0},{32,48},{48,32},{64,80},{80,64},{96,112},{112,96},{1... | collective-permute-start | bytes 6488072 | tf_op jit(solution)/shard_map/ppermute | solution.py:257
  12.7 57.2 %collective-permute-start.4 = (bf16[1,1,256,1024]{3,2,1,0:T(8,128)(2,1)}, bf16[1,1,256,1024]{3,2,1,0:T(8,128)(2,1)S(1)}, u32[]{:S(2)}, u32[]{:S(2)}) collective-permute-start(bf16[1,1,256,1024]{3,2,1,0:T(8,128)(2,1)} %bitcast.29), channel_id=1, source_target_pairs={{0,32},{16,48},{32,0},{48,16},{64,96},{80,112},{96,64},{112,80},{1... | collective-permute-start | bytes 1572872 | tf_op jit(solution)/shard_map/ppermute | solution.py:256
  20.6 2.2 %copy-start = (bf16[2,2,512,1024]{3,2,1,0:T(8,128)(2,1)S(1)}, bf16[2,2,512,1024]{3,2,1,0:T(8,128)(2,1)}, u32[]{:S(2)}) copy-start(bf16[2,2,512,1024]{3,2,1,0:T(8,128)(2,1)} %xraw_ref.1) | copy-start | bytes 12582916
  49.0 0.8 copy-start.1
  50.5 1.0 copy-start.2
  64.9 0.8 copy-start.4
  69.9 15.3 %copy-start.3 = (bf16[1,1,256,1024]{3,2,1,0:T(8,128)(2,1)S(1)}, bf16[1,1,256,1024]{3,2,1,0:T(8,128)(2,1)}, u32[]{:S(2)}) copy-start(bf16[1,1,256,1024]{3,2,1,0:T(8,128)(2,1)} %copy-done.1) | copy-start | bytes 1572868
  69.9 1.1 %copy-start.5 = (bf16[1,1,256,1024]{3,2,1,0:T(8,128)(2,1)S(1)}, bf16[1,1,256,1024]{3,2,1,0:T(8,128)(2,1)}, u32[]{:S(2)}) copy-start(bf16[1,1,256,1024]{3,2,1,0:T(8,128)(2,1)} %copy-done.4) | copy-start | bytes 1572868
  71.0 14.2 %copy-start.6 = (bf16[1,1,256,1024]{3,2,1,0:T(8,128)(2,1)S(1)}, bf16[1,1,256,1024]{3,2,1,0:T(8,128)(2,1)}, u32[]{:S(2)}) copy-start(bf16[1,1,256,1024]{3,2,1,0:T(8,128)(2,1)} %copy-done.4) | copy-start | bytes 1572868
  84.3 0.8 copy-start.7
  85.2 1.0 copy-start.8
  86.2 3.9 %copy-start.17 = (f32[2]{0:T(128)S(1)}, f32[2]{0:T(128)}, u32[]{:S(2)}) copy-start(f32[2]{0:T(128)} %constant.23.clone) | copy-start | bytes 28
  86.2 5.7 %copy-start.16 = (f32[2,2,64]{2,1,0:T(2,128)S(1)}, f32[2,2,64]{2,1,0:T(2,128)}, u32[]{:S(2)}) copy-start(f32[2,2,64]{2,1,0:T(2,128)} %get-tuple-element.59) | copy-start | bytes 3076
  86.2 5.7 %copy-start.18 = (f32[2]{0:T(128)S(1)}, f32[2]{0:T(128)}, u32[]{:S(2)}) copy-start(f32[2]{0:T(128)} %compare_convert_fusion.8) | copy-start | bytes 28
  86.2 5.8 %copy-start.10 = (f32[2,2,2,2,64]{4,3,2,0,1:T(2,128)S(1)}, f32[2,2,2,2,64]{4,3,2,0,1:T(2,128)}, u32[]{:S(2)}) copy-start(f32[2,2,2,2,64]{4,3,2,0,1:T(2,128)} %broadcast_multiply_fusion.3) | copy-start | bytes 12292
  86.2 5.8 %copy-start.12 = (f32[2,2,64,2]{2,1,0,3:T(2,128)S(1)}, f32[2,2,64,2]{2,1,0,3:T(2,128)}, u32[]{:S(2)}) copy-start(f32[2,2,64,2]{2,1,0,3:T(2,128)} %get-tuple-element.45) | copy-start | bytes 6148
  86.2 5.8 %copy-start.13 = (f32[2,2,64,2]{2,1,0,3:T(2,128)S(1)}, f32[2,2,64,2]{2,1,0,3:T(2,128)}, u32[]{:S(2)}) copy-start(f32[2,2,64,2]{2,1,0,3:T(2,128)} %get-tuple-element.46) | copy-start | bytes 6148
  86.2 5.8 %copy-start.14 = (f32[2,2,64,2]{2,1,0,3:T(2,128)S(1)}, f32[2,2,64,2]{2,1,0,3:T(2,128)}, u32[]{:S(2)}) copy-start(f32[2,2,64,2]{2,1,0,3:T(2,128)} %get-tuple-element.47) | copy-start | bytes 6148
  86.3 5.8 %copy-start.15 = (f32[2,2,64,2]{2,1,0,3:T(2,128)S(1)}, f32[2,2,64,2]{2,1,0,3:T(2,128)}, u32[]{:S(2)}) copy-start(f32[2,2,64,2]{2,1,0,3:T(2,128)} %get-tuple-element.48) | copy-start | bytes 6148

commit v9 on v6

--- a/solution.py
+++ b/solution.py
@@ -103,17 +103,20 @@
     copy.wait()
 
 
-def relay_call(kernel, args, outs, n_lags, width, samples, collective_id):
+def relay_call(kernel, args, outs, n_lags, width, samples, collective_id, hbm_args=()):
     vmem = pl.BlockSpec(memory_space=pltpu.VMEM)
+    hbm = pl.BlockSpec(memory_space=pl.ANY)
+    out_specs = tuple(hbm for _ in outs)
     scratch = []
     if n_lags:
         outs = (jax.ShapeDtypeStruct((n_lags, 8, 2 * width), jnp.float32),) + outs
+        out_specs = (vmem,) + out_specs
         scratch = [pltpu.VMEM((2, 2, width, samples), jnp.bfloat16)] * 2
     return pl.pallas_call(
         kernel,
         out_shape=outs,
-        in_specs=[vmem] * len(args),
-        out_specs=tuple(vmem for _ in outs),
+        in_specs=[hbm if i in hbm_args else vmem for i in range(len(args))],
+        out_specs=out_specs,
         scratch_shapes=scratch + [pltpu.SemaphoreType.DMA(()), pltpu.SemaphoreType.DMA(())],
         compiler_params=pltpu.CompilerParams(
             collective_id=collective_id, has_side_effects=True, vmem_limit_bytes=48 * 1024 * 1024
@@ -255,10 +258,10 @@
 
     chunk_shape = lambda k: (jax.ShapeDtypeStruct(got1[k].shape, got1[k].dtype),)
     lag0, relay0 = relay_call(
-        relay_own_kernel, (got1[0], volts, perm, perm_rev), chunk_shape(0), channels, width, samples, 1
-    )
-    (relay1,) = relay_call(relay_only_kernel, (got1[1], relay0), chunk_shape(1), 0, width, samples, 2)
-    (relay2,) = relay_call(relay_only_kernel, (got1[2], relay1), chunk_shape(2), 0, width, samples, 3)
+        relay_own_kernel, (got1[0], volts, perm, perm_rev), chunk_shape(0), channels, width, samples, 1, (0,)
+    )
+    (relay1,) = relay_call(relay_only_kernel, (got1[1], relay0), chunk_shape(1), 0, width, samples, 2, (0, 1))
+    (relay2,) = relay_call(relay_only_kernel, (got1[2], relay1), chunk_shape(2), 0, width, samples, 3, (0, 1))
     relayed = [relay0, relay1, relay2]
     lag0 = lag0.reshape(channels, 2, 2, 2, 2 * width)
     center = (jnp.arange(2 * width) == width - 1)
@@ -280,7 +283,7 @@
     perm1, tg1 = meta_of(got1[0], width)
     perm0, tg0 = meta_of(got0, rows)
     lag10, relay_last = relay_call(
-        relay_kernel, (volts, perm, *got1, perm1, got0, perm0, relay2), chunk_shape(3), 2, width, samples, 4
+        relay_kernel, (volts, perm, *got1, perm1, got0, perm0, relay2), chunk_shape(3), 2, width, samples, 4, (9,)
     )
     perm2, tg2 = meta_of(relayed[0], width)
     lag2 = pair_lags(mine[2][None].astype(jnp.int32), volts, perm, relayed + [relay_last], perm2, False)

time: 103 us -> 103 us (level)
  no operation moved by 1% of the time
where the time goes in v9:
time: 103 us
  Pallas kernels  66.9 us (65%)
  local copies, waits for them, and re-layouts  15 us (15%)
  other arithmetic  9.61 us (9%)
  waiting for transfers between devices  6.22 us (6%)
  starting transfers between devices  4.16 us (4%)
    pallas_call x4, Pallas kernels, relay_call(): pl.pallas_call(kernel, out_shape=outs, in_specs=[hbm if i in hbm_args els...  50.3 us
    pallas_call x1, Pallas kernels, reduce_scatter(): pl.pallas_call(scatter_kernel, out_shape=jax.ShapeDtypeStruct(slab, jnp.f...  11.4 us
    unnamed x32, local copies, waits for them, and re-layouts  11.2 us
    ppermute x4, waiting for transfers between devices, on_device(): lax.ppermute(part, 'inp', [(i, i ^ 2) for i in range(n_inp)])  6.22 us
    pallas_call x1, Pallas kernels, pair_lags(): pl.pallas_call(lag_kernel, out_shape=jax.ShapeDtypeStruct((n, 8, 2 * widt...  5.17 us
    ppermute x4, starting transfers between devices, on_device(): lax.ppermute(part, 'inp', [(i, i ^ 2) for i in range(n_inp)])  4.05 us
    select_n x1, other arithmetic, chunks(): jnp.where(chan == 1, volts[1, c, blk * width:(blk + 1) * width], volts[0,...  3.35 us
    select_n x1, other arithmetic, on_device(): jnp.where(mine[0] == 0, volts[1], volts[0])  2.44 us
  transfers between devices with their start and end apart: 5, of which 1 were waited for; matrix products, arithmetic and copies ran while one was open for 9% of the time, Pallas kernels for 36%

profile of v9, /device:TPU:32, one launch (start us, length us, event | category | flops | bytes accessed | tf_op | source)
XLA Modules:
  0.0 102.9 jit_solution(1159688424726948025)
XLA Ops:
  0.0 0.8 copy.18
  0.9 0.7 copy.40
  1.6 3.4 %slice_select_fusion = (bf16[1,1,256,1024]{3,2,1,0:T(8,128)(2,1)}, bf16[1,1,256,1024]{3,2,1,0:T(8,128)(2,1)}, bf16[256,1024]{1,0:T(8,128)(2,1)S(1)}, bf16[1,1,256,1024]{3,2,1,0:T(8,128)(2,1)}) fusion(bf16[2,2,512,1024]{3,2,1,0:T(8,128)(2,1)} %xraw_ref.1, pred[]{:T(512)S(6)} %eq.271), kind=kLoop, calls=%fused_computation.7 | loop fusion | flops 1048576 | bytes 6291457 | tf_op jit(solution)/shard_map/jit(_where)/select_n | solution.py:231
  5.0 1.6 %collective-permute-start.1 = (bf16[1,1,272,1024]{3,2,1,0:T(8,128)(2,1)S(1)}, bf16[1,1,272,1024]{3,2,1,0:T(8,128)(2,1)S(1)}, u32[]{:S(2)}, u32[]{:S(2)}) collective-permute-start(bf16[1,1,272,1024]{3,2,1,0:T(8,128)(2,1)S(1)} %maximum_bitcast_fusion.1), channel_id=1, source_target_pairs={{0,32},{16,48},{32,0},{48,16},{64,96},{80,112},{96,64},{112,80},{1... | collective-permute-start | bytes 1671176 | tf_op jit(solution)/shard_map/ppermute | solution.py:239
  6.6 2.4 %select_bitcast_fusion = bf16[2,512,1024]{2,1,0:T(8,128)(2,1)S(1)} fusion(bf16[2,2,512,1024]{3,2,1,0:T(8,128)(2,1)} %xraw_ref.1, pred[]{:T(512)S(6)} %eq.258), kind=kLoop, calls=%fused_computation.1 | loop fusion | flops 1048576 | bytes 6291457 | tf_op jit(solution)/shard_map/jit(_where)/select_n | solution.py:241
  9.0 1.5 %maximum_bitcast_fusion = bf16[1,2,528,1024]{3,2,1,0:T(8,128)(2,1)} fusion(bf16[2,16,1024]{2,1,0:T(8,128)(2,1)S(1)} %pad.18, bf16[2,512,1024]{2,1,0:T(8,128)(2,1)S(1)} %select_bitcast_fusion), kind=kLoop, calls=%fused_computation | loop fusion | flops 4325376 | bytes 4325376 | tf_op jit(solution)/shard_map/broadcast_in_dim | solution.py:241
  10.6 0.1 collective-permute-start
  10.7 0.5 collective-permute-start.2
  11.1 1.6 %collective-permute-start.3 = (bf16[1,1,256,1024]{3,2,1,0:T(8,128)(2,1)}, bf16[1,1,256,1024]{3,2,1,0:T(8,128)(2,1)S(1)}, u32[]{:S(2)}, u32[]{:S(2)}) collective-permute-start(bf16[1,1,256,1024]{3,2,1,0:T(8,128)(2,1)} %get-tuple-element.18), channel_id=1, source_target_pairs={{0,32},{16,48},{32,0},{48,16},{64,96},{80,112},{96,64},{112,80},{1... | collective-permute-start | bytes 1572872 | tf_op jit(solution)/shard_map/ppermute | solution.py:239
  12.7 0.5 collective-permute-start.4
  13.2 0.2 rev.26
  13.3 0.3 slice_reduce_fusion
  13.7 0.1 copy.22
  14.1 0.1 fusion.xperm_ref
  14.2 0.1 fusion.1.yperm_ref
  14.4 6.2 %collective-permute-done.1.chunk_ref.y00 = bf16[1,1,272,1024]{3,2,1,0:T(8,128)(2,1)S(1)} collective-permute-done((bf16[1,1,272,1024]{3,2,1,0:T(8,128)(2,1)S(1)}, bf16[1,1,272,1024]{3,2,1,0:T(8,128)(2,1)S(1)}, u32[]{:S(2)}, u32[]{:S(2)}) %collective-permute-start.1) | collective-permute-done | bytes 557088 | tf_op jit(solution)/shard_map/ppermute | solution.py:239
  20.6 2.2 %copy-done = bf16[2,2,512,1024]{3,2,1,0:T(8,128)(2,1)S(1)} copy-done((bf16[2,2,512,1024]{3,2,1,0:T(8,128)(2,1)S(1)}, bf16[2,2,512,1024]{3,2,1,0:T(8,128)(2,1)}, u32[]{:S(2)}) %copy-start) | copy-done | bytes 4194328
  22.8 13.7 %shard_map.46 = (f32[2,8,512]{2,1,0:T(8,128)S(1)}, bf16[1,1,272,1024]{3,2,1,0:T(8,128)(2,1)S(1)}) custom-call(bf16[1,1,272,1024]{3,2,1,0:T(8,128)(2,1)S(1)} %collective-permute-done.1.chunk_ref.y00, bf16[2,2,512,1024]{3,2,1,0:T(8,128)(2,1)S(1)} %copy-done, bf16[2,256,256]{2,1,0:T(8,128)(2,1)S(1)} %fusion.xperm_ref, bf16[2,256,256]{2,1,0:T(8,128)(2,1)S(1)} %fusion.1.yperm_ref), custom_call_target="tpu_custom_call" | custom-call | flops 25769803776 | bytes 16777216 | tf_op jit(solution)/shard_map/pallas_call | solution.py:115
  36.5 0.1 convert_element_type.92
  36.6 12.1 %shard_map.47.prev_ref.y01 = bf16[1,1,256,1024]{3,2,1,0:T(8,128)(2,1)S(1)} custom-call(bf16[1,1,256,1024]{3,2,1,0:T(8,128)(2,1)S(1)} %collective-permute-done.2.chunk_ref.y01, bf16[1,1,272,1024]{3,2,1,0:T(8,128)(2,1)S(1)} %get-tuple-element.9.prev_ref.y00), custom_call_target="tpu_custom_call" | custom-call | flops 12884901888 | bytes 16777216 | tf_op jit(solution)/shard_map/pallas_call | solution.py:115
  48.7 0.8 copy-done.1
  49.5 0.1 copy.21
  49.7 0.2 rev.32
  49.9 0.4 reverse
  50.3 0.1 slice.171
  50.5 0.1 fusion.4.yperm_ref
  50.7 1.0 %copy-done.2 = bf16[1,1,256,1024]{3,2,1,0:T(8,128)(2,1)S(1)} copy-done((bf16[1,1,256,1024]{3,2,1,0:T(8,128)(2,1)S(1)}, bf16[1,1,256,1024]{3,2,1,0:T(8,128)(2,1)}, u32[]{:S(2)}) %copy-start.2) | copy-done | bytes 524312
  51.7 11.1 %shard_map.48.prev_ref.y10 = bf16[1,1,256,1024]{3,2,1,0:T(8,128)(2,1)S(1)} custom-call(bf16[1,1,256,1024]{3,2,1,0:T(8,128)(2,1)S(1)} %collective-permute-done.3.chunk_ref.y10, bf16[1,1,256,1024]{3,2,1,0:T(8,128)(2,1)S(1)} %copy-done.2), custom_call_target="tpu_custom_call" | custom-call | flops 12884901888 | bytes 16777216 | tf_op jit(solution)/shard_map/pallas_call | solution.py:115
  62.9 0.8 copy-done.4
  63.7 0.7 slice_reduce_fusion.4
  64.5 0.1 copy.20
  64.7 0.1 copy.19
  64.9 0.7 fusion.8
  65.6 0.2 rev.28
  65.9 0.2 rev.29
  66.1 0.1 fusion.2.yperm_ref
  66.2 0.1 fusion.3.zperm_ref
  66.4 1.1 %copy-done.5 = bf16[1,1,256,1024]{3,2,1,0:T(8,128)(2,1)S(1)} copy-done((bf16[1,1,256,1024]{3,2,1,0:T(8,128)(2,1)S(1)}, bf16[1,1,256,1024]{3,2,1,0:T(8,128)(2,1)}, u32[]{:S(2)}) %copy-start.5) | copy-done | bytes 524312
  67.5 13.3 %shard_map.49 = (f32[2,8,512]{2,1,0:T(8,128)S(1)}, bf16[1,1,256,1024]{3,2,1,0:T(8,128)(2,1)S(1)}) custom-call(bf16[2,2,512,1024]{3,2,1,0:T(8,128)(2,1)} %xraw_ref.1, bf16[2,256,256]{2,1,0:T(8,128)(2,1)S(1)} %fusion.xperm_ref, bf16[1,1,272,1024]{3,2,1,0:T(8,128)(2,1)S(1)} %collective-permute-done.1.chunk_ref.y00, ...), custom_call_target="tpu_custom_call" | custom-call | flops 25769803776 | bytes 16777216 | tf_op jit(solution)/shard_map/pallas_call | solution.py:115
  80.9 5.2 %shard_map.50 = f32[1,8,512]{2,1,0:T(8,128)S(1)} custom-call(s32[1]{0:T(128)} %bitcast.28.sel_ref, bf16[2,2,512,1024]{3,2,1,0:T(8,128)(2,1)} %xraw_ref.1, bf16[2,256,256]{2,1,0:T(8,128)(2,1)S(1)} %fusion.xperm_ref, bf16[1,1,272,1024]{3,2,1,0:T(8,128)(2,1)S(1)} %get-tuple-element.9.prev_ref.y00, bf16[1,1,256,1024]{3,2,1,0:T(8,128)(2,1)S(1)} %copy-done.3, ...), custom_call_target="tpu_custom_call" | custom-call | flops 3221225472 | bytes 4194304 | tf_op jit(solution)/shard_map/pallas_call | solution.py:150
  86.2 0.4 reverse.1
  86.7 0.4 reverse.2
  87.2 0.4 reverse.3
  88.0 0.6 convolution_multiply_fusion
  88.6 0.4 copy.39
  89.0 1.0 pad.19.clone
  90.0 11.4 %shard_map.51 = f32[8,2,2,512]{3,2,1,0:T(2,128)} custom-call(f32[8,8,2,2,512]{4,3,2,1,0:T(2,128)} %bitcast.55), custom_call_target="tpu_custom_call" | custom-call | tf_op jit(solution)/shard_map/pallas_call | solution.py:202
  101.5 1.5 %copy.42 = f32[8,2,2,511]{3,2,1,0:T(2,128)} copy(f32[8,2,2,511]{3,2,1,0:T(2,128)} %bitcast.56) | data formatting | bytes 130816
  (69 shorter events, 1.8 us)
Async XLA Ops:
  5.0 15.6 %collective-permute-start.1 = (bf16[1,1,272,1024]{3,2,1,0:T(8,128)(2,1)S(1)}, bf16[1,1,272,1024]{3,2,1,0:T(8,128)(2,1)S(1)}, u32[]{:S(2)}, u32[]{:S(2)}) collective-permute-start(bf16[1,1,272,1024]{3,2,1,0:T(8,128)(2,1)S(1)} %maximum_bitcast_fusion.1), channel_id=1, source_target_pairs={{0,32},{16,48},{32,0},{48,16},{64,96},{80,112},{96,64},{112,80},{1... | collective-permute-start | bytes 1671176 | tf_op jit(solution)/shard_map/ppermute | solution.py:239
  9.0 4.1 %copy-start.8 = (s32[2,256]{1,0:T(2,128)S(1)}, s32[2,256]{1,0:T(2,128)}, u32[]{:S(2)}) copy-start(s32[2,256]{1,0:T(2,128)} %param.5) | copy-start | bytes 6148
  9.0 4.3 %copy-start.7 = (s32[2,4,2]{1,2,0:T(2,128)S(1)}, s32[2,4,2]{1,2,0:T(2,128)}, u32[]{:S(2)}) copy-start(s32[2,4,2]{1,2,0:T(2,128)} %param.6) | copy-start | bytes 196
  10.6 53.1 %collective-permute-start = (bf16[1,2,528,1024]{3,2,1,0:T(8,128)(2,1)}, bf16[1,2,528,1024]{3,2,1,0:T(8,128)(2,1)}, u32[]{:S(2)}, u32[]{:S(2)}) collective-permute-start(bf16[1,2,528,1024]{3,2,1,0:T(8,128)(2,1)} %maximum_bitcast_fusion), channel_id=1, source_target_pairs={{0,16},{16,0},{32,48},{48,32},{64,80},{80,64},{96,112},{112,96},{1... | collective-permute-start | bytes 6488072 | tf_op jit(solution)/shard_map/ppermute | solution.py:240
  10.7 25.9 %collective-permute-start.2 = (bf16[1,1,256,1024]{3,2,1,0:T(8,128)(2,1)}, bf16[1,1,256,1024]{3,2,1,0:T(8,128)(2,1)S(1)}, u32[]{:S(2)}, u32[]{:S(2)}) collective-permute-start(bf16[1,1,256,1024]{3,2,1,0:T(8,128)(2,1)} %get-tuple-element.20), channel_id=1, source_target_pairs={{0,32},{16,48},{32,0},{48,16},{64,96},{80,112},{96,64},{112,80},{1... | collective-permute-start | bytes 1572872 | tf_op jit(solution)/shard_map/ppermute | solution.py:239
  11.1 39.5 %collective-permute-start.3 = (bf16[1,1,256,1024]{3,2,1,0:T(8,128)(2,1)}, bf16[1,1,256,1024]{3,2,1,0:T(8,128)(2,1)S(1)}, u32[]{:S(2)}, u32[]{:S(2)}) collective-permute-start(bf16[1,1,256,1024]{3,2,1,0:T(8,128)(2,1)} %get-tuple-element.18), channel_id=1, source_target_pairs={{0,32},{16,48},{32,0},{48,16},{64,96},{80,112},{96,64},{112,80},{1... | collective-permute-start | bytes 1572872 | tf_op jit(solution)/shard_map/ppermute | solution.py:239
  12.7 53.7 %collective-permute-start.4 = (bf16[1,1,256,1024]{3,2,1,0:T(8,128)(2,1)}, bf16[1,1,256,1024]{3,2,1,0:T(8,128)(2,1)S(1)}, u32[]{:S(2)}, u32[]{:S(2)}) collective-permute-start(bf16[1,1,256,1024]{3,2,1,0:T(8,128)(2,1)} %get-tuple-element.17), channel_id=1, source_target_pairs={{0,32},{16,48},{32,0},{48,16},{64,96},{80,112},{96,64},{112,80},{1... | collective-permute-start | bytes 1572872 | tf_op jit(solution)/shard_map/ppermute | solution.py:239
  20.6 2.2 %copy-start = (bf16[2,2,512,1024]{3,2,1,0:T(8,128)(2,1)S(1)}, bf16[2,2,512,1024]{3,2,1,0:T(8,128)(2,1)}, u32[]{:S(2)}) copy-start(bf16[2,2,512,1024]{3,2,1,0:T(8,128)(2,1)} %xraw_ref.1) | copy-start | bytes 12582916
  48.7 0.8 copy-start.1
  50.7 1.0 %copy-start.2 = (bf16[1,1,256,1024]{3,2,1,0:T(8,128)(2,1)S(1)}, bf16[1,1,256,1024]{3,2,1,0:T(8,128)(2,1)}, u32[]{:S(2)}) copy-start(bf16[1,1,256,1024]{3,2,1,0:T(8,128)(2,1)} %copy-done.1) | copy-start | bytes 1572868
  62.9 0.8 copy-start.4
  66.4 14.5 %copy-start.3 = (bf16[1,1,256,1024]{3,2,1,0:T(8,128)(2,1)S(1)}, bf16[1,1,256,1024]{3,2,1,0:T(8,128)(2,1)}, u32[]{:S(2)}) copy-start(bf16[1,1,256,1024]{3,2,1,0:T(8,128)(2,1)} %copy-done.1) | copy-start | bytes 1572868
  66.4 1.1 %copy-start.5 = (bf16[1,1,256,1024]{3,2,1,0:T(8,128)(2,1)S(1)}, bf16[1,1,256,1024]{3,2,1,0:T(8,128)(2,1)}, u32[]{:S(2)}) copy-start(bf16[1,1,256,1024]{3,2,1,0:T(8,128)(2,1)} %copy-done.4) | copy-start | bytes 1572868
  67.5 13.4 %copy-start.6 = (bf16[1,1,256,1024]{3,2,1,0:T(8,128)(2,1)S(1)}, bf16[1,1,256,1024]{3,2,1,0:T(8,128)(2,1)}, u32[]{:S(2)}) copy-start(bf16[1,1,256,1024]{3,2,1,0:T(8,128)(2,1)} %copy-done.4) | copy-start | bytes 1572868
  80.9 5.3 %copy-start.9 = (f32[2]{0:T(128)S(1)}, f32[2]{0:T(128)}, u32[]{:S(2)}) copy-start(f32[2]{0:T(128)} %constant.23.clone) | copy-start | bytes 28

commit v10 on v9

--- a/solution.py
+++ b/solution.py
@@ -267,12 +267,15 @@
     center = (jnp.arange(2 * width) == width - 1)
     same = jnp.eye(2, dtype=bool)
     lag0 = jnp.where(same[None, :, :, None, None] & center[None, None, None, None, :], 0.0, lag0)
+    def flip_lags(lag):
+        return jnp.concatenate([jnp.flip(lag[..., :diffs], axis=-1), jnp.zeros_like(lag[..., diffs:])], axis=-1)
+
     contrib_w = []
     contrib_v = []
     w0 = (tile_group[:, 0, :, None] == group_ids).astype(jnp.float32)
     f0 = (chan_ids[:, None] == chan_ids[None, :]).astype(jnp.float32)
     contrib_w.append(jnp.einsum("abg,fh->fabgh", w0, f0).reshape(-1, groups_all, channels))
-    contrib_v.append(jnp.flip(lag0[..., :diffs], axis=-1).reshape(-1, 2, diffs))
+    contrib_v.append(flip_lags(lag0).reshape(-1, 2, 2 * width))
     sign = jnp.array([1.0, -1.0], jnp.float32)
 
     def meta_of(slab, row):
@@ -290,19 +293,18 @@
     level_lags = {0: (lag10[1], tg0), 1: (lag10[0], tg1), 2: (lag2[0], tg2)}
     for bit in range(levels):
         lag, got_tg = level_lags[bit]
-        lag = lag.reshape(2, 2, 2, 2 * width)[..., :diffs]
+        lag = lag.reshape(2, 2, 2, 2 * width)
         fmask = (chan_ids == mine[bit]).astype(jnp.float32)
         w_direct = (tile_group[:, bit + 1, :, None] == group_ids).astype(jnp.float32)
         w_trans = jnp.swapaxes((got_tg[:, bit + 1, :, None] == group_ids).astype(jnp.float32), 0, 1)
         contrib_w.append(jnp.einsum("abg,f->abgf", w_direct, fmask).reshape(-1, groups_all, channels))
-        contrib_v.append(jnp.flip(lag, axis=-1).reshape(-1, 2, diffs))
+        contrib_v.append(flip_lags(lag).reshape(-1, 2, 2 * width))
         contrib_w.append(jnp.einsum("abg,f->abgf", w_trans, fmask).reshape(-1, groups_all, channels))
-        contrib_v.append((lag * sign[:, None]).reshape(-1, 2, diffs))
+        contrib_v.append((lag * sign[:, None]).reshape(-1, 2, 2 * width))
     dense = jnp.einsum(
         "ngf,nck->gfck", jnp.concatenate(contrib_w), jnp.concatenate(contrib_v), precision=HIGH
     )
     dense = dense * (1.0 / samples)
-    dense = jnp.pad(dense, [(0, 0)] * 3 + [(0, 1)])
     dense = dense.reshape((n_inp, RG_DEV) + dense.shape[1:])
     return reduce_scatter(dense)[..., :diffs]
 

time: 103 us -> 103 us (level)
    mul x0 -> x1, local copies, waits for them, and re-layouts: none -> 1.19 us  [on_device(): dense = dense * (1.0 / samples)]
    unnamed x32 -> x31, local copies, waits for them, and re-layouts: 11.2 us -> 10.7 us
  transfers between devices with their start and end apart: 5 -> 5, of which waited for: 1 -> 1; matrix products, arithmetic and copies ran while one was open for 9% -> 8% of each run, Pallas kernels for 36% -> 36%
where the time goes in v10:
time: 103 us
  Pallas kernels  66.9 us (65%)
  local copies, waits for them, and re-layouts  14.9 us (14%)
  other arithmetic  9.59 us (9%)
  waiting for transfers between devices  6.22 us (6%)
  starting transfers between devices  4.16 us (4%)
    pallas_call x4, Pallas kernels, relay_call(): pl.pallas_call(kernel, out_shape=outs, in_specs=[hbm if i in hbm_args els...  50.3 us
    pallas_call x1, Pallas kernels, reduce_scatter(): pl.pallas_call(scatter_kernel, out_shape=jax.ShapeDtypeStruct(slab, jnp.f...  11.4 us
    unnamed x31, local copies, waits for them, and re-layouts  10.7 us
    ppermute x4, waiting for transfers between devices, on_device(): lax.ppermute(part, 'inp', [(i, i ^ 2) for i in range(n_inp)])  6.22 us
    pallas_call x1, Pallas kernels, pair_lags(): pl.pallas_call(lag_kernel, out_shape=jax.ShapeDtypeStruct((n, 8, 2 * widt...  5.17 us
    ppermute x4, starting transfers between devices, on_device(): lax.ppermute(part, 'inp', [(i, i ^ 2) for i in range(n_inp)])  4.05 us
    select_n x1, other arithmetic, chunks(): jnp.where(chan == 1, volts[1, c, blk * width:(blk + 1) * width], volts[0,...  3.35 us
    select_n x1, other arithmetic, on_device(): jnp.where(mine[0] == 0, volts[1], volts[0])  2.44 us
  transfers between devices with their start and end apart: 5, of which 1 were waited for; matrix products, arithmetic and copies ran while one was open for 8% of the time, Pallas kernels for 36%

profile of v10, /device:TPU:32, one launch (start us, length us, event | category | flops | bytes accessed | tf_op | source)
XLA Modules:
  0.0 102.8 jit_solution(4852470752062211712)
XLA Ops:
  0.0 0.8 copy.18
  0.9 0.7 copy.36
  1.6 3.4 %slice_select_fusion = (bf16[1,1,256,1024]{3,2,1,0:T(8,128)(2,1)}, bf16[1,1,256,1024]{3,2,1,0:T(8,128)(2,1)}, bf16[256,1024]{1,0:T(8,128)(2,1)S(1)}, bf16[1,1,256,1024]{3,2,1,0:T(8,128)(2,1)}) fusion(bf16[2,2,512,1024]{3,2,1,0:T(8,128)(2,1)} %xraw_ref.1, pred[]{:T(512)S(6)} %eq.271), kind=kLoop, calls=%fused_computation.7 | loop fusion | flops 1048576 | bytes 6291457 | tf_op jit(solution)/shard_map/jit(_where)/select_n | solution.py:231
  5.0 1.6 %collective-permute-start.1 = (bf16[1,1,272,1024]{3,2,1,0:T(8,128)(2,1)S(1)}, bf16[1,1,272,1024]{3,2,1,0:T(8,128)(2,1)S(1)}, u32[]{:S(2)}, u32[]{:S(2)}) collective-permute-start(bf16[1,1,272,1024]{3,2,1,0:T(8,128)(2,1)S(1)} %maximum_bitcast_fusion.1), channel_id=1, source_target_pairs={{0,32},{16,48},{32,0},{48,16},{64,96},{80,112},{96,64},{112,80},{1... | collective-permute-start | bytes 1671176 | tf_op jit(solution)/shard_map/ppermute | solution.py:239
  6.6 2.4 %select_bitcast_fusion = bf16[2,512,1024]{2,1,0:T(8,128)(2,1)S(1)} fusion(bf16[2,2,512,1024]{3,2,1,0:T(8,128)(2,1)} %xraw_ref.1, pred[]{:T(512)S(6)} %eq.258), kind=kLoop, calls=%fused_computation.1 | loop fusion | flops 1048576 | bytes 6291457 | tf_op jit(solution)/shard_map/jit(_where)/select_n | solution.py:241
  9.0 1.5 %maximum_bitcast_fusion = bf16[1,2,528,1024]{3,2,1,0:T(8,128)(2,1)} fusion(bf16[2,16,1024]{2,1,0:T(8,128)(2,1)S(1)} %pad.18, bf16[2,512,1024]{2,1,0:T(8,128)(2,1)S(1)} %select_bitcast_fusion), kind=kLoop, calls=%fused_computation | loop fusion | flops 4325376 | bytes 4325376 | tf_op jit(solution)/shard_map/broadcast_in_dim | solution.py:241
  10.6 0.1 collective-permute-start
  10.7 0.5 collective-permute-start.2
  11.1 1.6 %collective-permute-start.3 = (bf16[1,1,256,1024]{3,2,1,0:T(8,128)(2,1)}, bf16[1,1,256,1024]{3,2,1,0:T(8,128)(2,1)S(1)}, u32[]{:S(2)}, u32[]{:S(2)}) collective-permute-start(bf16[1,1,256,1024]{3,2,1,0:T(8,128)(2,1)} %get-tuple-element.18), channel_id=1, source_target_pairs={{0,32},{16,48},{32,0},{48,16},{64,96},{80,112},{96,64},{112,80},{1... | collective-permute-start | bytes 1572872 | tf_op jit(solution)/shard_map/ppermute | solution.py:239
  12.7 0.5 collective-permute-start.4
  13.2 0.2 rev.26
  13.3 0.3 slice_reduce_fusion
  13.7 0.1 copy.22
  14.1 0.1 fusion.xperm_ref
  14.2 0.1 fusion.1.yperm_ref
  14.4 6.2 %collective-permute-done.1.chunk_ref.y00 = bf16[1,1,272,1024]{3,2,1,0:T(8,128)(2,1)S(1)} collective-permute-done((bf16[1,1,272,1024]{3,2,1,0:T(8,128)(2,1)S(1)}, bf16[1,1,272,1024]{3,2,1,0:T(8,128)(2,1)S(1)}, u32[]{:S(2)}, u32[]{:S(2)}) %collective-permute-start.1) | collective-permute-done | bytes 557088 | tf_op jit(solution)/shard_map/ppermute | solution.py:239
  20.6 2.2 %copy-done = bf16[2,2,512,1024]{3,2,1,0:T(8,128)(2,1)S(1)} copy-done((bf16[2,2,512,1024]{3,2,1,0:T(8,128)(2,1)S(1)}, bf16[2,2,512,1024]{3,2,1,0:T(8,128)(2,1)}, u32[]{:S(2)}) %copy-start) | copy-done | bytes 4194328
  22.8 13.7 %shard_map.46 = (f32[2,8,512]{2,1,0:T(8,128)S(1)}, bf16[1,1,272,1024]{3,2,1,0:T(8,128)(2,1)S(1)}) custom-call(bf16[1,1,272,1024]{3,2,1,0:T(8,128)(2,1)S(1)} %collective-permute-done.1.chunk_ref.y00, bf16[2,2,512,1024]{3,2,1,0:T(8,128)(2,1)S(1)} %copy-done, bf16[2,256,256]{2,1,0:T(8,128)(2,1)S(1)} %fusion.xperm_ref, bf16[2,256,256]{2,1,0:T(8,128)(2,1)S(1)} %fusion.1.yperm_ref), custom_call_target="tpu_custom_call" | custom-call | flops 25769803776 | bytes 16777216 | tf_op jit(solution)/shard_map/pallas_call | solution.py:115
  36.5 0.1 convert_element_type.90
  36.6 12.1 %shard_map.47.prev_ref.y01 = bf16[1,1,256,1024]{3,2,1,0:T(8,128)(2,1)S(1)} custom-call(bf16[1,1,256,1024]{3,2,1,0:T(8,128)(2,1)S(1)} %collective-permute-done.2.chunk_ref.y01, bf16[1,1,272,1024]{3,2,1,0:T(8,128)(2,1)S(1)} %get-tuple-element.9.prev_ref.y00), custom_call_target="tpu_custom_call" | custom-call | flops 12884901888 | bytes 16777216 | tf_op jit(solution)/shard_map/pallas_call | solution.py:115
  48.7 0.8 copy-done.1
  49.5 0.1 copy.21
  49.7 0.2 rev.32
  49.9 0.4 reverse
  50.3 0.1 slice.168
  50.5 0.1 fusion.4.yperm_ref
  50.7 1.0 %copy-done.2 = bf16[1,1,256,1024]{3,2,1,0:T(8,128)(2,1)S(1)} copy-done((bf16[1,1,256,1024]{3,2,1,0:T(8,128)(2,1)S(1)}, bf16[1,1,256,1024]{3,2,1,0:T(8,128)(2,1)}, u32[]{:S(2)}) %copy-start.2) | copy-done | bytes 524312
  51.7 11.1 %shard_map.48.prev_ref.y10 = bf16[1,1,256,1024]{3,2,1,0:T(8,128)(2,1)S(1)} custom-call(bf16[1,1,256,1024]{3,2,1,0:T(8,128)(2,1)S(1)} %collective-permute-done.3.chunk_ref.y10, bf16[1,1,256,1024]{3,2,1,0:T(8,128)(2,1)S(1)} %copy-done.2), custom_call_target="tpu_custom_call" | custom-call | flops 12884901888 | bytes 16777216 | tf_op jit(solution)/shard_map/pallas_call | solution.py:115
  62.9 0.8 copy-done.4
  63.7 0.7 fusion.8
  64.4 0.2 rev.28
  64.6 0.2 rev.29
  64.9 0.1 fusion.2.yperm_ref
  65.0 0.1 fusion.3.zperm_ref
  65.2 1.1 %copy-done.5 = bf16[1,1,256,1024]{3,2,1,0:T(8,128)(2,1)S(1)} copy-done((bf16[1,1,256,1024]{3,2,1,0:T(8,128)(2,1)S(1)}, bf16[1,1,256,1024]{3,2,1,0:T(8,128)(2,1)}, u32[]{:S(2)}) %copy-start.5) | copy-done | bytes 524312
  66.3 13.3 %shard_map.49 = (f32[2,8,512]{2,1,0:T(8,128)S(1)}, bf16[1,1,256,1024]{3,2,1,0:T(8,128)(2,1)S(1)}) custom-call(bf16[2,2,512,1024]{3,2,1,0:T(8,128)(2,1)} %xraw_ref.1, bf16[2,256,256]{2,1,0:T(8,128)(2,1)S(1)} %fusion.xperm_ref, bf16[1,1,272,1024]{3,2,1,0:T(8,128)(2,1)S(1)} %collective-permute-done.1.chunk_ref.y00, ...), custom_call_target="tpu_custom_call" | custom-call | flops 25769803776 | bytes 16777216 | tf_op jit(solution)/shard_map/pallas_call | solution.py:115
  79.7 5.2 %shard_map.50 = f32[1,8,512]{2,1,0:T(8,128)S(1)} custom-call(s32[1]{0:T(128)} %bitcast.26.sel_ref, bf16[2,2,512,1024]{3,2,1,0:T(8,128)(2,1)} %xraw_ref.1, bf16[2,256,256]{2,1,0:T(8,128)(2,1)S(1)} %fusion.xperm_ref, bf16[1,1,272,1024]{3,2,1,0:T(8,128)(2,1)S(1)} %get-tuple-element.9.prev_ref.y00, bf16[1,1,256,1024]{3,2,1,0:T(8,128)(2,1)S(1)} %copy-done.3, ...), custom_call_target="tpu_custom_call" | custom-call | flops 3221225472 | bytes 4194304 | tf_op jit(solution)/shard_map/pallas_call | solution.py:150
  85.0 0.7 slice_reduce_fusion.4
  85.7 0.1 convert_element_type.87
  85.8 0.1 copy.20
  86.0 0.1 copy.19
  86.2 0.4 reverse.3
  86.7 0.4 reverse.1
  87.2 0.4 reverse.2
  88.1 0.6 convolution_multiply_fusion
  88.7 1.2 %copy.30 = f32[64,2,2,512]{3,2,1,0:T(2,128)} copy(f32[64,2,2,512]{3,0,2,1:T(8,128)S(1)} %convolution_multiply_fusion) | data formatting | bytes 1048576 | tf_op jit(solution)/shard_map/mul | solution.py:307
  89.9 11.4 %shard_map.51 = f32[8,2,2,512]{3,2,1,0:T(2,128)} custom-call(f32[8,8,2,2,512]{4,3,2,1,0:T(2,128)} %bitcast.55), custom_call_target="tpu_custom_call" | custom-call | tf_op jit(solution)/shard_map/pallas_call | solution.py:202
  101.3 1.5 %copy.41 = f32[8,2,2,511]{3,2,1,0:T(2,128)} copy(f32[8,2,2,511]{3,2,1,0:T(2,128)} %bitcast.56) | data formatting | bytes 130816
  (72 shorter events, 1.8 us)
Async XLA Ops:
  5.0 15.6 %collective-permute-start.1 = (bf16[1,1,272,1024]{3,2,1,0:T(8,128)(2,1)S(1)}, bf16[1,1,272,1024]{3,2,1,0:T(8,128)(2,1)S(1)}, u32[]{:S(2)}, u32[]{:S(2)}) collective-permute-start(bf16[1,1,272,1024]{3,2,1,0:T(8,128)(2,1)S(1)} %maximum_bitcast_fusion.1), channel_id=1, source_target_pairs={{0,32},{16,48},{32,0},{48,16},{64,96},{80,112},{96,64},{112,80},{1... | collective-permute-start | bytes 1671176 | tf_op jit(solution)/shard_map/ppermute | solution.py:239
  9.0 4.1 %copy-start.8 = (s32[2,256]{1,0:T(2,128)S(1)}, s32[2,256]{1,0:T(2,128)}, u32[]{:S(2)}) copy-start(s32[2,256]{1,0:T(2,128)} %param.5) | copy-start | bytes 6148
  9.0 4.3 %copy-start.7 = (s32[2,4,2]{1,2,0:T(2,128)S(1)}, s32[2,4,2]{1,2,0:T(2,128)}, u32[]{:S(2)}) copy-start(s32[2,4,2]{1,2,0:T(2,128)} %param.6) | copy-start | bytes 196
  10.6 53.1 %collective-permute-start = (bf16[1,2,528,1024]{3,2,1,0:T(8,128)(2,1)}, bf16[1,2,528,1024]{3,2,1,0:T(8,128)(2,1)}, u32[]{:S(2)}, u32[]{:S(2)}) collective-permute-start(bf16[1,2,528,1024]{3,2,1,0:T(8,128)(2,1)} %maximum_bitcast_fusion), channel_id=1, source_target_pairs={{0,16},{16,0},{32,48},{48,32},{64,80},{80,64},{96,112},{112,96},{1... | collective-permute-start | bytes 6488072 | tf_op jit(solution)/shard_map/ppermute | solution.py:240
  10.7 25.9 %collective-permute-start.2 = (bf16[1,1,256,1024]{3,2,1,0:T(8,128)(2,1)}, bf16[1,1,256,1024]{3,2,1,0:T(8,128)(2,1)S(1)}, u32[]{:S(2)}, u32[]{:S(2)}) collective-permute-start(bf16[1,1,256,1024]{3,2,1,0:T(8,128)(2,1)} %get-tuple-element.20), channel_id=1, source_target_pairs={{0,32},{16,48},{32,0},{48,16},{64,96},{80,112},{96,64},{112,80},{1... | collective-permute-start | bytes 1572872 | tf_op jit(solution)/shard_map/ppermute | solution.py:239
  11.1 39.6 %collective-permute-start.3 = (bf16[1,1,256,1024]{3,2,1,0:T(8,128)(2,1)}, bf16[1,1,256,1024]{3,2,1,0:T(8,128)(2,1)S(1)}, u32[]{:S(2)}, u32[]{:S(2)}) collective-permute-start(bf16[1,1,256,1024]{3,2,1,0:T(8,128)(2,1)} %get-tuple-element.18), channel_id=1, source_target_pairs={{0,32},{16,48},{32,0},{48,16},{64,96},{80,112},{96,64},{112,80},{1... | collective-permute-start | bytes 1572872 | tf_op jit(solution)/shard_map/ppermute | solution.py:239
  12.7 52.5 %collective-permute-start.4 = (bf16[1,1,256,1024]{3,2,1,0:T(8,128)(2,1)}, bf16[1,1,256,1024]{3,2,1,0:T(8,128)(2,1)S(1)}, u32[]{:S(2)}, u32[]{:S(2)}) collective-permute-start(bf16[1,1,256,1024]{3,2,1,0:T(8,128)(2,1)} %get-tuple-element.17), channel_id=1, source_target_pairs={{0,32},{16,48},{32,0},{48,16},{64,96},{80,112},{96,64},{112,80},{1... | collective-permute-start | bytes 1572872 | tf_op jit(solution)/shard_map/ppermute | solution.py:239
  20.6 2.2 %copy-start = (bf16[2,2,512,1024]{3,2,1,0:T(8,128)(2,1)S(1)}, bf16[2,2,512,1024]{3,2,1,0:T(8,128)(2,1)}, u32[]{:S(2)}) copy-start(bf16[2,2,512,1024]{3,2,1,0:T(8,128)(2,1)} %xraw_ref.1) | copy-start | bytes 12582916
  48.7 0.8 copy-start.1
  50.7 1.0 %copy-start.2 = (bf16[1,1,256,1024]{3,2,1,0:T(8,128)(2,1)S(1)}, bf16[1,1,256,1024]{3,2,1,0:T(8,128)(2,1)}, u32[]{:S(2)}) copy-start(bf16[1,1,256,1024]{3,2,1,0:T(8,128)(2,1)} %copy-done.1) | copy-start | bytes 1572868
  62.9 0.8 copy-start.4
  65.2 14.5 %copy-start.3 = (bf16[1,1,256,1024]{3,2,1,0:T(8,128)(2,1)S(1)}, bf16[1,1,256,1024]{3,2,1,0:T(8,128)(2,1)}, u32[]{:S(2)}) copy-start(bf16[1,1,256,1024]{3,2,1,0:T(8,128)(2,1)} %copy-done.1) | copy-start | bytes 1572868
  65.2 1.1 %copy-start.5 = (bf16[1,1,256,1024]{3,2,1,0:T(8,128)(2,1)S(1)}, bf16[1,1,256,1024]{3,2,1,0:T(8,128)(2,1)}, u32[]{:S(2)}) copy-start(bf16[1,1,256,1024]{3,2,1,0:T(8,128)(2,1)} %copy-done.4) | copy-start | bytes 1572868
  66.3 13.4 %copy-start.6 = (bf16[1,1,256,1024]{3,2,1,0:T(8,128)(2,1)S(1)}, bf16[1,1,256,1024]{3,2,1,0:T(8,128)(2,1)}, u32[]{:S(2)}) copy-start(bf16[1,1,256,1024]{3,2,1,0:T(8,128)(2,1)} %copy-done.4) | copy-start | bytes 1572868
  79.6 8.1 %copy-start.9 = (f32[2]{0:T(128)S(1)}, f32[2]{0:T(128)}, u32[]{:S(2)}) copy-start(f32[2]{0:T(128)} %constant.24.clone) | copy-start | bytes 28

commit v11 on v10

--- a/solution.py
+++ b/solution.py
@@ -231,7 +231,7 @@
         pick = lambda c, blk: jnp.where(chan == 1, volts[1, c, blk * width:(blk + 1) * width],
                                         volts[0, c, blk * width:(blk + 1) * width])
         parts = [pick(c, blk) for blk in range(2) for c in range(2)]
-        parts[0] = jnp.concatenate([parts[0], meta[0]], axis=0)
+        parts[1] = jnp.concatenate([parts[1], meta[0]], axis=0)
         return [part[None, None] for part in parts]
 
     mine = [me & 1] + [((me >> 1) ^ (me >> 2)) & 1] * min(levels - 1, 2)
@@ -283,12 +283,12 @@
         got_tg = slab[0, 0, row + 1, : tg_flat.shape[0]].astype(jnp.int32).reshape(tile_group.shape)
         return one_hot(got_pos, True), got_tg
 
-    perm1, tg1 = meta_of(got1[0], width)
+    perm1, tg1 = meta_of(got1[1], width)
     perm0, tg0 = meta_of(got0, rows)
     lag10, relay_last = relay_call(
         relay_kernel, (volts, perm, *got1, perm1, got0, perm0, relay2), chunk_shape(3), 2, width, samples, 4, (9,)
     )
-    perm2, tg2 = meta_of(relayed[0], width)
+    perm2, tg2 = meta_of(relayed[1], width)
     lag2 = pair_lags(mine[2][None].astype(jnp.int32), volts, perm, relayed + [relay_last], perm2, False)
     level_lags = {0: (lag10[1], tg0), 1: (lag10[0], tg1), 2: (lag2[0], tg2)}
     for bit in range(levels):

time: 103 us -> 106 us (1.029)
  local copies, waits for them, and re-layouts: 14.9 us -> 17.4 us
  waiting for transfers between devices: 6.22 us -> 4.45 us
  Pallas kernels: 66.9 us -> 68.4 us
    unnamed x31 -> x35, local copies, waits for them, and re-layouts: 10.7 us -> 13.2 us
    ppermute x4, waiting for transfers between devices: 6.22 us -> 4.45 us  [on_device(): lax.ppermute(part, 'inp', [(i, i ^ 2) for i in range(n_inp)])]
    pallas_call x4, Pallas kernels: 50.3 us -> 51.8 us  [relay_call(): pl.pallas_call(kernel, out_shape=outs, in_specs=[hbm if i in hbm_args els...]
  transfers between devices with their start and end apart: 5 -> 5, of which waited for: 1 -> 1; matrix products, arithmetic and copies ran while one was open for 8% -> 8% of each run, Pallas kernels for 36% -> 35%
where the time goes in v11:
time: 106 us
  Pallas kernels  68.4 us (65%)
  local copies, waits for them, and re-layouts  17.4 us (16%)
  other arithmetic  10.5 us (10%)
  waiting for transfers between devices  4.45 us (4%)
  starting transfers between devices  4.08 us (4%)
    pallas_call x4, Pallas kernels, relay_call(): pl.pallas_call(kernel, out_shape=outs, in_specs=[hbm if i in hbm_args els...  51.8 us
    unnamed x35, local copies, waits for them, and re-layouts  13.2 us
    pallas_call x1, Pallas kernels, reduce_scatter(): pl.pallas_call(scatter_kernel, out_shape=jax.ShapeDtypeStruct(slab, jnp.f...  11.4 us
    pallas_call x1, Pallas kernels, pair_lags(): pl.pallas_call(lag_kernel, out_shape=jax.ShapeDtypeStruct((n, 8, 2 * widt...  5.17 us
    ppermute x4, waiting for transfers between devices, on_device(): lax.ppermute(part, 'inp', [(i, i ^ 2) for i in range(n_inp)])  4.45 us
    ppermute x4, starting transfers between devices, on_device(): lax.ppermute(part, 'inp', [(i, i ^ 2) for i in range(n_inp)])  4.05 us
    select_n x1, other arithmetic, chunks(): jnp.where(chan == 1, volts[1, c, blk * width:(blk + 1) * width], volts[0,...  3.4 us
    select_n x1, other arithmetic, on_device(): jnp.where(mine[0] == 0, volts[1], volts[0])  2.44 us
  transfers between devices with their start and end apart: 5, of which 1 were waited for; matrix products, arithmetic and copies ran while one was open for 8% of the time, Pallas kernels for 35%

profile of v11, /device:TPU:32, one launch (start us, length us, event | category | flops | bytes accessed | tf_op | source)
XLA Modules:
  0.0 105.9 jit_solution(18160194028796880487)
XLA Ops:
  0.0 3.4 %slice_select_fusion = (bf16[1,1,256,1024]{3,2,1,0:T(8,128)(2,1)}, bf16[1,1,256,1024]{3,2,1,0:T(8,128)(2,1)S(1)}, bf16[1,1,256,1024]{3,2,1,0:T(8,128)(2,1)}, bf16[256,1024]{1,0:T(8,128)(2,1)S(1)}) fusion(bf16[2,2,512,1024]{3,2,1,0:T(8,128)(2,1)} %xraw_ref.1, pred[]{:T(512)S(6)} %eq.271), kind=kLoop, calls=%fused_computation.7 | loop fusion | flops 1048576 | bytes 6291457 | tf_op jit(solution)/shard_map/jit(_where)/select_n | solution.py:231
  3.4 1.5 %collective-permute-start.2 = (bf16[1,1,256,1024]{3,2,1,0:T(8,128)(2,1)S(1)}, bf16[1,1,256,1024]{3,2,1,0:T(8,128)(2,1)S(1)}, u32[]{:S(2)}, u32[]{:S(2)}) collective-permute-start(bf16[1,1,256,1024]{3,2,1,0:T(8,128)(2,1)S(1)} %get-tuple-element.18), channel_id=1, source_target_pairs={{0,32},{16,48},{32,0},{48,16},{64,96},{80,112},{96,64},{112,80},{1... | collective-permute-start | bytes 1572872 | tf_op jit(solution)/shard_map/ppermute | solution.py:239
  4.9 0.1 copy.18
  5.2 0.9 maximum_bitcast_fusion.1
  6.0 0.5 collective-permute-start.1
  6.5 1.5 %collective-permute-start.3 = (bf16[1,1,256,1024]{3,2,1,0:T(8,128)(2,1)}, bf16[1,1,256,1024]{3,2,1,0:T(8,128)(2,1)S(1)}, u32[]{:S(2)}, u32[]{:S(2)}) collective-permute-start(bf16[1,1,256,1024]{3,2,1,0:T(8,128)(2,1)} %get-tuple-element.19), channel_id=1, source_target_pairs={{0,32},{16,48},{32,0},{48,16},{64,96},{80,112},{96,64},{112,80},{1... | collective-permute-start | bytes 1572872 | tf_op jit(solution)/shard_map/ppermute | solution.py:239
  8.0 0.5 collective-permute-start.4
  8.6 2.4 %select_bitcast_fusion = bf16[2,512,1024]{2,1,0:T(8,128)(2,1)S(1)} fusion(bf16[2,2,512,1024]{3,2,1,0:T(8,128)(2,1)} %xraw_ref.1, pred[]{:T(512)S(6)} %eq.258), kind=kLoop, calls=%fused_computation.1 | loop fusion | flops 1048576 | bytes 6291457 | tf_op jit(solution)/shard_map/jit(_where)/select_n | solution.py:241
  11.0 1.5 %maximum_bitcast_fusion = bf16[1,2,528,1024]{3,2,1,0:T(8,128)(2,1)} fusion(bf16[2,16,1024]{2,1,0:T(8,128)(2,1)S(1)} %pad.18, bf16[2,512,1024]{2,1,0:T(8,128)(2,1)S(1)} %select_bitcast_fusion), kind=kLoop, calls=%fused_computation | loop fusion | flops 4325376 | bytes 4325376 | tf_op jit(solution)/shard_map/broadcast_in_dim | solution.py:241
  12.6 0.2 rev.26
  12.8 0.3 slice_reduce_fusion
  13.1 0.1 copy.22
  13.5 0.1 fusion.xperm_ref
  13.6 0.1 fusion.1.yperm_ref
  13.8 4.4 %collective-permute-done.2.chunk_ref.y00 = bf16[1,1,256,1024]{3,2,1,0:T(8,128)(2,1)S(1)} collective-permute-done((bf16[1,1,256,1024]{3,2,1,0:T(8,128)(2,1)S(1)}, bf16[1,1,256,1024]{3,2,1,0:T(8,128)(2,1)S(1)}, u32[]{:S(2)}, u32[]{:S(2)}) %collective-permute-start.2) | collective-permute-done | bytes 524320 | tf_op jit(solution)/shard_map/ppermute | solution.py:239
  18.2 2.2 %copy-done = bf16[2,2,512,1024]{3,2,1,0:T(8,128)(2,1)S(1)} copy-done((bf16[2,2,512,1024]{3,2,1,0:T(8,128)(2,1)S(1)}, bf16[2,2,512,1024]{3,2,1,0:T(8,128)(2,1)}, u32[]{:S(2)}) %copy-start) | copy-done | bytes 4194328
  20.4 12.9 %shard_map.46 = (f32[2,8,512]{2,1,0:T(8,128)S(1)}, bf16[1,1,256,1024]{3,2,1,0:T(8,128)(2,1)S(1)}) custom-call(bf16[1,1,256,1024]{3,2,1,0:T(8,128)(2,1)S(1)} %collective-permute-done.2.chunk_ref.y00, bf16[2,2,512,1024]{3,2,1,0:T(8,128)(2,1)S(1)} %copy-done, bf16[2,256,256]{2,1,0:T(8,128)(2,1)S(1)} %fusion.xperm_ref, bf16[2,256,256]{2,1,0:T(8,128)(2,1)S(1)} %fusion.1.yperm_ref), custom_call_target="tpu_custom_call" | custom-call | flops 25769803776 | bytes 16777216 | tf_op jit(solution)/shard_map/pallas_call | solution.py:115
  33.3 0.8 copy-done.1
  34.1 0.4 reverse
  34.7 1.0 copy-done.2
  35.8 12.7 %shard_map.47.prev_ref.y01 = bf16[1,1,272,1024]{3,2,1,0:T(8,128)(2,1)S(1)} custom-call(bf16[1,1,272,1024]{3,2,1,0:T(8,128)(2,1)S(1)} %collective-permute-done.1.chunk_ref.y01, bf16[1,1,256,1024]{3,2,1,0:T(8,128)(2,1)S(1)} %copy-done.2), custom_call_target="tpu_custom_call" | custom-call | flops 12884901888 | bytes 16777216 | tf_op jit(solution)/shard_map/pallas_call | solution.py:115
  48.6 0.2 rev.32
  48.8 0.1 copy.21
  48.9 0.1 fusion.4.yperm_ref
  49.1 11.1 %shard_map.48.prev_ref.y10 = bf16[1,1,256,1024]{3,2,1,0:T(8,128)(2,1)S(1)} custom-call(bf16[1,1,256,1024]{3,2,1,0:T(8,128)(2,1)S(1)} %collective-permute-done.3.chunk_ref.y10, bf16[1,1,272,1024]{3,2,1,0:T(8,128)(2,1)S(1)} %shard_map.47.prev_ref.y01), custom_call_target="tpu_custom_call" | custom-call | flops 12884901888 | bytes 16777216 | tf_op jit(solution)/shard_map/pallas_call | solution.py:115
  60.2 0.8 copy-done.4
  61.0 0.7 fusion.8
  61.8 0.2 rev.28
  62.0 0.2 rev.29
  62.2 0.1 fusion.2.yperm_ref
  62.4 0.1 fusion.3.zperm_ref
  62.5 1.0 copy-done.5
  63.6 15.2 %shard_map.49 = (f32[2,8,512]{2,1,0:T(8,128)S(1)}, bf16[1,1,256,1024]{3,2,1,0:T(8,128)(2,1)S(1)}) custom-call(bf16[2,2,512,1024]{3,2,1,0:T(8,128)(2,1)} %xraw_ref.1, bf16[2,256,256]{2,1,0:T(8,128)(2,1)S(1)} %fusion.xperm_ref, bf16[1,1,256,1024]{3,2,1,0:T(8,128)(2,1)S(1)} %collective-permute-done.2.chunk_ref.y00, ...), custom_call_target="tpu_custom_call" | custom-call | flops 25769803776 | bytes 16777216 | tf_op jit(solution)/shard_map/pallas_call | solution.py:115
  78.8 0.8 copy-done.7
  79.7 1.0 copy-done.3
  80.7 1.0 copy-done.6
  81.7 1.0 copy-done.8
  82.8 5.2 %shard_map.50 = f32[1,8,512]{2,1,0:T(8,128)S(1)} custom-call(s32[1]{0:T(128)} %bitcast.26.sel_ref, bf16[2,2,512,1024]{3,2,1,0:T(8,128)(2,1)} %xraw_ref.1, bf16[2,256,256]{2,1,0:T(8,128)(2,1)S(1)} %fusion.xperm_ref, bf16[1,1,256,1024]{3,2,1,0:T(8,128)(2,1)S(1)} %copy-done.3, bf16[1,1,272,1024]{3,2,1,0:T(8,128)(2,1)S(1)} %shard_map.47.prev_ref.y01, ...), custom_call_target="tpu_custom_call" | custom-call | flops 3221225472 | bytes 4194304 | tf_op jit(solution)/shard_map/pallas_call | solution.py:150
  88.0 0.4 reverse.1
  88.5 0.4 reverse.2
  89.0 0.4 reverse.3
  89.5 0.7 slice_reduce_fusion.4
  90.3 0.1 copy.19
  90.6 0.1 copy.20
  91.1 0.6 convolution_multiply_fusion
  91.8 1.2 %copy.30 = f32[64,2,2,512]{3,2,1,0:T(2,128)} copy(f32[64,2,2,512]{3,0,2,1:T(8,128)S(1)} %convolution_multiply_fusion) | data formatting | bytes 1048576 | tf_op jit(solution)/shard_map/mul | solution.py:307
  93.0 11.4 %shard_map.51 = f32[8,2,2,512]{3,2,1,0:T(2,128)} custom-call(f32[8,8,2,2,512]{4,3,2,1,0:T(2,128)} %bitcast.55), custom_call_target="tpu_custom_call" | custom-call | tf_op jit(solution)/shard_map/pallas_call | solution.py:202
  104.4 1.5 %copy.41 = f32[8,2,2,511]{3,2,1,0:T(2,128)} copy(f32[8,2,2,511]{3,2,1,0:T(2,128)} %bitcast.56) | data formatting | bytes 130816
  (76 shorter events, 2.1 us)
Async XLA Ops:
  0.0 4.9 %copy-start.9 = (s32[2,4,2]{1,2,0:T(2,128)S(1)}, s32[2,4,2]{1,2,0:T(2,128)}, u32[]{:S(2)}) copy-start(s32[2,4,2]{1,2,0:T(2,128)} %param.6) | copy-start | bytes 196
  0.0 5.1 %copy-start.10 = (s32[2,256]{1,0:T(2,128)S(1)}, s32[2,256]{1,0:T(2,128)}, u32[]{:S(2)}) copy-start(s32[2,256]{1,0:T(2,128)} %param.5) | copy-start | bytes 6148
  3.4 14.8 %collective-permute-start.2 = (bf16[1,1,256,1024]{3,2,1,0:T(8,128)(2,1)S(1)}, bf16[1,1,256,1024]{3,2,1,0:T(8,128)(2,1)S(1)}, u32[]{:S(2)}, u32[]{:S(2)}) collective-permute-start(bf16[1,1,256,1024]{3,2,1,0:T(8,128)(2,1)S(1)} %get-tuple-element.18), channel_id=1, source_target_pairs={{0,32},{16,48},{32,0},{48,16},{64,96},{80,112},{96,64},{112,80},{1... | collective-permute-start | bytes 1572872 | tf_op jit(solution)/shard_map/ppermute | solution.py:239
  6.0 28.7 %collective-permute-start.1 = (bf16[1,1,272,1024]{3,2,1,0:T(8,128)(2,1)}, bf16[1,1,272,1024]{3,2,1,0:T(8,128)(2,1)S(1)}, u32[]{:S(2)}, u32[]{:S(2)}) collective-permute-start(bf16[1,1,272,1024]{3,2,1,0:T(8,128)(2,1)} %maximum_bitcast_fusion.1), channel_id=1, source_target_pairs={{0,32},{16,48},{32,0},{48,16},{64,96},{80,112},{96,64},{112,80},{1... | collective-permute-start | bytes 1671176 | tf_op jit(solution)/shard_map/ppermute | solution.py:239
  6.5 42.5 %collective-permute-start.3 = (bf16[1,1,256,1024]{3,2,1,0:T(8,128)(2,1)}, bf16[1,1,256,1024]{3,2,1,0:T(8,128)(2,1)S(1)}, u32[]{:S(2)}, u32[]{:S(2)}) collective-permute-start(bf16[1,1,256,1024]{3,2,1,0:T(8,128)(2,1)} %get-tuple-element.19), channel_id=1, source_target_pairs={{0,32},{16,48},{32,0},{48,16},{64,96},{80,112},{96,64},{112,80},{1... | collective-permute-start | bytes 1572872 | tf_op jit(solution)/shard_map/ppermute | solution.py:239
  8.0 54.5 %collective-permute-start.4 = (bf16[1,1,256,1024]{3,2,1,0:T(8,128)(2,1)}, bf16[1,1,256,1024]{3,2,1,0:T(8,128)(2,1)S(1)}, u32[]{:S(2)}, u32[]{:S(2)}) collective-permute-start(bf16[1,1,256,1024]{3,2,1,0:T(8,128)(2,1)} %get-tuple-element.17), channel_id=1, source_target_pairs={{0,32},{16,48},{32,0},{48,16},{64,96},{80,112},{96,64},{112,80},{1... | collective-permute-start | bytes 1572872 | tf_op jit(solution)/shard_map/ppermute | solution.py:239
  12.5 48.5 %collective-permute-start = (bf16[1,2,528,1024]{3,2,1,0:T(8,128)(2,1)}, bf16[1,2,528,1024]{3,2,1,0:T(8,128)(2,1)}, u32[]{:S(2)}, u32[]{:S(2)}) collective-permute-start(bf16[1,2,528,1024]{3,2,1,0:T(8,128)(2,1)} %maximum_bitcast_fusion), channel_id=1, source_target_pairs={{0,16},{16,0},{32,48},{48,32},{64,80},{80,64},{96,112},{112,96},{1... | collective-permute-start | bytes 6488072 | tf_op jit(solution)/shard_map/ppermute | solution.py:240
  18.2 2.2 %copy-start = (bf16[2,2,512,1024]{3,2,1,0:T(8,128)(2,1)S(1)}, bf16[2,2,512,1024]{3,2,1,0:T(8,128)(2,1)}, u32[]{:S(2)}) copy-start(bf16[2,2,512,1024]{3,2,1,0:T(8,128)(2,1)} %xraw_ref.1) | copy-start | bytes 12582916
  33.3 0.8 copy-start.1
  34.7 1.0 copy-start.2
  60.2 0.8 copy-start.4
  62.5 1.0 copy-start.5
  78.8 0.8 copy-start.7
  79.7 1.0 copy-start.3
  80.7 1.0 copy-start.6
  81.7 1.0 copy-start.8
  82.8 8.0 %copy-start.11 = (f32[2]{0:T(128)S(1)}, f32[2]{0:T(128)}, u32[]{:S(2)}) copy-start(f32[2]{0:T(128)} %constant.24.clone) | copy-start | bytes 28

commit v12 on v6

--- a/solution.py
+++ b/solution.py
@@ -82,9 +82,8 @@
     copy.wait()
 
 
-def relay_kernel(x_ref, xperm_ref, y00, y01, y10, y11, yperm_ref, z_ref, zperm_ref, prev_ref,
+def relay_kernel(x_ref, xperm_ref, y00, y01, y10, y11, yperm_ref, z_ref, zperm_ref, r00, r01, r10, rperm_ref,
                  o_ref, relay_ref, xs, ys, send_sem, recv_sem):
-    del prev_ref
     width = xperm_ref.shape[1]
     me = lax.axis_index("inp")
     copy = start_relay(y11, relay_ref, send_sem, recv_sem)
@@ -101,6 +100,12 @@
         xperm_ref, zperm_ref, o_ref, 1, xs, ys,
     )
     copy.wait()
+    relayed = ((r00, r01), (r10, relay_ref))
+    lags_into(
+        lambda a, c: block_rows(x_ref, parity, c, a, width),
+        lambda b, c: relayed[b][c][0, 0, pl.ds(0, width), :],
+        xperm_ref, rperm_ref, o_ref, 2, xs, ys,
+    )
 
 
 def relay_call(kernel, args, outs, n_lags, width, samples, collective_id):
@@ -279,12 +284,11 @@
 
     perm1, tg1 = meta_of(got1[0], width)
     perm0, tg0 = meta_of(got0, rows)
-    lag10, relay_last = relay_call(
-        relay_kernel, (volts, perm, *got1, perm1, got0, perm0, relay2), chunk_shape(3), 2, width, samples, 4
-    )
     perm2, tg2 = meta_of(relayed[0], width)
-    lag2 = pair_lags(mine[2][None].astype(jnp.int32), volts, perm, relayed + [relay_last], perm2, False)
-    level_lags = {0: (lag10[1], tg0), 1: (lag10[0], tg1), 2: (lag2[0], tg2)}
+    lag10, _ = relay_call(
+        relay_kernel, (volts, perm, *got1, perm1, got0, perm0, *relayed, perm2), chunk_shape(3), 3, width, samples, 4
+    )
+    level_lags = {0: (lag10[1], tg0), 1: (lag10[0], tg1), 2: (lag10[2], tg2)}
     for bit in range(levels):
         lag, got_tg = level_lags[bit]
         lag = lag.reshape(2, 2, 2, 2 * width)[..., :diffs]

time: 103 us -> 103 us (level)
  Pallas kernels: 66.9 us -> 65.1 us
    pallas_call x1 -> x0, Pallas kernels: 5.17 us -> none  [pair_lags(): pl.pallas_call(lag_kernel, out_shape=jax.ShapeDtypeStruct((n, 8, 2 * widt...]
    pallas_call x4, Pallas kernels: 50.3 us -> 53.8 us  [relay_call(): pl.pallas_call(kernel, out_shape=outs, in_specs=[vmem] * len(args), out_s...]
    unnamed x32 -> x30, local copies, waits for them, and re-layouts: 11.2 us -> 12.2 us
  transfers between devices with their start and end apart: 5 -> 5, of which waited for: 1 -> 1; matrix products, arithmetic and copies ran while one was open for 9% -> 8% of each run, Pallas kernels for 36% -> 36%
where the time goes in v12:
time: 103 us; the launch traced here: 102 us
  Pallas kernels  65.1 us (63%)
  local copies, waits for them, and re-layouts  16 us (16%)
  other arithmetic  9.6 us (9%)
  waiting for transfers between devices  6.23 us (6%)
  starting transfers between devices  4.16 us (4%)
    pallas_call x4, Pallas kernels, relay_call(): pl.pallas_call(kernel, out_shape=outs, in_specs=[vmem] * len(args), out_s...  53.8 us
    unnamed x30, local copies, waits for them, and re-layouts  12.2 us
    pallas_call x1, Pallas kernels, reduce_scatter(): pl.pallas_call(scatter_kernel, out_shape=jax.ShapeDtypeStruct(slab, jnp.f...  11.3 us
    ppermute x4, waiting for transfers between devices, on_device(): lax.ppermute(part, 'inp', [(i, i ^ 2) for i in range(n_inp)])  6.22 us
    ppermute x4, starting transfers between devices, on_device(): lax.ppermute(part, 'inp', [(i, i ^ 2) for i in range(n_inp)])  4.13 us
    select_n x1, other arithmetic, chunks(): jnp.where(chan == 1, volts[1, c, blk * width:(blk + 1) * width], volts[0,...  3.35 us
    select_n x1, other arithmetic, on_device(): jnp.where(mine[0] == 0, volts[1], volts[0])  2.44 us
  transfers between devices with their start and end apart: 5, of which 1 were waited for; matrix products, arithmetic and copies ran while one was open for 8% of the time, Pallas kernels for 36%

profile of v12, /device:TPU:32, one launch (start us, length us, event | category | flops | bytes accessed | tf_op | source)
XLA Modules:
  0.0 102.2 jit_solution(4347841622375386146)
XLA Ops:
  0.0 0.8 copy.18
  0.9 0.7 copy.40
  1.6 3.3 %slice_select_fusion = (bf16[1,1,256,1024]{3,2,1,0:T(8,128)(2,1)}, bf16[256,1024]{1,0:T(8,128)(2,1)S(1)}, bf16[1,1,256,1024]{3,2,1,0:T(8,128)(2,1)}, bf16[1,1,256,1024]{3,2,1,0:T(8,128)(2,1)}) fusion(bf16[2,2,512,1024]{3,2,1,0:T(8,128)(2,1)} %x_ref.3, pred[]{:T(512)S(6)} %eq.271), kind=kLoop, calls=%fused_computation.7 | loop fusion | flops 1048576 | bytes 6291457 | tf_op jit(solution)/shard_map/jit(_where)/select_n | solution.py:233
  5.0 1.6 %collective-permute-start.1 = (bf16[1,1,272,1024]{3,2,1,0:T(8,128)(2,1)S(1)}, bf16[1,1,272,1024]{3,2,1,0:T(8,128)(2,1)S(1)}, u32[]{:S(2)}, u32[]{:S(2)}) collective-permute-start(bf16[1,1,272,1024]{3,2,1,0:T(8,128)(2,1)S(1)} %maximum_bitcast_fusion.1), channel_id=1, source_target_pairs={{0,32},{16,48},{32,0},{48,16},{64,96},{80,112},{96,64},{112,80},{1... | collective-permute-start | bytes 1671176 | tf_op jit(solution)/shard_map/ppermute | solution.py:241
  6.6 0.5 collective-permute-start.2
  7.1 1.5 %collective-permute-start.3 = (bf16[1,1,256,1024]{3,2,1,0:T(8,128)(2,1)}, bf16[1,1,256,1024]{3,2,1,0:T(8,128)(2,1)S(1)}, u32[]{:S(2)}, u32[]{:S(2)}) collective-permute-start(bf16[1,1,256,1024]{3,2,1,0:T(8,128)(2,1)} %get-tuple-element.18), channel_id=1, source_target_pairs={{0,32},{16,48},{32,0},{48,16},{64,96},{80,112},{96,64},{112,80},{1... | collective-permute-start | bytes 1572872 | tf_op jit(solution)/shard_map/ppermute | solution.py:241
  8.6 0.5 collective-permute-start.4
  9.1 2.4 %select_bitcast_fusion = bf16[2,512,1024]{2,1,0:T(8,128)(2,1)S(1)} fusion(bf16[2,2,512,1024]{3,2,1,0:T(8,128)(2,1)} %x_ref.3, pred[]{:T(512)S(6)} %eq.258), kind=kLoop, calls=%fused_computation.1 | loop fusion | flops 1048576 | bytes 6291457 | tf_op jit(solution)/shard_map/jit(_where)/select_n | solution.py:243
  11.6 1.5 %maximum_bitcast_fusion = bf16[1,2,528,1024]{3,2,1,0:T(8,128)(2,1)} fusion(bf16[2,16,1024]{2,1,0:T(8,128)(2,1)S(1)} %pad.18, bf16[2,512,1024]{2,1,0:T(8,128)(2,1)S(1)} %select_bitcast_fusion), kind=kLoop, calls=%fused_computation | loop fusion | flops 4325376 | bytes 4325376 | tf_op jit(solution)/shard_map/broadcast_in_dim | solution.py:243
  13.2 0.2 rev.26
  13.4 0.3 slice_reduce_fusion
  13.7 0.1 copy.22
  14.1 0.1 fusion.xperm_ref
  14.2 0.1 fusion.1.yperm_ref
  14.4 6.2 %collective-permute-done.1.chunk_ref.y00 = bf16[1,1,272,1024]{3,2,1,0:T(8,128)(2,1)S(1)} collective-permute-done((bf16[1,1,272,1024]{3,2,1,0:T(8,128)(2,1)S(1)}, bf16[1,1,272,1024]{3,2,1,0:T(8,128)(2,1)S(1)}, u32[]{:S(2)}, u32[]{:S(2)}) %collective-permute-start.1) | collective-permute-done | bytes 557088 | tf_op jit(solution)/shard_map/ppermute | solution.py:241
  20.6 2.2 %copy-done = bf16[2,2,512,1024]{3,2,1,0:T(8,128)(2,1)S(1)} copy-done((bf16[2,2,512,1024]{3,2,1,0:T(8,128)(2,1)S(1)}, bf16[2,2,512,1024]{3,2,1,0:T(8,128)(2,1)}, u32[]{:S(2)}) %copy-start) | copy-done | bytes 4194328
  22.8 13.7 %shard_map.46 = (f32[2,8,512]{2,1,0:T(8,128)S(1)}, bf16[1,1,272,1024]{3,2,1,0:T(8,128)(2,1)S(1)}) custom-call(bf16[1,1,272,1024]{3,2,1,0:T(8,128)(2,1)S(1)} %collective-permute-done.1.chunk_ref.y00, bf16[2,2,512,1024]{3,2,1,0:T(8,128)(2,1)S(1)} %copy-done, bf16[2,256,256]{2,1,0:T(8,128)(2,1)S(1)} %fusion.xperm_ref, bf16[2,256,256]{2,1,0:T(8,128)(2,1)S(1)} %fusion.1.yperm_ref), custom_call_target="tpu_custom_call" | custom-call | flops 25769803776 | bytes 16777216 | tf_op jit(solution)/shard_map/pallas_call | solution.py:117
  36.5 12.1 %shard_map.47.prev_ref.r01 = bf16[1,1,256,1024]{3,2,1,0:T(8,128)(2,1)S(1)} custom-call(bf16[1,1,256,1024]{3,2,1,0:T(8,128)(2,1)S(1)} %collective-permute-done.2.chunk_ref.y01, bf16[1,1,272,1024]{3,2,1,0:T(8,128)(2,1)S(1)} %get-tuple-element.8.prev_ref.r00), custom_call_target="tpu_custom_call" | custom-call | flops 12884901888 | bytes 16777216 | tf_op jit(solution)/shard_map/pallas_call | solution.py:117
  48.7 0.8 copy-done.1
  49.5 0.4 reverse
  49.9 0.1 slice.175
  50.2 0.2 rev.30
  50.4 0.1 copy.21
  50.6 0.1 fusion.4.rperm_ref
  50.7 1.0 %copy-done.2 = bf16[1,1,256,1024]{3,2,1,0:T(8,128)(2,1)S(1)} copy-done((bf16[1,1,256,1024]{3,2,1,0:T(8,128)(2,1)S(1)}, bf16[1,1,256,1024]{3,2,1,0:T(8,128)(2,1)}, u32[]{:S(2)}) %copy-start.2) | copy-done | bytes 524312
  51.8 11.1 %shard_map.48.r10 = bf16[1,1,256,1024]{3,2,1,0:T(8,128)(2,1)S(1)} custom-call(bf16[1,1,256,1024]{3,2,1,0:T(8,128)(2,1)S(1)} %collective-permute-done.3.chunk_ref.y10, bf16[1,1,256,1024]{3,2,1,0:T(8,128)(2,1)S(1)} %copy-done.2), custom_call_target="tpu_custom_call" | custom-call | flops 12884901888 | bytes 16777216 | tf_op jit(solution)/shard_map/pallas_call | solution.py:117
  62.9 0.8 copy-done.4
  63.7 0.7 fusion.8
  64.5 0.2 rev.28
  64.7 0.2 rev.29
  64.9 0.1 fusion.2.yperm_ref
  65.0 0.1 fusion.3.zperm_ref
  65.2 1.0 %copy-done.3 = bf16[1,1,256,1024]{3,2,1,0:T(8,128)(2,1)S(1)} copy-done((bf16[1,1,256,1024]{3,2,1,0:T(8,128)(2,1)S(1)}, bf16[1,1,256,1024]{3,2,1,0:T(8,128)(2,1)}, u32[]{:S(2)}) %copy-start.3) | copy-done | bytes 524312
  66.2 1.0 %copy-done.5 = bf16[1,1,256,1024]{3,2,1,0:T(8,128)(2,1)S(1)} copy-done((bf16[1,1,256,1024]{3,2,1,0:T(8,128)(2,1)S(1)}, bf16[1,1,256,1024]{3,2,1,0:T(8,128)(2,1)}, u32[]{:S(2)}) %copy-start.5) | copy-done | bytes 524312
  67.3 16.9 %shard_map.49 = (f32[3,8,512]{2,1,0:T(8,128)S(1)}, bf16[1,1,256,1024]{3,2,1,0:T(8,128)(2,1)}) custom-call(bf16[2,2,512,1024]{3,2,1,0:T(8,128)(2,1)} %x_ref.3, bf16[2,256,256]{2,1,0:T(8,128)(2,1)S(1)} %fusion.xperm_ref, bf16[1,1,272,1024]{3,2,1,0:T(8,128)(2,1)S(1)} %collective-permute-done.1.chunk_ref.y00, ...), custom_call_target="tpu_custom_call" | custom-call | flops 38654705664 | bytes 16777216 | tf_op jit(solution)/shard_map/pallas_call | solution.py:117
  84.4 0.4 reverse.1
  84.8 0.4 reverse.2
  85.3 0.4 reverse.3
  85.8 0.7 slice_reduce_fusion.4
  86.5 0.1 convert_element_type.88
  86.6 0.1 copy.19
  86.9 0.1 copy.20
  87.2 0.1 concatenate.22
  87.4 0.6 convolution_multiply_fusion
  88.0 0.4 copy.39
  88.4 1.0 pad.19.clone
  89.4 11.3 %shard_map.50 = f32[8,2,2,512]{3,2,1,0:T(2,128)} custom-call(f32[8,8,2,2,512]{4,3,2,1,0:T(2,128)} %bitcast.54), custom_call_target="tpu_custom_call" | custom-call | tf_op jit(solution)/shard_map/pallas_call | solution.py:204
  100.7 1.5 %copy.42 = f32[8,2,2,511]{3,2,1,0:T(2,128)} copy(f32[8,2,2,511]{3,2,1,0:T(2,128)} %bitcast.55) | data formatting | bytes 130816
  (66 shorter events, 1.7 us)
Async XLA Ops:
  5.0 15.6 %collective-permute-start.1 = (bf16[1,1,272,1024]{3,2,1,0:T(8,128)(2,1)S(1)}, bf16[1,1,272,1024]{3,2,1,0:T(8,128)(2,1)S(1)}, u32[]{:S(2)}, u32[]{:S(2)}) collective-permute-start(bf16[1,1,272,1024]{3,2,1,0:T(8,128)(2,1)S(1)} %maximum_bitcast_fusion.1), channel_id=1, source_target_pairs={{0,32},{16,48},{32,0},{48,16},{64,96},{80,112},{96,64},{112,80},{1... | collective-permute-start | bytes 1671176 | tf_op jit(solution)/shard_map/ppermute | solution.py:241
  6.6 29.9 %collective-permute-start.2 = (bf16[1,1,256,1024]{3,2,1,0:T(8,128)(2,1)}, bf16[1,1,256,1024]{3,2,1,0:T(8,128)(2,1)S(1)}, u32[]{:S(2)}, u32[]{:S(2)}) collective-permute-start(bf16[1,1,256,1024]{3,2,1,0:T(8,128)(2,1)} %get-tuple-element.17), channel_id=1, source_target_pairs={{0,32},{16,48},{32,0},{48,16},{64,96},{80,112},{96,64},{112,80},{1... | collective-permute-start | bytes 1572872 | tf_op jit(solution)/shard_map/ppermute | solution.py:241
  7.1 43.6 %collective-permute-start.3 = (bf16[1,1,256,1024]{3,2,1,0:T(8,128)(2,1)}, bf16[1,1,256,1024]{3,2,1,0:T(8,128)(2,1)S(1)}, u32[]{:S(2)}, u32[]{:S(2)}) collective-permute-start(bf16[1,1,256,1024]{3,2,1,0:T(8,128)(2,1)} %get-tuple-element.18), channel_id=1, source_target_pairs={{0,32},{16,48},{32,0},{48,16},{64,96},{80,112},{96,64},{112,80},{1... | collective-permute-start | bytes 1572872 | tf_op jit(solution)/shard_map/ppermute | solution.py:241
  8.6 56.6 %collective-permute-start.4 = (bf16[1,1,256,1024]{3,2,1,0:T(8,128)(2,1)}, bf16[1,1,256,1024]{3,2,1,0:T(8,128)(2,1)S(1)}, u32[]{:S(2)}, u32[]{:S(2)}) collective-permute-start(bf16[1,1,256,1024]{3,2,1,0:T(8,128)(2,1)} %get-tuple-element.15), channel_id=1, source_target_pairs={{0,32},{16,48},{32,0},{48,16},{64,96},{80,112},{96,64},{112,80},{1... | collective-permute-start | bytes 1572872 | tf_op jit(solution)/shard_map/ppermute | solution.py:241
  11.6 1.6 %copy-start.7 = (s32[2,256]{1,0:T(2,128)S(1)}, s32[2,256]{1,0:T(2,128)}, u32[]{:S(2)}) copy-start(s32[2,256]{1,0:T(2,128)} %param.5) | copy-start | bytes 6148
  11.6 1.7 %copy-start.6 = (s32[2,4,2]{1,2,0:T(2,128)S(1)}, s32[2,4,2]{1,2,0:T(2,128)}, u32[]{:S(2)}) copy-start(s32[2,4,2]{1,2,0:T(2,128)} %param.6) | copy-start | bytes 196
  13.1 50.6 %collective-permute-start = (bf16[1,2,528,1024]{3,2,1,0:T(8,128)(2,1)}, bf16[1,2,528,1024]{3,2,1,0:T(8,128)(2,1)}, u32[]{:S(2)}, u32[]{:S(2)}) collective-permute-start(bf16[1,2,528,1024]{3,2,1,0:T(8,128)(2,1)} %maximum_bitcast_fusion), channel_id=1, source_target_pairs={{0,16},{16,0},{32,48},{48,32},{64,80},{80,64},{96,112},{112,96},{1... | collective-permute-start | bytes 6488072 | tf_op jit(solution)/shard_map/ppermute | solution.py:242
  20.6 2.2 %copy-start = (bf16[2,2,512,1024]{3,2,1,0:T(8,128)(2,1)S(1)}, bf16[2,2,512,1024]{3,2,1,0:T(8,128)(2,1)}, u32[]{:S(2)}) copy-start(bf16[2,2,512,1024]{3,2,1,0:T(8,128)(2,1)} %x_ref.3) | copy-start | bytes 12582916
  48.6 0.8 copy-start.1
  50.7 1.0 %copy-start.2 = (bf16[1,1,256,1024]{3,2,1,0:T(8,128)(2,1)S(1)}, bf16[1,1,256,1024]{3,2,1,0:T(8,128)(2,1)}, u32[]{:S(2)}) copy-start(bf16[1,1,256,1024]{3,2,1,0:T(8,128)(2,1)} %copy-done.1) | copy-start | bytes 1572868
  62.9 0.8 copy-start.4
  65.2 1.0 %copy-start.3 = (bf16[1,1,256,1024]{3,2,1,0:T(8,128)(2,1)S(1)}, bf16[1,1,256,1024]{3,2,1,0:T(8,128)(2,1)}, u32[]{:S(2)}) copy-start(bf16[1,1,256,1024]{3,2,1,0:T(8,128)(2,1)} %copy-done.1) | copy-start | bytes 1572868
  66.2 1.0 %copy-start.5 = (bf16[1,1,256,1024]{3,2,1,0:T(8,128)(2,1)S(1)}, bf16[1,1,256,1024]{3,2,1,0:T(8,128)(2,1)}, u32[]{:S(2)}) copy-start(bf16[1,1,256,1024]{3,2,1,0:T(8,128)(2,1)} %copy-done.4) | copy-start | bytes 1572868
  67.3 17.0 %copy-start.8 = (f32[2]{0:T(128)S(1)}, f32[2]{0:T(128)}, u32[]{:S(2)}) copy-start(f32[2]{0:T(128)} %constant.23.clone) | copy-start | bytes 28
